TPU v7x, 512 devices: a whole 4x8x8 slice. The times are simulated.
512 devices in a mesh: blk: 128 (over z, y, x_lo), rep: 4 (over x_hi, core).
Axes of the slice: x: 4 (x_hi: 2, x_lo: 2; x = x_hi * 2 + x_lo), y: 8, z: 8, core: 2. Of those that a mesh axis runs over, the one named last changes fastest.
Arguments:
- left_emb: float32 [32768, 256], P('blk'), may hold values from -6 to 6
- left_state: float32 [32768], P('blk'), may hold values from 0.3 to 30
- right_emb: float32 [32768, 256], P('blk'), may hold values from -8 to 8
- right_state: float32 [32768], P('blk'), may hold values from 0.3 to 30
- relation: float32 [2, 256, 256], replicated, may hold values from -0.375 to 0.375
- relation_state: float32 [2, 256, 256], replicated, may hold values from 5242.88 to 524288
- edge_src: int32 [128, 4, 2, 2, 512], P('blk', 'rep'), may hold values from 0 to 255
- edge_dst: int32 [128, 4, 2, 2, 512], P('blk', 'rep'), may hold values from 0 to 255
- edge_rel: int32 [128, 4, 2, 2, 512], P('blk', 'rep'), may hold values from 0 to 1
- negatives: int32 [128, 4, 2, 2, 512], P('blk', 'rep'), may hold values from 0 to 255
- batch_counts: int32 [128, 4, 2], P('blk', 'rep'), may hold values from 0 to 2, as said below
Outputs:
- left_new: float32 [32768, 256], P('blk')
- left_state_new: float32 [32768], P('blk')
- right_new: float32 [32768, 256], P('blk')
- right_state_new: float32 [32768], P('blk')
- relation_new: float32 [2, 256, 256], replicated
- relation_state_new: float32 [2, 256, 256], replicated
Inputs may be any that keep to these rules, and one draw needn't show every extreme that they name: `batch_counts`: in each bucket the live edge batches of the 4 devices of one blk index number at most 4; in every draw some bucket has exactly that many, with some device at 2.
All inputs are finite; a program needn't handle non-finite values.
Results may differ from a plain program's by a relative error of at most 0.035.
Values sent between devices are 32-bit elements; how exact they have to be, the bound alone decides.
No kernel may reach another device: no remote copies, remote signals or barrier semaphores. Data moves between devices by JAX's collectives and lax.ppermute only.
A program may use at most 64 MiB of HBM per device.

v0:
```python
import jax
import jax.numpy as jnp
from jax import lax
from jax.sharding import PartitionSpec as P

learn_rate = 0.1


def from_behind(block, axis, distance):
    devices = range(lax.axis_size(axis))
    route = [((i - distance) % len(devices), i) for i in devices]
    return lax.ppermute(block, axis, route)


def batch_terms(query_table, right_bf, src_row, dst_row, rel_row, neg_row, live_flag):
    queries = query_table[rel_row, src_row]
    pos_rows = right_bf[dst_row]
    neg_rows = right_bf[neg_row]
    pos_score = jnp.sum(queries.astype(jnp.float32) * pos_rows.astype(jnp.float32), axis=-1)
    neg_score = lax.dot_general(
        queries, neg_rows, (((1,), (1,)), ((), ())), preferred_element_type=jnp.float32
    )
    row_top = jnp.maximum(jnp.max(neg_score, axis=1), pos_score)
    pos_exp = jnp.exp(pos_score - row_top)
    neg_exp = jnp.exp(neg_score - row_top[:, None])
    row_total = pos_exp + jnp.sum(neg_exp, axis=1)
    pos_weight = (pos_exp / row_total - 1.0) * live_flag
    weights = (neg_exp / row_total[:, None] * live_flag).astype(jnp.bfloat16)
    query_grad = jnp.dot(weights, neg_rows, preferred_element_type=jnp.float32) + pos_weight[
        :, None
    ] * pos_rows.astype(jnp.float32)
    neg_grad = lax.dot_general(
        weights, queries, (((0,), (0,)), ((), ())), preferred_element_type=jnp.float32
    )
    pos_grad = pos_weight[:, None] * queries.astype(jnp.float32)
    return (query_grad, neg_grad, pos_grad)


def bucket_terms(left_rows, right_rows, operator_bf, sources, targets, relations, negs, live_flags):
    left_bf = left_rows.astype(jnp.bfloat16)
    right_bf = right_rows.astype(jnp.bfloat16)
    query_table = jnp.einsum(
        "nd,rkd->rnk", left_bf, operator_bf, preferred_element_type=jnp.float32
    ).astype(jnp.bfloat16)
    nrel, rows, width = query_table.shape

    def step(position, carry):
        table_grad, right_grad = carry
        src_row = lax.dynamic_index_in_dim(sources, position, 0, keepdims=False)
        dst_row = lax.dynamic_index_in_dim(targets, position, 0, keepdims=False)
        rel_row = lax.dynamic_index_in_dim(relations, position, 0, keepdims=False)
        neg_row = lax.dynamic_index_in_dim(negs, position, 0, keepdims=False)
        live_flag = lax.dynamic_index_in_dim(live_flags, position, 0, keepdims=False)
        query_grad, neg_grad, pos_grad = batch_terms(
            query_table, right_bf, src_row, dst_row, rel_row, neg_row, live_flag
        )
        table_grad = table_grad.at[rel_row, src_row].add(query_grad)
        right_grad = right_grad.at[neg_row].add(neg_grad).at[dst_row].add(pos_grad)
        return (table_grad, right_grad)

    start = (jnp.zeros((nrel, rows, width), jnp.float32), jnp.zeros((rows, width), jnp.float32))
    table_grad, right_grad = lax.fori_loop(0, sources.shape[0], step, start)
    table_bf = table_grad.astype(jnp.bfloat16)
    left_grad = jnp.einsum("rnk,rkd->nd", table_bf, operator_bf, preferred_element_type=jnp.float32)
    operator_grad = jnp.einsum("rnk,nd->rkd", table_bf, left_bf, preferred_element_type=jnp.float32)
    return (left_grad, right_grad, operator_grad)


def row_update(embedding, accum, gradient):
    accum_next = accum + jnp.mean(gradient * gradient, axis=-1)
    return (embedding - learn_rate * gradient / jnp.sqrt(accum_next)[:, None], accum_next)


def body(
    left_emb,
    left_state,
    right_emb,
    right_state,
    relation,
    relation_state,
    edge_src,
    edge_dst,
    edge_rel,
    negatives,
    batch_counts,
):
    operator_bf = relation.astype(jnp.bfloat16)
    nbatch = edge_src.shape[3]
    left_rows, left_accum = (left_emb, left_state)
    right_rows, right_accum = (right_emb, right_state)
    operator_total = jnp.zeros(relation.shape, jnp.float32)
    for bucket in range(2):
        sources = edge_src[0, 0, bucket]
        targets = edge_dst[0, 0, bucket]
        relations = edge_rel[0, 0, bucket]
        negs = negatives[0, 0, bucket]
        live_flags = (jnp.arange(nbatch) < batch_counts[0, 0, bucket]).astype(jnp.float32)
        left_grad, right_grad, operator_grad = bucket_terms(
            left_rows, right_rows, operator_bf, sources, targets, relations, negs, live_flags
        )
        operator_total = operator_total + lax.psum(operator_grad, ("blk", "rep"))
        left_sum, right_sum = lax.psum((left_grad, right_grad), "rep")
        left_rows, left_accum = row_update(left_rows, left_accum, left_sum)
        right_rows, right_accum = row_update(right_rows, right_accum, right_sum)
        if bucket == 0:
            left_rows, left_accum = from_behind((left_rows, left_accum), "blk", 1)
    relation_state_new = relation_state + operator_total * operator_total
    relation_new = relation - learn_rate * operator_total / jnp.sqrt(relation_state_new)
    return (left_rows, left_accum, right_rows, right_accum, relation_new, relation_state_new)


def solution(mesh):
    in_specs = (
        P("blk", None),
        P("blk"),
        P("blk", None),
        P("blk"),
        P(),
        P(),
        P("blk", "rep", None, None, None),
        P("blk", "rep", None, None, None),
        P("blk", "rep", None, None, None),
        P("blk", "rep", None, None, None),
        P("blk", "rep", None),
    )
    out_specs = (P("blk", None), P("blk"), P("blk", None), P("blk"), P(), P())
    return jax.shard_map(body, mesh=mesh, in_specs=in_specs, out_specs=out_specs, check_vma=False)
```

profile of v0, /device:TPU:1, one launch (start us, length us, event | category | flops | bytes accessed | tf_op | source)
XLA Modules:
  0.0 608.1 jit_solution(12801148130178979247)
XLA Ops:
  7.2 0.6 copy-done.23
  8.4 1.2 compare_convert_fusion.1
  9.6 1.0 convert_element_type.107
  10.6 1.1 convert_element_type.103
  14.1 91.2 %while.34 = (s32[]{:T(128)}, f32[2,256,256]{2,1,0:T(8,128)S(1)}, f32[256,256]{1,0:T(8,128)S(1)}, s32[2,512]{1,0:T(2,128)}, s32[2,512]{1,0:T(2,128)}, /*index=5*/...) while((s32[]{:T(128)}, f32[2,256,256]{2,1,0:T(8,128)S(1)}, ...), condition=%wide.region_7.8_spmd, body=%wide.region_0.7_spmd.sunk | while | flops 406075392 | bytes 12953801 | solution.py:62
  14.1 1.2 dynamic_slice.141
  15.3 0.7 compare_select_fusion.10
  16.0 0.7 or_select_fusion.4
  16.8 2.0 gather_fusion.1
  18.7 2.0 gather_fusion.2
  20.7 3.2 gather_fusion
  25.1 0.8 multiply_convert_fusion.4
  26.3 26.1 %scatter_fusion = f32[2,256,256]{2,1,0:T(8,128)S(1)} fusion(f32[2,256,256]{2,1,0:T(8,128)S(1)} %get-tuple-element.764, s32[512]{0:T(512)S(1)} %bitcast.154, f32[512,256]{1,0:T(8,128)S(1)} %convolution_add_fusion.5), kind=kCustom, calls=%fused_computation.6.clone.1 | custom fusion | flops 131072 | bytes 1576960 | tf_op jit(solution)/shard_map/while/body/eval_jaxpr/scatter-add | solution.py:57
  52.6 3.4 scatter_fusion.1
  56.1 3.6 scatter_custom_fusion.19
  59.7 1.2 dynamic_slice.141
  60.9 0.7 compare_select_fusion.10
  61.6 0.7 or_select_fusion.4
  62.4 2.0 gather_fusion.1
  64.3 2.0 gather_fusion.2
  66.3 3.2 gather_fusion
  70.8 0.8 multiply_convert_fusion.4
  71.9 26.1 %scatter_fusion = f32[2,256,256]{2,1,0:T(8,128)S(1)} fusion(f32[2,256,256]{2,1,0:T(8,128)S(1)} %get-tuple-element.764, s32[512]{0:T(512)S(1)} %bitcast.154, f32[512,256]{1,0:T(8,128)S(1)} %convolution_add_fusion.5), kind=kCustom, calls=%fused_computation.6.clone.1 | custom fusion | flops 131072 | bytes 1576960 | tf_op jit(solution)/shard_map/while/body/eval_jaxpr/scatter-add | solution.py:57
  98.3 3.4 scatter_fusion.1
  101.7 3.6 scatter_custom_fusion.19
  105.4 0.9 convolution_bitcast_fusion.1
  106.4 0.7 compare_convert_fusion
  107.0 1.1 fusion.16
  108.1 57.2 %all-reduce.10.cloned.1.call-done = (f32[256,256]{1,0:T(8,128)}, f32[256,256]{1,0:T(8,128)}) async-done(((f32[256,256]{1,0:T(8,128)}, f32[256,256]{1,0:T(8,128)}), (f32[256,256]{1,0:T(8,128)}, f32[256,256]{1,0:T(8,128)})) %all-reduce.10.cloned.1.call-update) | async-done | bytes 524304 | tf_op jit(solution)/shard_map/psum | solution.py:102
  165.3 1.1 multiply_reduce_fusion.2
  167.8 2.5 collective-permute-start
  171.0 11.4 %collective-permute-done = f32[256,256]{1,0:T(8,128)S(1)} collective-permute-done((f32[256,256]{1,0:T(8,128)S(1)}, f32[256,256]{1,0:T(8,128)S(1)}, u32[]{:S(2)}, u32[]{:S(2)}) %collective-permute-start) | collective-permute-done | bytes 262176 | tf_op jit(solution)/shard_map/ppermute | solution.py:12
  182.7 91.3 %while.35 = (s32[]{:T(128)}, f32[2,256,256]{2,1,0:T(8,128)S(1)}, f32[256,256]{1,0:T(8,128)S(1)}, s32[2,512]{1,0:T(2,128)}, s32[2,512]{1,0:T(2,128)}, /*index=5*/...) while((s32[]{:T(128)}, f32[2,256,256]{2,1,0:T(8,128)S(1)}, ...), condition=%wide.region_19.20_spmd, body=%wide.region_12.19_spmd.sunk | while | flops 406075392 | bytes 12921097 | solution.py:62
  183.8 0.7 compare_select_fusion.11
  184.5 0.7 or_select_fusion.5
  185.3 2.0 gather_fusion.4
  187.2 2.0 gather_fusion.5
  189.2 3.2 gather_fusion.3
  193.1 0.7 add_multiply_fusion.5
  193.7 0.8 multiply_convert_fusion.5
  194.9 26.1 %scatter_fusion.2 = f32[2,256,256]{2,1,0:T(8,128)S(1)} fusion(f32[2,256,256]{2,1,0:T(8,128)S(1)} %get-tuple-element.797, s32[512]{0:T(512)S(1)} %bitcast.155, f32[512,256]{1,0:T(8,128)S(1)} %convolution_add_fusion.6), kind=kCustom, calls=%fused_computation.9.clone.1 | custom fusion | flops 131072 | bytes 1576960 | tf_op jit(solution)/shard_map/while/body/eval_jaxpr/scatter-add | solution.py:57
  221.3 3.4 scatter_fusion.3
  224.8 3.6 scatter_custom_fusion.23
  229.5 0.7 compare_select_fusion.11
  230.2 0.7 or_select_fusion.5
  230.9 2.0 gather_fusion.4
  232.9 2.0 gather_fusion.5
  234.9 3.2 gather_fusion.3
  238.7 0.7 add_multiply_fusion.5
  239.4 0.8 multiply_convert_fusion.5
  240.6 26.1 %scatter_fusion.2 = f32[2,256,256]{2,1,0:T(8,128)S(1)} fusion(f32[2,256,256]{2,1,0:T(8,128)S(1)} %get-tuple-element.797, s32[512]{0:T(512)S(1)} %bitcast.155, f32[512,256]{1,0:T(8,128)S(1)} %convolution_add_fusion.6), kind=kCustom, calls=%fused_computation.9.clone.1 | custom fusion | flops 131072 | bytes 1576960 | tf_op jit(solution)/shard_map/while/body/eval_jaxpr/scatter-add | solution.py:57
  267.0 3.4 scatter_fusion.3
  270.5 3.6 scatter_custom_fusion.23
  274.1 2.2 convolution_add_fusion.2
  276.4 0.9 convolution_bitcast_fusion
  277.4 0.7 copy-done.25
  278.1 1.9 collective-permute-start.1
  280.0 262.6 %all-reduce.6.cloned.1.call-done = f32[2,256,256]{2,1,0:T(8,128)} async-done(((f32[2,256,256]{2,1,0:T(8,128)}), f32[2,256,256]{2,1,0:T(8,128)}) %all-reduce.6.cloned.1.call-update) | async-done | bytes 524304 | tf_op jit(solution)/shard_map/psum | solution.py:101
  542.6 2.2 multiply_subtract_fusion
  544.7 51.2 %all-reduce.8.cloned.1.call-done = (f32[256,256]{1,0:T(8,128)}, f32[256,256]{1,0:T(8,128)}) async-done(((f32[256,256]{1,0:T(8,128)}, f32[256,256]{1,0:T(8,128)}), (f32[256,256]{1,0:T(8,128)}, f32[256,256]{1,0:T(8,128)})) %all-reduce.8.cloned.1.call-update) | async-done | bytes 524304 | tf_op jit(solution)/shard_map/psum | solution.py:102
  595.9 1.1 multiply_reduce_fusion
  597.6 0.7 copy-done.16
  598.3 1.8 divide_subtract_fusion
  600.8 0.8 divide_subtract_fusion.1
  (122 shorter events, 15.3 us)
Async XLA Ops:
  7.2 158.1 %all-reduce.10.cloned.1.call-start = ((), (), s32[]{:S(2)}) async-start(), calls=%async_computation.2 | async-start | bytes 1048576 | tf_op jit(solution)/shard_map/psum | solution.py:102
  7.2 0.7 copy-start.23
  10.6 1.1 copy-start.2
  12.0 0.7 copy-start.17
  12.0 0.7 copy-start.18
  12.7 0.7 copy-start.19
  12.7 0.7 copy-start.20
  14.1 1.2 copy-start.11
  56.1 3.6 copy-start.12
  59.7 1.2 copy-start.11
  101.7 3.6 copy-start.12
  105.3 0.9 copy-start.1
  106.3 436.2 %all-reduce.6.cloned.1.call-start = ((), (), s32[]{:S(2)}) async-start(), calls=%async_computation | async-start | bytes 1048576 | tf_op jit(solution)/shard_map/psum | solution.py:101
  165.3 1.1 copy-start.9
  166.4 3.9 copy-start.13
  166.4 0.7 copy-start.24
  167.7 2.7 copy-start.21
  167.7 2.7 copy-start.3
  167.7 2.7 copy-start.5
  167.8 14.6 %collective-permute-start = (f32[256,256]{1,0:T(8,128)S(1)}, f32[256,256]{1,0:T(8,128)S(1)}, u32[]{:S(2)}, u32[]{:S(2)}) collective-permute-start(f32[256,256]{1,0:T(8,128)S(1)} %divide_subtract_fusion.3), channel_id=1, source_target_pairs={{508,0},{0,4},{4,8},{8,12},{12,16},{16,20},{20,24},{24,28},{28,32}... | collective-permute-start | bytes 786440 | tf_op jit(solution)/shard_map/ppermute | solution.py:12
  170.4 0.6 copy-start.15
  182.7 0.5 copy-start.26
  224.8 3.6 copy-start.27
  228.4 0.5 copy-start.26
  270.5 3.6 copy-start.27
  274.1 2.2 copy-start
  276.3 319.6 %all-reduce.8.cloned.1.call-start = ((), (), s32[]{:S(2)}) async-start(), calls=%async_computation.1 | async-start | bytes 1048576 | tf_op jit(solution)/shard_map/psum | solution.py:102
  276.4 266.2 %copy-start.10 = (f32[2,256,256]{2,1,0:T(8,128)S(1)}, f32[2,256,256]{2,1,0:T(8,128)}, u32[]{:S(2)}) copy-start(f32[2,256,256]{2,1,0:T(8,128)} %param.20) | copy-start | bytes 1572868
  277.3 265.2 %copy-start.7 = (f32[2,256,256]{2,1,0:T(8,128)S(1)}, f32[2,256,256]{2,1,0:T(8,128)}, u32[]{:S(2)}) copy-start(f32[2,256,256]{2,1,0:T(8,128)} %param.19) | copy-start | bytes 1572868
  277.3 0.7 copy-start.25
  278.1 322.1 %collective-permute-start.1 = (f32[256]{0:T(256)S(1)}, f32[256]{0:T(256)S(1)}, u32[]{:S(2)}, u32[]{:S(2)}) collective-permute-start(f32[256]{0:T(256)S(1)} %copy-done.25), channel_id=1, source_target_pairs={{508,0},{0,4},{4,8},{8,12},{12,16},{16,20},{20,24},{24,28},{28,32}... | collective-permute-start | bytes 3080 | tf_op jit(solution)/shard_map/ppermute | solution.py:12
  542.6 55.0 %copy-start.6 = (f32[256,256]{1,0:T(8,128)S(1)}, f32[256,256]{1,0:T(8,128)}, u32[]{:S(2)}) copy-start(f32[256,256]{1,0:T(8,128)} %get-tuple-element.559) | copy-start | bytes 786436
  544.7 52.9 %copy-start.4 = (f32[256,256]{1,0:T(8,128)S(1)}, f32[256,256]{1,0:T(8,128)}, u32[]{:S(2)}) copy-start(f32[256,256]{1,0:T(8,128)} %param.17) | copy-start | bytes 786436
  595.9 1.1 copy-start.14
  595.9 1.1 copy-start.22
  597.6 0.7 copy-start.16
  598.3 1.8 copy-start.8
Sparse Core Ops, SparseCore 0:
  106.4 58.8 all-reduce.9
  276.4 266.0 all-reduce.5
  546.4 49.4 all-reduce.7
where the time goes:
time: 609 us; the launch traced here: 608 us
  waiting for transfers between devices  382 us (63%)
  other arithmetic  158 us (26%)
  local copies, waits for them, and re-layouts  38.7 us (6%)
  between operations  14.1 us (2%)
  matrix products  9.58 us (2%)
    psum x1, waiting for transfers between devices, body(): operator_total = operator_total + lax.psum(operator_grad, ('blk', 'rep'))  263 us
    psum x2, waiting for transfers between devices, body(): left_sum, right_sum = lax.psum((left_grad, right_grad), 'rep')  108 us
    scatter-add x4, other arithmetic, step(): table_grad = table_grad.at[rel_row, src_row].add(query_grad)  104 us
    scatter-add x8, other arithmetic, step(): right_grad = right_grad.at[neg_row].add(neg_grad).at[dst_row].add(pos_grad)  28.1 us
    gather x4, local copies, waits for them, and re-layouts, batch_terms(): queries = query_table[rel_row, src_row]  12.7 us
  transfers between devices with their start and end apart: 5, of which 4 were waited for; matrix products, arithmetic and copies ran while one was open for 1% of the time, Pallas kernels for 0%

commit v1 on v0

v1 whole, which is shorter than its diff:
```python
import functools

import jax
import jax.numpy as jnp
from jax import lax
from jax.experimental import pallas as pl
from jax.experimental.pallas import tpu as pltpu
from jax.sharding import PartitionSpec as P

learn_rate = 0.1
BF = jnp.bfloat16
F32 = jnp.float32


def dot(a, b, dims):
    return lax.dot_general(a, b, ((dims[:1], dims[1:]), ((), ())), preferred_element_type=F32)


def same(rows, cols):
    shape = (rows, cols)
    return lax.broadcasted_iota(jnp.int32, shape, 0) == lax.broadcasted_iota(jnp.int32, shape, 1)


def to_column(row):
    size = row.shape[1]
    return jnp.sum(jnp.where(same(size, size), row, 0.0), axis=1, keepdims=True)


def to_row(column):
    size = column.shape[0]
    return jnp.sum(jnp.where(same(size, size), column, 0.0), axis=0, keepdims=True)


def one_hot(index_row, count):
    rows = lax.broadcasted_iota(jnp.int32, (count, index_row.shape[1]), 0)
    return jnp.where(rows == index_row, 1.0, 0.0).astype(BF)


def row_update(embedding, accum_row, gradient):
    mean = jnp.mean(gradient * gradient, axis=1, keepdims=True)
    accum = to_column(accum_row) + mean
    return embedding - learn_rate * gradient / jnp.sqrt(accum), to_row(accum)


def bucket_kernel(
    bucket, nbatch, idx_ref, left_ref, accum_ref, right_ref, right_accum_ref, op_ref, *refs
):
    if bucket == 0:
        left_out, right_out, right_accum_out, grad_out = refs[:4]
    else:
        grad_in, left_out, left_accum_out, right_out, right_accum_out, grad_out = refs[:6]
    query_t, scores_t, total, table_t = refs[-4:]
    nrel, width, _ = op_ref.shape
    rows = right_ref.shape[0]
    pairs = nrel * rows
    left = left_ref[0:rows, :]
    left_bf = left.astype(BF)
    right = right_ref[...]
    right_bf = right.astype(BF)
    for r in range(nrel):
        query_t[:, r * rows : (r + 1) * rows] = dot(op_ref[r].astype(BF), left_bf, (1, 1)).astype(BF)
    scores_t[...] = dot(right_bf, query_t[...], (1, 0))
    total[...] = jnp.zeros_like(total)

    def member_step(member, _):
        live = jnp.max(idx_ref[member, pl.ds(8 * nbatch + bucket, 1), :])

        def batch_step(batch, _):
            base = (bucket * nbatch + batch) * 4
            source = idx_ref[member, pl.ds(base, 1), :]
            target = idx_ref[member, pl.ds(base + 1, 1), :]
            relation = idx_ref[member, pl.ds(base + 2, 1), :]
            negative = idx_ref[member, pl.ds(base + 3, 1), :]
            edges = dot(one_hot(target, rows), one_hot(relation * rows + source, pairs), (1, 1))
            counts = dot(
                one_hot(negative, rows), jnp.ones((negative.shape[1], 128), BF), (1, 0)
            )
            for start in range(0, pairs, 128):
                cols = slice(start, start + 128)
                score = scores_t[:, cols]
                edge = edges[:, cols]
                top = jnp.max(jnp.where(counts > 0.0, score, -3.0e38), axis=0, keepdims=True)
                above = score - top
                small = jnp.exp(-jnp.abs(above))
                weighted = counts * small
                neg_total = jnp.sum(weighted, axis=0, keepdims=True)
                neg_scale = jnp.where(above > 0.0, small, 1.0)
                pos_exp = jnp.where(above > 0.0, 1.0, small)
                factor = edge * neg_scale / (pos_exp + neg_total * neg_scale)
                factor_sum = jnp.sum(factor, axis=0, keepdims=True)
                total[:, cols] += weighted * factor_sum - neg_total * factor
            return 0

        return lax.fori_loop(0, live, batch_step, 0)

    lax.fori_loop(0, idx_ref.shape[0], member_step, 0)

    total_bf = total[...].astype(BF)
    right_grad = dot(total_bf, query_t[...], (1, 1))
    table_t[...] = dot(right_bf, total_bf, (0, 0)).astype(BF)
    left_grad = jnp.zeros((rows, width), F32)
    for r in range(nrel):
        left_grad += dot(table_t[:, r * rows : (r + 1) * rows], op_ref[r].astype(BF), (0, 0))
    core = lax.axis_index("core")
    mine = table_t[:, pl.ds(pl.multiple_of(core * rows, rows), rows)]
    grad = dot(mine, left_bf, (1, 0))
    if bucket == 0:
        grad_out[...] = grad
        new_left, new_accum = row_update(left, accum_ref[...], left_grad)
        left_out[0:rows, :] = new_left
        left_out[rows : rows + 8, :] = jnp.broadcast_to(new_accum, (8, rows))
    else:
        grad = grad + grad_in[...]
        for half in range(2):
            grad_out[half] = grad[:, half * 128 : (half + 1) * 128].reshape(grad_out.shape[1:])
        accum = accum_ref[rows : rows + 1, :]
        left_out[...], left_accum_out[...] = row_update(left, accum, left_grad)
    right_out[...], right_accum_out[...] = row_update(right, right_accum_ref[...], right_grad)


def run_bucket(bucket, nbatch, idx, left, accum, right, right_accum, relation, grad=None):
    nrel, width, _ = relation.shape
    rows = right.shape[0]
    f32 = lambda *shape: jax.ShapeDtypeStruct(shape, F32)
    if bucket == 0:
        outs = (f32(rows + 8, width), f32(rows, width), f32(1, rows), f32(width, width))
        args = (idx, left, accum, right, right_accum, relation)
    else:
        outs = (
            f32(rows, width),
            f32(1, rows),
            f32(rows, width),
            f32(1, rows),
            f32(2, width // 4, 4, 128),
        )
        args = (idx, left, accum, right, right_accum, relation, grad)
    return pl.pallas_call(
        functools.partial(bucket_kernel, bucket, nbatch),
        out_shape=outs,
        in_specs=[pl.BlockSpec(memory_space=pltpu.VMEM)] * len(args),
        out_specs=[pl.BlockSpec(memory_space=pltpu.VMEM)] * len(outs),
        scratch_shapes=[
            pltpu.VMEM((width, nrel * rows), BF),
            pltpu.VMEM((rows, nrel * rows), F32),
            pltpu.VMEM((rows, nrel * rows), F32),
            pltpu.VMEM((width, nrel * rows), BF),
        ],
        compiler_params=pltpu.CompilerParams(vmem_limit_bytes=40 << 20),
        name=f"bucket{bucket}",
    )(*args)


def final_kernel(total_ref, relation_ref, state_ref, relation_out, state_out):
    nrel, width, _ = relation_ref.shape
    for r in range(nrel):
        for half in range(2):
            cols = slice(half * 128, (half + 1) * 128)
            grad = total_ref[r, half].reshape(width, 128)
            state = state_ref[r, :, cols] + grad * grad
            state_out[r, :, cols] = state
            relation_out[r, :, cols] = relation_ref[r, :, cols] - learn_rate * grad / jnp.sqrt(state)


def final_update(total, relation, state):
    shape = jax.ShapeDtypeStruct(relation.shape, F32)
    return pl.pallas_call(
        final_kernel,
        out_shape=(shape, shape),
        in_specs=[pl.BlockSpec(memory_space=pltpu.VMEM)] * 3,
        out_specs=[pl.BlockSpec(memory_space=pltpu.VMEM)] * 2,
        name="final_update",
    )(total, relation, state)


BLK = ("z", "y", "xl")
REP = ("xh", "core")


def body(
    left_emb,
    left_state,
    right_emb,
    right_state,
    relation,
    relation_state,
    edge_src,
    edge_dst,
    edge_rel,
    negatives,
    batch_counts,
):
    nbatch, batch = edge_src.shape[3:]
    rows, width = left_emb.shape
    blocks = lax.axis_size(BLK)
    index = jnp.stack([edge_src[0, 0], edge_dst[0, 0], edge_rel[0, 0], negatives[0, 0]], axis=2)
    index = index.reshape(8 * nbatch, batch)
    live = jnp.broadcast_to(batch_counts.reshape(2, 1), (2, batch))
    pad = -(8 * nbatch + 2) % 8
    index = jnp.concatenate([index, live, jnp.zeros((pad, batch), jnp.int32)], axis=0)
    index = lax.all_gather(index, REP, axis=0, tiled=False)

    left, right, right_accum, grad = run_bucket(
        0, nbatch, index, left_emb, left_state.reshape(1, rows), right_emb, right_state.reshape(1, rows), relation
    )
    left = lax.ppermute(left, BLK, [(i, (i + 1) % blocks) for i in range(blocks)])
    left, left_accum, right, right_accum, grad = run_bucket(
        1, nbatch, index, left, left, right, right_accum, relation, grad
    )
    grad = grad.reshape(blocks, -1, 128)
    grad = jnp.sum(lax.all_to_all(grad, BLK, 0, 0, tiled=True), axis=0)
    grad = jnp.broadcast_to(grad[None], (blocks, *grad.shape))
    grad = lax.all_to_all(grad, BLK, 0, 0, tiled=True)
    grad = lax.all_gather(grad, "core", axis=0, tiled=False)
    grad = grad.reshape(relation.shape[0], 2, width // 4, 4, 128)
    relation_new, relation_state_new = final_update(grad, relation, relation_state)
    return (
        left,
        left_accum.reshape(rows),
        right,
        right_accum.reshape(rows),
        relation_new,
        relation_state_new,
    )


def solution(mesh):
    sizes = (8, 8, 2, 2, 2)
    mesh = jax.sharding.Mesh(mesh.devices.reshape(sizes), (*BLK, *REP))
    row, edge = P(BLK, None), P(BLK, REP, None, None, None)
    in_specs = (row, P(BLK), row, P(BLK), P(), P(), edge, edge, edge, edge, P(BLK, REP, None))
    out_specs = (row, P(BLK), row, P(BLK), P(), P())
    return jax.shard_map(body, mesh=mesh, in_specs=in_specs, out_specs=out_specs, check_vma=False)
```

time: 609 us -> 96.3 us (0.16)
  waiting for transfers between devices: 382 us -> 13.9 us
  other arithmetic: 158 us -> 0.95 us
  blocking collectives: 0 us -> 59.6 us
  local copies, waits for them, and re-layouts: 38.7 us -> 3.44 us
  Pallas kernels: 0 us -> 15.4 us
  between operations: 14.1 us -> 0.69 us
  matrix products: 9.58 us -> 0 us
    psum x3 -> x0, waiting for transfers between devices: 371 us -> none  [the longest x1 263 us: body(): operator_total = operator_total + lax.psum(operator_grad, ('blk', 'rep'))]
    scatter-add x12 -> x0, other arithmetic: 132 us -> none  [the longest x4 104 us: step(): table_grad = table_grad.at[rel_row, src_row].add(query_grad)]
    all_to_all x0 -> x2, blocking collectives: none -> 40.6 us  [the longest x1 20.4 us: body(): grad = lax.all_to_all(grad, BLK, 0, 0, tiled=True)]
    gather x12 -> x0, local copies, waits for them, and re-layouts: 28.3 us -> none  [the longest x4 12.7 us: batch_terms(): queries = query_table[rel_row, src_row]]
    all_gather x0 -> x2, blocking collectives: none -> 19 us  [the longest x1 13.9 us: body(): index = lax.all_gather(index, REP, axis=0, tiled=False)]
    pallas_call x0 -> x3, Pallas kernels: none -> 15.4 us  [the longest x2 12.8 us: run_bucket(): pl.pallas_call(functools.partial(bucket_kernel, bucket, nbatch), out_shap...]
    dot_general x18 -> x0, matrix products: 9.58 us -> none  [the longest x2 3.27 us: bucket_terms(): jnp.einsum('rnk,nd->rkd', table_bf, left_bf, preferred_element_type=jnp.f...]
    convert_element_type x9 -> x0, other arithmetic: 7.21 us -> none  [the longest x4 3.21 us: batch_terms(): weights = (neg_exp / row_total[:, None] * live_flag).astype(jnp.bfloat16)]
  transfers between devices with their start and end apart: 5 -> 1, of which waited for: 4 -> 1; matrix products, arithmetic and copies ran while one was open for 1% -> 0% of each run, Pallas kernels for 0% -> 0%
where the time goes in v1:
time: 96.3 us; the launch traced here: 95.9 us
  blocking collectives  59.6 us (62%)
  Pallas kernels  15.4 us (16%)
  waiting for transfers between devices  13.9 us (14%)
  local copies, waits for them, and re-layouts  3.44 us (4%)
  starting transfers between devices  1.92 us (2%)
    all_to_all x1, blocking collectives, body(): grad = lax.all_to_all(grad, BLK, 0, 0, tiled=True)  20.4 us
    all_to_all x1, blocking collectives, body(): grad = jnp.sum(lax.all_to_all(grad, BLK, 0, 0, tiled=True), axis=0)  20.1 us
    all_gather x1, blocking collectives, body(): index = lax.all_gather(index, REP, axis=0, tiled=False)  13.9 us
    ppermute x1, waiting for transfers between devices, body(): lax.ppermute(left, BLK, [(i, (i + 1) % blocks) for i in range(blocks)])  13.9 us
    pallas_call x2, Pallas kernels, run_bucket(): pl.pallas_call(functools.partial(bucket_kernel, bucket, nbatch), out_shap...  12.8 us
    all_gather x1, blocking collectives, body(): grad = lax.all_gather(grad, 'core', axis=0, tiled=False)  5.07 us
    unnamed x14, local copies, waits for them, and re-layouts  3.21 us
    pallas_call x1, Pallas kernels, final_update(): pl.pallas_call(final_kernel, out_shape=(shape, shape), in_specs=[pl.Block...  2.6 us
  transfers between devices with their start and end apart: 1, of which 1 were waited for; matrix products, arithmetic and copies ran while one was open for 0% of the time, Pallas kernels for 0%

profile of v1, /device:TPU:1, one launch (start us, length us, event | category | flops | bytes accessed | tf_op | source)
XLA Modules:
  0.0 95.9 jit_solution(7543432350390089935)
XLA Ops:
  0.6 0.0 copy-start.6
  0.6 0.0 copy-start.5
  0.7 0.0 copy-start
  0.7 0.6 copy-done.6
  1.3 0.1 pad.1.clone
  1.4 0.1 pad.2.clone
  1.4 0.0 copy-done.5
  1.4 0.7 pad_add_fusion
  2.2 0.1 add_add_fusion
  2.3 0.0 copy-start.4
  2.3 13.9 %all-gather = s32[96,512]{1,0:T(8,128)S(1)} all-gather(s32[24,512]{1,0:T(8,128)S(1)} %add_add_fusion), channel_id=2, replica_groups=mesh['z'=8,'y'=8,'xl'=2,'xh'=2,'core'=2] {'xh','core'}, dimensions={0}, use_global_device_ids=true | all-gather | bytes 245760 | tf_op jit(solution)/shard_map/all_gather | solution.py:200
  16.2 0.0 copy-start.3
  16.2 0.0 copy-done
  16.2 0.0 copy-done.4
  16.2 0.7 copy-done.3
  16.9 0.0 copy-start.1
  16.9 0.9 copy-done.1
  17.9 0.0 copy-start.2
  17.9 0.9 copy-done.2
  18.8 6.0 %bucket0.1 = (f32[264,256]{1,0:T(8,128)S(1)}, f32[256,256]{1,0:T(8,128)S(1)}, f32[1,256]{1,0:T(1,128)S(1)}, f32[256,256]{1,0:T(8,128)S(1)}) custom-call(s32[4,24,512]{2,1,0:T(8,128)S(1)} %bitcast.12, f32[256,256]{1,0:T(8,128)S(1)} %copy-done.1, f32[1,256]{1,0:T(1,128)S(1)} %bitcast.15, f32[256,256]{1,0:T(8,128)S(1)} %copy-done.2, f32[1,256]{1,0:T(1,128)S(1)} %bitcast.16, ...), custom_call_target="tpu_custom_call" | custom-call | tf_op jit(solution)/shard_map/bucket0/pallas_call | solution.py:137
  24.8 1.9 %collective-permute-start = (f32[264,256]{1,0:T(8,128)S(1)}, f32[264,256]{1,0:T(8,128)S(1)}, u32[]{:S(2)}, u32[]{:S(2)}) collective-permute-start(f32[264,256]{1,0:T(8,128)S(1)} %get-tuple-element.17), channel_id=1, source_target_pairs={{0,4},{4,8},{8,12},{12,16},{16,20},{20,24},{24,28},{28,32},{32,36}... | collective-permute-start | bytes 811016 | tf_op jit(solution)/shard_map/ppermute | solution.py:205
  26.8 13.9 %collective-permute-done.left_ref.accum_ref = f32[264,256]{1,0:T(8,128)S(1)} collective-permute-done((f32[264,256]{1,0:T(8,128)S(1)}, f32[264,256]{1,0:T(8,128)S(1)}, u32[]{:S(2)}, u32[]{:S(2)}) %collective-permute-start) | collective-permute-done | bytes 270368 | tf_op jit(solution)/shard_map/ppermute | solution.py:205
  40.6 6.8 %bucket1.1 = (f32[256,256]{1,0:T(8,128)}, f32[1,256]{1,0:T(1,128)}, f32[256,256]{1,0:T(8,128)}, f32[1,256]{1,0:T(1,128)}, f32[2,64,4,128]{3,2,1,0:T(4,128)S(1)}) custom-call(s32[4,24,512]{2,1,0:T(8,128)S(1)} %bitcast.13, f32[264,256]{1,0:T(8,128)S(1)} %collective-permute-done.left_ref.accum_ref, f32[264,256]{1,0:T(8,128)S(1)} %collective-permute-done.left_ref.accum_ref, ...), custom_call_target="tpu_custom_call" | custom-call | tf_op jit(solution)/shard_map/bucket1/pallas_call | solution.py:137
  47.5 20.1 %all_to_all.10 = f32[128,4,128]{2,1,0:T(4,128)S(1)} all-to-all(f32[128,4,128]{2,1,0:T(4,128)S(1)} %bitcast.14), channel_id=1, replica_groups=mesh['z'=8,'y'=8,'xl'=2,'xh'=2,'core'=2] {'z','y','xl'}, dimensions={0} | all-to-all | bytes 524288 | tf_op jit(solution)/shard_map/all_to_all | solution.py:210
  67.6 0.1 reduce_sum.9
  67.8 20.4 %all_to_all.11 = f32[128,4,128]{2,1,0:T(4,128)S(1)} all-to-all(f32[128,4,128]{2,1,0:T(4,128)S(1)} %broadcast_in_dim.19), channel_id=1, replica_groups=mesh['z'=8,'y'=8,'xl'=2,'xh'=2,'core'=2] {'z','y','xl'}, dimensions={0} | all-to-all | bytes 524288 | tf_op jit(solution)/shard_map/all_to_all | solution.py:212
  88.2 5.1 %all-gather.1 = f32[256,4,128]{2,1,0:T(4,128)} all-gather(f32[128,4,128]{2,1,0:T(4,128)S(1)} %all_to_all.11), channel_id=3, replica_groups=mesh['z'=8,'y'=8,'xl'=2,'xh'=2,'core'=2] {'core'}, dimensions={0}, use_global_device_ids=true | all-gather | bytes 786432 | tf_op jit(solution)/shard_map/all_gather | solution.py:213
  93.3 2.6 %final_update.1 = (f32[2,256,256]{2,1,0:T(8,128)}, f32[2,256,256]{2,1,0:T(8,128)}) custom-call(f32[2,2,64,4,128]{4,3,2,1,0:T(4,128)} %bitcast.17, f32[2,256,256]{2,1,0:T(8,128)} %relation_ref.1, f32[2,256,256]{2,1,0:T(8,128)} %state_ref.1), custom_call_target="tpu_custom_call" | custom-call | tf_op jit(solution)/shard_map/final_update/pallas_call | solution.py:166
  (4 shorter events, 0.1 us)
Async XLA Ops:
  0.6 0.7 copy-start.6
  0.6 0.8 copy-start.5
  0.7 15.6 %copy-start = (f32[2,256,256]{2,1,0:T(8,128)S(1)}, f32[2,256,256]{2,1,0:T(8,128)}, u32[]{:S(2)}) copy-start(f32[2,256,256]{2,1,0:T(8,128)} %relation_ref.1) | copy-start | bytes 1572868
  2.3 14.0 %copy-start.4 = (f32[256]{0:T(256)S(1)}, f32[256]{0:T(256)}, u32[]{:S(2)}) copy-start(f32[256]{0:T(256)} %param.14) | copy-start | bytes 3076
  16.2 0.7 copy-start.3
  16.9 0.9 copy-start.1
  17.9 0.9 copy-start.2
  24.8 15.8 %collective-permute-start = (f32[264,256]{1,0:T(8,128)S(1)}, f32[264,256]{1,0:T(8,128)S(1)}, u32[]{:S(2)}, u32[]{:S(2)}) collective-permute-start(f32[264,256]{1,0:T(8,128)S(1)} %get-tuple-element.17), channel_id=1, source_target_pairs={{0,4},{4,8},{8,12},{12,16},{16,20},{20,24},{24,28},{28,32},{32,36}... | collective-permute-start | bytes 811016 | tf_op jit(solution)/shard_map/ppermute | solution.py:205

commit v2 on v1

v2 whole, which is shorter than its diff:
```python
import functools

import jax
import jax.numpy as jnp
from jax import lax
from jax.experimental import pallas as pl
from jax.experimental.pallas import tpu as pltpu
from jax.sharding import PartitionSpec as P

learn_rate = 0.1
BF = jnp.bfloat16
F32 = jnp.float32
BLK = ("z", "y", "xl")
REP = ("xh", "core")
SLOTS = 4


def dot(a, b, dims):
    return lax.dot_general(a, b, ((dims[:1], dims[1:]), ((), ())), preferred_element_type=F32)


def same(size):
    shape = (size, size)
    return lax.broadcasted_iota(jnp.int32, shape, 0) == lax.broadcasted_iota(jnp.int32, shape, 1)


def to_column(row):
    return jnp.sum(jnp.where(same(row.shape[1]), row, 0.0), axis=1, keepdims=True)


def to_row(column):
    return jnp.sum(jnp.where(same(column.shape[0]), column, 0.0), axis=0, keepdims=True)


def one_hot(index_row, count):
    rows = lax.broadcasted_iota(jnp.int16, (count, index_row.shape[1]), 0)
    return jnp.where(rows == index_row.astype(jnp.int16), BF(1.0), BF(0.0))


def row_update(embedding, accum, gradient):
    accum = accum + jnp.mean(gradient * gradient, axis=1, keepdims=True)
    return embedding - learn_rate * gradient / jnp.sqrt(accum), accum


def count_batch(idx_ref, member, base, rows, pairs):
    source = idx_ref[member, pl.ds(base, 1), :]
    target = idx_ref[member, pl.ds(base + 1, 1), :]
    relation = idx_ref[member, pl.ds(base + 2, 1), :]
    negative = idx_ref[member, pl.ds(base + 3, 1), :]
    edges = dot(one_hot(target, rows), one_hot(relation * rows + source, pairs), (1, 1))
    counts = dot(one_hot(negative, rows), jnp.ones((negative.shape[1], 128), BF), (1, 0))
    return edges, counts


def each_live_batch(idx_ref, bucket, nbatch, step):
    def member_step(member, slot):
        live = jnp.max(idx_ref[member, pl.ds(8 * nbatch + bucket, 1), :])

        def batch_step(batch, slot):
            step(member, (bucket * nbatch + batch) * 4, slot)
            return slot + 1

        return lax.fori_loop(0, live, batch_step, slot)

    lax.fori_loop(0, idx_ref.shape[0], member_step, 0)


def score_grad(scores_t, edges_of, counts, total):
    for start in range(0, scores_t.shape[1], 128):
        cols = slice(start, start + 128)
        score = scores_t[:, cols]
        top = jnp.max(jnp.where(counts > 0.0, score, -3.0e38), axis=0, keepdims=True)
        above = score - top
        small = jnp.exp(-jnp.abs(above))
        weighted = counts * small
        neg_total = jnp.sum(weighted, axis=0, keepdims=True)
        neg_scale = jnp.where(above > 0.0, small, 1.0)
        pos_exp = jnp.where(above > 0.0, 1.0, small)
        factor = edges_of(cols) * neg_scale / (pos_exp + neg_total * neg_scale)
        factor_sum = jnp.sum(factor, axis=0, keepdims=True)
        total[:, cols] += weighted * factor_sum - neg_total * factor


def queries_and_scores(left_bf, right_bf, op_ref, query_t, scores_t):
    rows = left_bf.shape[0]
    for r in range(op_ref.shape[0]):
        cols = slice(r * rows, (r + 1) * rows)
        query = dot(op_ref[r].astype(BF), left_bf, (1, 1)).astype(BF)
        query_t[:, cols] = query
        scores_t[:, cols] = dot(right_bf, query, (1, 0))


def first_kernel(nbatch, idx_ref, left_ref, accum_ref, right_ref, op_ref, left_out, query_t, grad_bf, scores_t, total):
    nrel = op_ref.shape[0]
    rows, width = left_ref.shape
    half = rows // 2
    right_bf = right_ref[...].astype(BF)
    queries_and_scores(left_ref[...].astype(BF), right_bf, op_ref, query_t, scores_t)
    total[...] = jnp.zeros_like(total)

    def step(member, base, slot):
        edges, counts = count_batch(idx_ref, member, base, rows, nrel * rows)
        score_grad(scores_t, lambda cols: edges[:, cols], counts, total)

    each_live_batch(idx_ref, 0, nbatch, step)
    grad_bf[...] = total[...].astype(BF)
    first = lax.axis_index("core") * half
    left_grad = jnp.zeros((half, width), F32)
    for r in range(nrel):
        cols = pl.ds(pl.multiple_of(r * rows + first, half), half)
        table_t = dot(right_bf, grad_bf[:, cols], (0, 0)).astype(BF)
        left_grad += dot(table_t, op_ref[r].astype(BF), (0, 0))
    mine = pl.ds(pl.multiple_of(first, half), half)
    accum = to_column(accum_ref[:, mine])
    left_out[0:half, :], accum = row_update(left_ref[mine, :], accum, left_grad)
    accum = jnp.concatenate([to_row(accum)] * (width // half), axis=1)
    left_out[half : half + 8, :] = jnp.broadcast_to(accum, (8, width))


def between_kernel(
    nbatch, idx_ref, left_ref, right_ref, accum_ref, query_t, grad_bf, op_ref, right_out, accum_out, grad_out, edges_out, counts_out
):
    rows = right_ref.shape[0]
    pairs = query_t.shape[1]

    def step(member, base, slot):
        edges_out[slot], counts_out[slot] = count_batch(idx_ref, member, base, rows, pairs)

    each_live_batch(idx_ref, 1, nbatch, step)
    right = right_ref[...]
    right_grad = dot(grad_bf[...], query_t[...], (1, 1))
    cols = pl.ds(pl.multiple_of(lax.axis_index("core") * rows, rows), rows)
    table_t = dot(right.astype(BF), grad_bf[:, cols], (0, 0)).astype(BF)
    grad_out[...] = dot(table_t, left_ref[...].astype(BF), (1, 0))
    right_out[...], accum = row_update(right, to_column(accum_ref[...]), right_grad)
    accum_out[...] = to_row(accum)


def second_kernel(
    nbatch, idx_ref, edges_ref, counts_ref, left_ref, right_ref, accum_ref, op_ref, grad_ref,
    left_out, left_accum_out, right_out, right_accum_out, grad_out, query_t, scores_t, total, grad_bf, table_t
):
    nrel = op_ref.shape[0]
    rows, width = right_ref.shape
    half = rows // 2
    left = jnp.concatenate([left_ref[0, 0:half, :], left_ref[1, 0:half, :]], axis=0)
    left_accum = jnp.concatenate([left_ref[0, half : half + 1, 0:half], left_ref[1, half : half + 1, 0:half]], axis=1)
    right = right_ref[...]
    left_bf, right_bf = left.astype(BF), right.astype(BF)
    queries_and_scores(left_bf, right_bf, op_ref, query_t, scores_t)
    total[...] = jnp.zeros_like(total)
    live = 0
    for member in range(idx_ref.shape[0]):
        live += idx_ref[member, 8 * nbatch + 1 : 8 * nbatch + 2, :]

    def step(slot, _):
        score_grad(scores_t, lambda cols: edges_ref[slot, :, cols], counts_ref[slot], total)
        return 0

    lax.fori_loop(0, jnp.max(live), step, 0)
    grad_bf[...] = total[...].astype(BF)
    table_t[...] = dot(right_bf, grad_bf[...], (0, 0)).astype(BF)
    mine = pl.ds(pl.multiple_of(lax.axis_index("core") * rows, rows), rows)
    grad = dot(table_t[:, mine], left_bf, (1, 0)) + grad_ref[...]
    for part in range(2):
        grad_out[part] = grad[:, part * 128 : (part + 1) * 128].reshape(grad_out.shape[1:])
    left_grad = jnp.zeros((rows, width), F32)
    for r in range(nrel):
        left_grad += dot(table_t[:, r * rows : (r + 1) * rows], op_ref[r].astype(BF), (0, 0))
    left_out[...], accum = row_update(left, to_column(left_accum), left_grad)
    left_accum_out[...] = to_row(accum)
    right_grad = dot(grad_bf[...], query_t[...], (1, 1))
    right_out[...], accum = row_update(right, to_column(accum_ref[...]), right_grad)
    right_accum_out[...] = to_row(accum)


def final_kernel(total_ref, relation_ref, state_ref, relation_out, state_out):
    nrel, width, _ = relation_ref.shape
    for r in range(nrel):
        for part in range(2):
            cols = slice(part * 128, (part + 1) * 128)
            grad = total_ref[r, part].reshape(width, 128)
            state = state_ref[r, :, cols] + grad * grad
            state_out[r, :, cols] = state
            relation_out[r, :, cols] = relation_ref[r, :, cols] - learn_rate * grad / jnp.sqrt(state)


def f32(*shape):
    return jax.ShapeDtypeStruct(shape, F32)


def call(kernel, name, outs, args, scratch=(), flops=0):
    return pl.pallas_call(
        kernel,
        out_shape=outs,
        in_specs=[pl.BlockSpec(memory_space=pltpu.VMEM)] * len(args),
        out_specs=[pl.BlockSpec(memory_space=pltpu.VMEM)] * len(outs),
        scratch_shapes=[pltpu.VMEM(shape, dtype) for shape, dtype in scratch],
        compiler_params=pltpu.CompilerParams(vmem_limit_bytes=30 << 20),
        cost_estimate=pl.CostEstimate(flops=flops, bytes_accessed=4 << 20, transcendentals=0),
        name=name,
    )(*args)


def buckets(index, left, left_accum, right, right_accum, relation, nbatch, move):
    nrel, width, _ = relation.shape
    rows = left.shape[0]
    pairs = nrel * rows
    pair_bf = jax.ShapeDtypeStruct((rows, pairs), BF)
    left_half, query_t, grad_bf = call(
        functools.partial(first_kernel, nbatch),
        "bucket0_left",
        (f32(rows // 2 + 8, width), jax.ShapeDtypeStruct((width, pairs), BF), pair_bf),
        (index, left, left_accum, right, relation),
        [((rows, pairs), F32), ((rows, pairs), F32)],
        flops=2 << 30,
    )
    moved = move(left_half)
    right, right_accum, grad, edges, counts = call(
        functools.partial(between_kernel, nbatch),
        "bucket0_right",
        (f32(rows, width), f32(1, rows), f32(width, width), f32(SLOTS, rows, pairs), f32(SLOTS, rows, 128)),
        (index, left, right, right_accum, query_t, grad_bf, relation),
        flops=1 << 30,
    )
    moved = lax.all_gather(moved, "core", axis=0, tiled=False)
    return call(
        functools.partial(second_kernel, nbatch),
        "bucket1",
        (f32(rows, width), f32(1, rows), f32(rows, width), f32(1, rows), f32(2, width // 4, 4, 128)),
        (index, edges, counts, moved, right, right_accum, relation, grad),
        [((width, pairs), BF), ((rows, pairs), F32), ((rows, pairs), F32), ((rows, pairs), BF), ((width, pairs), BF)],
        flops=2 << 30,
    )


def body(
    left_emb,
    left_state,
    right_emb,
    right_state,
    relation,
    relation_state,
    edge_src,
    edge_dst,
    edge_rel,
    negatives,
    batch_counts,
):
    nbatch, batch = edge_src.shape[3:]
    rows, width = left_emb.shape
    blocks = lax.axis_size(BLK)
    index = jnp.stack([edge_src[0, 0], edge_dst[0, 0], edge_rel[0, 0], negatives[0, 0]], axis=2)
    index = index.reshape(8 * nbatch, batch)
    live = jnp.broadcast_to(batch_counts.reshape(2, 1), (2, batch))
    pad = -(8 * nbatch + 2) % 8
    index = jnp.concatenate([index, live, jnp.zeros((pad, batch), jnp.int32)], axis=0)
    index = lax.all_gather(index, REP, axis=0, tiled=False)
    route = [(i, (i + 1) % blocks) for i in range(blocks)]
    left, left_accum, right, right_accum, grad = buckets(
        index,
        left_emb,
        left_state.reshape(1, rows),
        right_emb,
        right_state.reshape(1, rows),
        relation,
        nbatch,
        lambda half: lax.ppermute(half, BLK, route),
    )
    grad = grad.reshape(blocks, -1, 128)
    grad = jnp.sum(lax.all_to_all(grad, BLK, 0, 0, tiled=True), axis=0)
    grad = jnp.broadcast_to(grad[None], (blocks, *grad.shape))
    grad = lax.all_to_all(grad, BLK, 0, 0, tiled=True)
    grad = lax.all_gather(grad, "core", axis=0, tiled=False)
    grad = grad.reshape(relation.shape[0], 2, width // 4, 4, 128)
    relation_new, relation_state_new = call(
        final_kernel, "final_update", (f32(*relation.shape),) * 2, (grad, relation, relation_state)
    )
    return (
        left,
        left_accum.reshape(rows),
        right,
        right_accum.reshape(rows),
        relation_new,
        relation_state_new,
    )


def solution(mesh):
    sizes = (8, 8, 2, 2, 2)
    mesh = jax.sharding.Mesh(mesh.devices.reshape(sizes), (*BLK, *REP))
    row, edge = P(BLK, None), P(BLK, REP, None, None, None)
    in_specs = (row, P(BLK), row, P(BLK), P(), P(), edge, edge, edge, edge, P(BLK, REP, None))
    out_specs = (row, P(BLK), row, P(BLK), P(), P())
    return jax.shard_map(body, mesh=mesh, in_specs=in_specs, out_specs=out_specs, check_vma=False)
```

time: 96.3 us -> 93.3 us (0.969)
  Pallas kernels: 15.4 us -> 10.8 us
  blocking collectives: 59.6 us -> 64.1 us
  waiting for transfers between devices: 13.9 us -> 10 us
  local copies, waits for them, and re-layouts: 3.44 us -> 4.51 us
    pallas_call x3 -> x4, Pallas kernels: 15.4 us -> 10.8 us  [call(): pl.pallas_call(kernel, out_shape=outs, in_specs=[pl.BlockSpec(memory_spac...]
    ppermute x1, waiting for transfers between devices: 13.9 us -> 10 us  [body(): lax.ppermute(half, BLK, route)]
    all_to_all x1, blocking collectives: 20.1 us -> 23.3 us  [body(): grad = jnp.sum(lax.all_to_all(grad, BLK, 0, 0, tiled=True), axis=0)]
    all_gather x0 -> x1, blocking collectives: none -> 2.28 us  [buckets(): moved = lax.all_gather(moved, 'core', axis=0, tiled=False)]
  transfers between devices with their start and end apart: 1 -> 1, of which waited for: 1 -> 1; matrix products, arithmetic and copies ran while one was open for 0% -> 0% of each run, Pallas kernels for 0% -> 2%
where the time goes in v2:
time: 93.3 us; the launch traced here: 92.9 us
  blocking collectives  64.1 us (69%)
  Pallas kernels  10.8 us (12%)
  waiting for transfers between devices  10 us (11%)
  local copies, waits for them, and re-layouts  4.51 us (5%)
  starting transfers between devices  1.92 us (2%)
  other arithmetic  0.97 us (1%)
    all_to_all x1, blocking collectives, body(): grad = jnp.sum(lax.all_to_all(grad, BLK, 0, 0, tiled=True), axis=0)  23.3 us
    all_to_all x1, blocking collectives, body(): grad = lax.all_to_all(grad, BLK, 0, 0, tiled=True)  19.8 us
    all_gather x1, blocking collectives, body(): index = lax.all_gather(index, REP, axis=0, tiled=False)  13.8 us
    pallas_call x4, Pallas kernels, call(): pl.pallas_call(kernel, out_shape=outs, in_specs=[pl.BlockSpec(memory_spac...  10.8 us
    ppermute x1, waiting for transfers between devices, body(): lax.ppermute(half, BLK, route)  10 us
    all_gather x1, blocking collectives, body(): grad = lax.all_gather(grad, 'core', axis=0, tiled=False)  4.94 us
    unnamed x14, local copies, waits for them, and re-layouts  3.63 us
    all_gather x1, blocking collectives, buckets(): moved = lax.all_gather(moved, 'core', axis=0, tiled=False)  2.28 us
  transfers between devices with their start and end apart: 1, of which 1 were waited for; matrix products, arithmetic and copies ran while one was open for 0% of the time, Pallas kernels for 2%

profile of v2, /device:TPU:1, one launch (start us, length us, event | category | flops | bytes accessed | tf_op | source)
XLA Modules:
  0.0 92.9 jit_solution(12706222824822060081)
XLA Ops:
  0.6 0.7 pad.1.clone
  1.4 0.1 pad.2.clone
  1.4 0.7 pad_add_fusion
  2.2 0.1 add_add_fusion
  2.3 13.8 %all-gather = s32[96,512]{1,0:T(8,128)S(1)} all-gather(s32[24,512]{1,0:T(8,128)S(1)} %add_add_fusion), channel_id=2, replica_groups=mesh['z'=8,'y'=8,'xl'=2,'xh'=2,'core'=2] {'xh','core'}, dimensions={0}, use_global_device_ids=true | all-gather | bytes 245760 | tf_op jit(solution)/shard_map/all_gather | solution.py:258
  16.1 0.0 copy-start
  16.1 1.0 %copy-done = f32[2,256,256]{2,1,0:T(8,128)S(1)} copy-done((f32[2,256,256]{2,1,0:T(8,128)S(1)}, f32[2,256,256]{2,1,0:T(8,128)}, u32[]{:S(2)}) %copy-start) | copy-done | bytes 524312
  17.2 0.0 copy-start.3
  17.2 0.9 %copy-done.3 = f32[256,256]{1,0:T(8,128)S(1)} copy-done((f32[256,256]{1,0:T(8,128)S(1)}, f32[256,256]{1,0:T(8,128)}, u32[]{:S(2)}) %copy-start.3) | copy-done | bytes 262168
  18.1 0.0 copy-start.4
  18.1 0.9 %copy-done.4 = f32[256,256]{1,0:T(8,128)S(1)} copy-done((f32[256,256]{1,0:T(8,128)S(1)}, f32[256,256]{1,0:T(8,128)}, u32[]{:S(2)}) %copy-start.4) | copy-done | bytes 262168
  19.1 0.0 copy-start.5
  19.1 0.7 copy-done.5
  19.7 0.0 copy-start.1
  19.7 0.0 copy-start.6
  19.7 4.1 %bucket0_left.1 = (f32[136,256]{1,0:T(8,128)S(1)}, bf16[256,512]{1,0:T(8,128)(2,1)S(1)}, bf16[256,512]{1,0:T(8,128)(2,1)S(1)}) custom-call(s32[4,24,512]{2,1,0:T(8,128)S(1)} %bitcast.16, f32[256,256]{1,0:T(8,128)S(1)} %copy-done.3, f32[1,256]{1,0:T(1,128)S(1)} %bitcast.19, f32[256,256]{1,0:T(8,128)S(1)} %copy-done.4, f32[2,256,256]{2,1,0:T(8,128)S(1)} %copy-done), custom_call_target="tpu_custom_call" | custom-call | flops 2147483648 | bytes 4194304 | tf_op jit(solution)/shard_map/bucket0_left/pallas_call | solution.py:193
  23.8 1.9 %collective-permute-start = (f32[136,256]{1,0:T(8,128)S(1)}, f32[136,256]{1,0:T(8,128)S(1)}, u32[]{:S(2)}, u32[]{:S(2)}) collective-permute-start(f32[136,256]{1,0:T(8,128)S(1)} %get-tuple-element.25), channel_id=1, source_target_pairs={{0,4},{4,8},{8,12},{12,16},{16,20},{20,24},{24,28},{28,32},{32,36}... | collective-permute-start | bytes 417800 | tf_op jit(solution)/shard_map/ppermute | solution.py:268
  25.8 0.0 copy-done.1
  25.8 0.0 copy-done.6
  25.8 2.1 %bucket0_right.1 = (f32[256,256]{1,0:T(8,128)S(1)}, f32[1,256]{1,0:T(1,128)S(1)}, f32[256,256]{1,0:T(8,128)S(1)}, f32[4,256,512]{2,1,0:T(8,128)S(1)}, f32[4,256,128]{2,1,0:T(8,128)S(1)}) custom-call(s32[4,24,512]{2,1,0:T(8,128)S(1)} %bitcast.17, f32[256,256]{1,0:T(8,128)S(1)} %copy-done.3, f32[256,256]{1,0:T(8,128)S(1)} %copy-done.4, f32[1,256]{1,0:T(1,128)S(1)} %bitcast.20, ...), custom_call_target="tpu_custom_call" | custom-call | flops 1073741824 | bytes 4194304 | tf_op jit(solution)/shard_map/bucket0_right/pallas_call | solution.py:193
  27.9 10.0 %collective-permute-done = f32[136,256]{1,0:T(8,128)S(1)} collective-permute-done((f32[136,256]{1,0:T(8,128)S(1)}, f32[136,256]{1,0:T(8,128)S(1)}, u32[]{:S(2)}, u32[]{:S(2)}) %collective-permute-start) | collective-permute-done | bytes 139296 | tf_op jit(solution)/shard_map/ppermute | solution.py:268
  37.9 2.3 %all-gather.1 = f32[272,256]{1,0:T(8,128)S(1)} all-gather(f32[136,256]{1,0:T(8,128)S(1)} %collective-permute-done), channel_id=3, replica_groups=mesh['z'=8,'y'=8,'xl'=2,'xh'=2,'core'=2] {'core'}, dimensions={0}, use_global_device_ids=true | all-gather | bytes 417792 | tf_op jit(solution)/shard_map/all_gather | solution.py:226
  40.2 3.4 %bucket1.1 = (f32[256,256]{1,0:T(8,128)}, f32[1,256]{1,0:T(1,128)}, f32[256,256]{1,0:T(8,128)}, f32[1,256]{1,0:T(1,128)}, f32[2,64,4,128]{3,2,1,0:T(4,128)S(1)}) custom-call(s32[4,24,512]{2,1,0:T(8,128)S(1)} %bitcast.18, f32[4,256,512]{2,1,0:T(8,128)S(1)} %get-tuple-element.23.edges_ref, f32[4,256,128]{2,1,0:T(8,128)S(1)} %get-tuple-element.24.counts_ref, ...), custom_call_target="tpu_custom_call" | custom-call | flops 2147483648 | bytes 4194304 | tf_op jit(solution)/shard_map/bucket1/pallas_call | solution.py:193
  43.5 0.0 copy-start.2
  43.5 23.3 %all_to_all.10 = f32[128,4,128]{2,1,0:T(4,128)S(1)} all-to-all(f32[128,4,128]{2,1,0:T(4,128)S(1)} %bitcast.15), channel_id=1, replica_groups=mesh['z'=8,'y'=8,'xl'=2,'xh'=2,'core'=2] {'z','y','xl'}, dimensions={0} | all-to-all | bytes 524288 | tf_op jit(solution)/shard_map/all_to_all | solution.py:271
  66.8 0.1 reduce_sum.9
  67.0 19.8 %all_to_all.11 = f32[128,4,128]{2,1,0:T(4,128)S(1)} all-to-all(f32[128,4,128]{2,1,0:T(4,128)S(1)} %broadcast_in_dim.19), channel_id=1, replica_groups=mesh['z'=8,'y'=8,'xl'=2,'xh'=2,'core'=2] {'z','y','xl'}, dimensions={0} | all-to-all | bytes 524288 | tf_op jit(solution)/shard_map/all_to_all | solution.py:273
  86.7 4.9 %all-gather.2 = f32[256,4,128]{2,1,0:T(4,128)S(1)} all-gather(f32[128,4,128]{2,1,0:T(4,128)S(1)} %all_to_all.11), channel_id=4, replica_groups=mesh['z'=8,'y'=8,'xl'=2,'xh'=2,'core'=2] {'core'}, dimensions={0}, use_global_device_ids=true | all-gather | bytes 786432 | tf_op jit(solution)/shard_map/all_gather | solution.py:274
  91.7 0.0 copy-done.2
  91.7 1.2 %final_update.1 = (f32[2,256,256]{2,1,0:T(8,128)}, f32[2,256,256]{2,1,0:T(8,128)}) custom-call(f32[2,2,64,4,128]{4,3,2,1,0:T(4,128)S(1)} %bitcast.13, f32[2,256,256]{2,1,0:T(8,128)S(1)} %copy-done.1, f32[2,256,256]{2,1,0:T(8,128)S(1)} %copy-done.2), custom_call_target="tpu_custom_call" | custom-call | bytes 4194304 | tf_op jit(solution)/shard_map/final_update/pallas_call | solution.py:193
  (4 shorter events, 0.1 us)
Async XLA Ops:
  16.1 1.0 %copy-start = (f32[2,256,256]{2,1,0:T(8,128)S(1)}, f32[2,256,256]{2,1,0:T(8,128)}, u32[]{:S(2)}) copy-start(f32[2,256,256]{2,1,0:T(8,128)} %relation_ref.1) | copy-start | bytes 1572868
  17.2 0.9 %copy-start.3 = (f32[256,256]{1,0:T(8,128)S(1)}, f32[256,256]{1,0:T(8,128)}, u32[]{:S(2)}) copy-start(f32[256,256]{1,0:T(8,128)} %left_ref.3) | copy-start | bytes 786436
  18.1 0.9 %copy-start.4 = (f32[256,256]{1,0:T(8,128)S(1)}, f32[256,256]{1,0:T(8,128)}, u32[]{:S(2)}) copy-start(f32[256,256]{1,0:T(8,128)} %right_ref.3) | copy-start | bytes 786436
  19.1 0.7 copy-start.5
  19.7 6.0 %copy-start.1 = (f32[2,256,256]{2,1,0:T(8,128)S(1)}, f32[2,256,256]{2,1,0:T(8,128)}, u32[]{:S(2)}) copy-start(f32[2,256,256]{2,1,0:T(8,128)} %relation_ref.1) | copy-start | bytes 1572868
  19.7 6.0 %copy-start.6 = (f32[256]{0:T(256)S(1)}, f32[256]{0:T(256)}, u32[]{:S(2)}) copy-start(f32[256]{0:T(256)} %param.14) | copy-start | bytes 3076
  23.8 14.1 %collective-permute-start = (f32[136,256]{1,0:T(8,128)S(1)}, f32[136,256]{1,0:T(8,128)S(1)}, u32[]{:S(2)}, u32[]{:S(2)}) collective-permute-start(f32[136,256]{1,0:T(8,128)S(1)} %get-tuple-element.25), channel_id=1, source_target_pairs={{0,4},{4,8},{8,12},{12,16},{16,20},{20,24},{24,28},{28,32},{32,36}... | collective-permute-start | bytes 417800 | tf_op jit(solution)/shard_map/ppermute | solution.py:268
  43.5 48.2 %copy-start.2 = (f32[2,256,256]{2,1,0:T(8,128)S(1)}, f32[2,256,256]{2,1,0:T(8,128)}, u32[]{:S(2)}) copy-start(f32[2,256,256]{2,1,0:T(8,128)} %state_ref.1) | copy-start | bytes 1572868

commit v3 on v2

--- a/solution.py
+++ b/solution.py
@@ -62,7 +62,7 @@
 
         return lax.fori_loop(0, live, batch_step, slot)
 
-    lax.fori_loop(0, idx_ref.shape[0], member_step, 0)
+    return lax.fori_loop(0, idx_ref.shape[0], member_step, 0)
 
 
 def score_grad(scores_t, edges_of, counts, total):
@@ -90,19 +90,49 @@
         scores_t[:, cols] = dot(right_bf, query, (1, 0))
 
 
-def first_kernel(nbatch, idx_ref, left_ref, accum_ref, right_ref, op_ref, left_out, query_t, grad_bf, scores_t, total):
+def gather_kernel(nbatch, *refs):
+    sources, out_ref, buffers, sems = refs[:5], refs[5], refs[6:11], refs[11]
+    copies = [pltpu.make_async_copy(a, b, sems.at[i]) for i, (a, b) in enumerate(zip(sources, buffers))]
+    for copy in copies:
+        copy.start()
+    out_ref[8 * nbatch :, :] = jnp.zeros_like(out_ref[8 * nbatch :, :])
+    for copy in copies:
+        copy.wait()
+    *buffers, live_ref = buffers
+    for bucket in range(2):
+        row = 8 * nbatch + bucket
+        out_ref[row : row + 1, :] = jnp.full((1, out_ref.shape[1]), live_ref[0, 0, bucket])
+    for bucket in range(2):
+        for batch in range(nbatch):
+            for i, buffer in enumerate(buffers):
+                row = (bucket * nbatch + batch) * 4 + i
+                out_ref[row : row + 1, :] = buffer[0, 0, bucket, batch : batch + 1, :]
+
+
+def first_kernel(nbatch, idx_ref, left_hbm, accum_hbm, right_hbm, op_hbm, left_out, query_t, grad_bf, left_ref, accum_ref, right_ref, op_ref, scores_t, total, edges_ref, counts_ref, sems):
+    pairs = ((op_hbm, op_ref), (left_hbm, left_ref), (right_hbm, right_ref), (accum_hbm, accum_ref))
+    copies = [pltpu.make_async_copy(*pair, sems.at[i]) for i, pair in enumerate(pairs)]
+    for copy in copies:
+        copy.start()
     nrel = op_ref.shape[0]
     rows, width = left_ref.shape
     half = rows // 2
+
+    def count(member, base, slot):
+        edges_ref[slot], counts_ref[slot] = count_batch(idx_ref, member, base, rows, nrel * rows)
+
+    live = each_live_batch(idx_ref, 0, nbatch, count)
+    for copy in copies:
+        copy.wait()
     right_bf = right_ref[...].astype(BF)
     queries_and_scores(left_ref[...].astype(BF), right_bf, op_ref, query_t, scores_t)
     total[...] = jnp.zeros_like(total)
 
-    def step(member, base, slot):
-        edges, counts = count_batch(idx_ref, member, base, rows, nrel * rows)
-        score_grad(scores_t, lambda cols: edges[:, cols], counts, total)
-
-    each_live_batch(idx_ref, 0, nbatch, step)
+    def step(slot, _):
+        score_grad(scores_t, lambda cols: edges_ref[slot, :, cols], counts_ref[slot], total)
+        return 0
+
+    lax.fori_loop(0, live, step, 0)
     grad_bf[...] = total[...].astype(BF)
     first = lax.axis_index("core") * half
     left_grad = jnp.zeros((half, width), F32)
@@ -189,17 +219,19 @@
     return jax.ShapeDtypeStruct(shape, F32)
 
 
-def call(kernel, name, outs, args, scratch=(), flops=0):
+def call(kernel, name, outs, args, scratch=(), flops=0, outside=()):
+    spaces = [pltpu.HBM if i in outside else pltpu.VMEM for i in range(len(args))]
+    sems = [pltpu.SemaphoreType.DMA((len(outside),))] if outside else []
     return pl.pallas_call(
         kernel,
         out_shape=outs,
-        in_specs=[pl.BlockSpec(memory_space=pltpu.VMEM)] * len(args),
+        in_specs=[pl.BlockSpec(memory_space=space) for space in spaces],
         out_specs=[pl.BlockSpec(memory_space=pltpu.VMEM)] * len(outs),
-        scratch_shapes=[pltpu.VMEM(shape, dtype) for shape, dtype in scratch],
+        scratch_shapes=[pltpu.VMEM(*one) if isinstance(one, tuple) else one for one in scratch] + sems,
         compiler_params=pltpu.CompilerParams(vmem_limit_bytes=30 << 20),
         cost_estimate=pl.CostEstimate(flops=flops, bytes_accessed=4 << 20, transcendentals=0),
         name=name,
-    )(*args)
+    )(*(pltpu.with_memory_space_constraint(a, pltpu.HBM) if i in outside else a for i, a in enumerate(args)))
 
 
 def buckets(index, left, left_accum, right, right_accum, relation, nbatch, move):
@@ -212,8 +244,10 @@
         "bucket0_left",
         (f32(rows // 2 + 8, width), jax.ShapeDtypeStruct((width, pairs), BF), pair_bf),
         (index, left, left_accum, right, relation),
-        [((rows, pairs), F32), ((rows, pairs), F32)],
+        [((rows, width), F32), ((1, rows), F32), ((rows, width), F32), (relation.shape, F32), ((rows, pairs), F32), ((rows, pairs), F32),
+         ((SLOTS, rows, pairs), F32), ((SLOTS, rows, 128), F32)],
         flops=2 << 30,
+        outside=(1, 2, 3, 4),
     )
     moved = move(left_half)
     right, right_accum, grad, edges, counts = call(
@@ -250,11 +284,15 @@
     nbatch, batch = edge_src.shape[3:]
     rows, width = left_emb.shape
     blocks = lax.axis_size(BLK)
-    index = jnp.stack([edge_src[0, 0], edge_dst[0, 0], edge_rel[0, 0], negatives[0, 0]], axis=2)
-    index = index.reshape(8 * nbatch, batch)
-    live = jnp.broadcast_to(batch_counts.reshape(2, 1), (2, batch))
-    pad = -(8 * nbatch + 2) % 8
-    index = jnp.concatenate([index, live, jnp.zeros((pad, batch), jnp.int32)], axis=0)
+    index_rows = -(-(8 * nbatch + 2) // 8) * 8
+    index = call(
+        functools.partial(gather_kernel, nbatch),
+        "gather_index",
+        (jax.ShapeDtypeStruct((index_rows, batch), jnp.int32),),
+        (edge_src, edge_dst, edge_rel, negatives, batch_counts),
+        [(edge_src.shape, jnp.int32)] * 4 + [pltpu.SMEM(batch_counts.shape, jnp.int32)],
+        outside=(0, 1, 2, 3, 4),
+    )[0]
     index = lax.all_gather(index, REP, axis=0, tiled=False)
     route = [(i, (i + 1) % blocks) for i in range(blocks)]
     left, left_accum, right, right_accum, grad = buckets(

time: 93.3 us -> 88.8 us (0.952)
  local copies, waits for them, and re-layouts: 4.51 us -> 0.06 us
  Pallas kernels: 10.8 us -> 14.6 us
  waiting for transfers between devices: 10 us -> 8.09 us
  blocking collectives: 64.1 us -> 63 us
    pallas_call x4 -> x5, Pallas kernels: 10.8 us -> 14.6 us  [call(): pl.pallas_call(kernel, out_shape=outs, in_specs=[pl.BlockSpec(memory_spac...]
    unnamed x14 -> x10, local copies, waits for them, and re-layouts: 3.63 us -> 0.02 us
    ppermute x1, waiting for transfers between devices: 10 us -> 8.09 us  [body(): lax.ppermute(half, BLK, route)]
    all_to_all x1, blocking collectives: 23.3 us -> 22.1 us  [body(): grad = jnp.sum(lax.all_to_all(grad, BLK, 0, 0, tiled=True), axis=0)]
  transfers between devices with their start and end apart: 1 -> 1, of which waited for: 1 -> 1; matrix products, arithmetic and copies ran while one was open for 0% -> 0% of each run, Pallas kernels for 2% -> 3%
where the time goes in v3:
time: 88.8 us; the launch traced here: 88.5 us
  blocking collectives  63 us (71%)
  Pallas kernels  14.6 us (16%)
  waiting for transfers between devices  8.09 us (9%)
  starting transfers between devices  1.92 us (2%)
    all_to_all x1, blocking collectives, body(): grad = jnp.sum(lax.all_to_all(grad, BLK, 0, 0, tiled=True), axis=0)  22.1 us
    all_to_all x1, blocking collectives, body(): grad = lax.all_to_all(grad, BLK, 0, 0, tiled=True)  19.8 us
    pallas_call x5, Pallas kernels, call(): pl.pallas_call(kernel, out_shape=outs, in_specs=[pl.BlockSpec(memory_spac...  14.6 us
    all_gather x1, blocking collectives, body(): index = lax.all_gather(index, REP, axis=0, tiled=False)  13.8 us
    ppermute x1, waiting for transfers between devices, body(): lax.ppermute(half, BLK, route)  8.09 us
    all_gather x1, blocking collectives, body(): grad = lax.all_gather(grad, 'core', axis=0, tiled=False)  4.94 us
    all_gather x1, blocking collectives, buckets(): moved = lax.all_gather(moved, 'core', axis=0, tiled=False)  2.36 us
    ppermute x1, starting transfers between devices, body(): lax.ppermute(half, BLK, route)  1.92 us
  transfers between devices with their start and end apart: 1, of which 1 were waited for; matrix products, arithmetic and copies ran while one was open for 0% of the time, Pallas kernels for 3%

profile of v3, /device:TPU:1, one launch (start us, length us, event | category | flops | bytes accessed | tf_op | source)
XLA Modules:
  0.0 88.5 jit_solution(11928712468361645539)
XLA Ops:
  0.6 0.9 gather_index.1
  1.5 13.8 %all-gather = s32[96,512]{1,0:T(8,128)S(1)} all-gather(s32[24,512]{1,0:T(8,128)S(1)} %gather_index.1), channel_id=2, replica_groups=mesh['z'=8,'y'=8,'xl'=2,'xh'=2,'core'=2] {'xh','core'}, dimensions={0}, use_global_device_ids=true | all-gather | bytes 245760 | tf_op jit(solution)/shard_map/all_gather | solution.py:296
  15.3 0.0 copy-start
  15.3 0.0 copy-start.2
  15.3 0.0 copy-start.3
  15.3 0.0 copy-start.4
  15.3 5.0 %bucket0_left.1 = (f32[136,256]{1,0:T(8,128)S(1)}, bf16[256,512]{1,0:T(8,128)(2,1)S(1)}, bf16[256,512]{1,0:T(8,128)(2,1)S(1)}) custom-call(s32[4,24,512]{2,1,0:T(8,128)S(1)} %bitcast.11, f32[256,256]{1,0:T(8,128)} %left_ref.1, f32[1,256]{1,0:T(1,128)} %bitcast.15, f32[256,256]{1,0:T(8,128)} %right_ref.1, f32[2,256,256]{2,1,0:T(8,128)} %relation_ref.1), custom_call_target="tpu_custom_call" | custom-call | flops 2147483648 | bytes 4194304 | tf_op jit(solution)/shard_map/bucket0_left/pallas_call | solution.py:225
  20.4 1.9 %collective-permute-start = (f32[136,256]{1,0:T(8,128)S(1)}, f32[136,256]{1,0:T(8,128)S(1)}, u32[]{:S(2)}, u32[]{:S(2)}) collective-permute-start(f32[136,256]{1,0:T(8,128)S(1)} %get-tuple-element.25), channel_id=1, source_target_pairs={{0,4},{4,8},{8,12},{12,16},{16,20},{20,24},{24,28},{28,32},{32,36}... | collective-permute-start | bytes 417800 | tf_op jit(solution)/shard_map/ppermute | solution.py:306
  22.3 0.0 copy-done
  22.3 0.0 copy-done.2
  22.3 0.0 copy-done.3
  22.3 0.0 copy-done.4
  22.3 2.9 %bucket0_right.1 = (f32[256,256]{1,0:T(8,128)S(1)}, f32[1,256]{1,0:T(1,128)S(1)}, f32[256,256]{1,0:T(8,128)S(1)}, f32[4,256,512]{2,1,0:T(8,128)S(1)}, f32[4,256,128]{2,1,0:T(8,128)S(1)}) custom-call(s32[4,24,512]{2,1,0:T(8,128)S(1)} %bitcast.12, f32[256,256]{1,0:T(8,128)S(1)} %copy-done.2, f32[256,256]{1,0:T(8,128)S(1)} %copy-done.3, f32[1,256]{1,0:T(1,128)S(1)} %bitcast.14, ...), custom_call_target="tpu_custom_call" | custom-call | flops 1073741824 | bytes 4194304 | tf_op jit(solution)/shard_map/bucket0_right/pallas_call | solution.py:225
  25.3 8.1 %collective-permute-done = f32[136,256]{1,0:T(8,128)S(1)} collective-permute-done((f32[136,256]{1,0:T(8,128)S(1)}, f32[136,256]{1,0:T(8,128)S(1)}, u32[]{:S(2)}, u32[]{:S(2)}) %collective-permute-start) | collective-permute-done | bytes 139296 | tf_op jit(solution)/shard_map/ppermute | solution.py:306
  33.4 2.4 %all-gather.1 = f32[272,256]{1,0:T(8,128)S(1)} all-gather(f32[136,256]{1,0:T(8,128)S(1)} %collective-permute-done), channel_id=3, replica_groups=mesh['z'=8,'y'=8,'xl'=2,'xh'=2,'core'=2] {'core'}, dimensions={0}, use_global_device_ids=true | all-gather | bytes 417792 | tf_op jit(solution)/shard_map/all_gather | solution.py:260
  35.8 4.5 %bucket1.1 = (f32[256,256]{1,0:T(8,128)}, f32[1,256]{1,0:T(1,128)}, f32[256,256]{1,0:T(8,128)}, f32[1,256]{1,0:T(1,128)}, f32[2,64,4,128]{3,2,1,0:T(4,128)S(1)}) custom-call(s32[4,24,512]{2,1,0:T(8,128)S(1)} %bitcast.13, f32[4,256,512]{2,1,0:T(8,128)S(1)} %get-tuple-element.23.edges_ref, f32[4,256,128]{2,1,0:T(8,128)S(1)} %get-tuple-element.24.counts_ref, ...), custom_call_target="tpu_custom_call" | custom-call | flops 2147483648 | bytes 4194304 | tf_op jit(solution)/shard_map/bucket1/pallas_call | solution.py:225
  40.3 0.0 copy-start.1
  40.3 22.1 %all_to_all.10 = f32[128,4,128]{2,1,0:T(4,128)S(1)} all-to-all(f32[128,4,128]{2,1,0:T(4,128)S(1)} %bitcast.10), channel_id=1, replica_groups=mesh['z'=8,'y'=8,'xl'=2,'xh'=2,'core'=2] {'z','y','xl'}, dimensions={0} | all-to-all | bytes 524288 | tf_op jit(solution)/shard_map/all_to_all | solution.py:309
  62.4 0.1 reduce_sum.9
  62.6 19.8 %all_to_all.11 = f32[128,4,128]{2,1,0:T(4,128)S(1)} all-to-all(f32[128,4,128]{2,1,0:T(4,128)S(1)} %broadcast_in_dim.2), channel_id=1, replica_groups=mesh['z'=8,'y'=8,'xl'=2,'xh'=2,'core'=2] {'z','y','xl'}, dimensions={0} | all-to-all | bytes 524288 | tf_op jit(solution)/shard_map/all_to_all | solution.py:311
  82.3 4.9 %all-gather.2 = f32[256,4,128]{2,1,0:T(4,128)S(1)} all-gather(f32[128,4,128]{2,1,0:T(4,128)S(1)} %all_to_all.11), channel_id=4, replica_groups=mesh['z'=8,'y'=8,'xl'=2,'xh'=2,'core'=2] {'core'}, dimensions={0}, use_global_device_ids=true | all-gather | bytes 786432 | tf_op jit(solution)/shard_map/all_gather | solution.py:312
  87.3 0.0 copy-done.1
  87.3 1.2 %final_update.1 = (f32[2,256,256]{2,1,0:T(8,128)}, f32[2,256,256]{2,1,0:T(8,128)}) custom-call(f32[2,2,64,4,128]{4,3,2,1,0:T(4,128)S(1)} %bitcast.8, f32[2,256,256]{2,1,0:T(8,128)S(1)} %copy-done, f32[2,256,256]{2,1,0:T(8,128)S(1)} %copy-done.1), custom_call_target="tpu_custom_call" | custom-call | bytes 4194304 | tf_op jit(solution)/shard_map/final_update/pallas_call | solution.py:225
  (1 shorter events, 0.0 us)
Async XLA Ops:
  15.3 7.0 %copy-start = (f32[2,256,256]{2,1,0:T(8,128)S(1)}, f32[2,256,256]{2,1,0:T(8,128)}, u32[]{:S(2)}) copy-start(f32[2,256,256]{2,1,0:T(8,128)} %relation_ref.1) | copy-start | bytes 1572868
  15.3 7.0 %copy-start.2 = (f32[256,256]{1,0:T(8,128)S(1)}, f32[256,256]{1,0:T(8,128)}, u32[]{:S(2)}) copy-start(f32[256,256]{1,0:T(8,128)} %left_ref.1) | copy-start | bytes 786436
  15.3 7.0 %copy-start.3 = (f32[256,256]{1,0:T(8,128)S(1)}, f32[256,256]{1,0:T(8,128)}, u32[]{:S(2)}) copy-start(f32[256,256]{1,0:T(8,128)} %right_ref.1) | copy-start | bytes 786436
  15.3 7.0 %copy-start.4 = (f32[256]{0:T(256)S(1)}, f32[256]{0:T(256)}, u32[]{:S(2)}) copy-start(f32[256]{0:T(256)} %param.14) | copy-start | bytes 3076
  20.4 13.0 %collective-permute-start = (f32[136,256]{1,0:T(8,128)S(1)}, f32[136,256]{1,0:T(8,128)S(1)}, u32[]{:S(2)}, u32[]{:S(2)}) collective-permute-start(f32[136,256]{1,0:T(8,128)S(1)} %get-tuple-element.25), channel_id=1, source_target_pairs={{0,4},{4,8},{8,12},{12,16},{16,20},{20,24},{24,28},{28,32},{32,36}... | collective-permute-start | bytes 417800 | tf_op jit(solution)/shard_map/ppermute | solution.py:306
  40.3 47.0 %copy-start.1 = (f32[2,256,256]{2,1,0:T(8,128)S(1)}, f32[2,256,256]{2,1,0:T(8,128)}, u32[]{:S(2)}) copy-start(f32[2,256,256]{2,1,0:T(8,128)} %state_ref.1) | copy-start | bytes 1572868

commit v4 on v3

--- a/solution.py
+++ b/solution.py
@@ -12,6 +12,7 @@
 F32 = jnp.float32
 BLK = ("z", "y", "xl")
 REP = ("xh", "core")
+NREL = 2
 SLOTS = 4
 
 
@@ -42,27 +43,34 @@
     return embedding - learn_rate * gradient / jnp.sqrt(accum), accum
 
 
-def count_batch(idx_ref, member, base, rows, pairs):
-    source = idx_ref[member, pl.ds(base, 1), :]
+def count_batch(idx_ref, member, base, rows, half, first):
+    source = idx_ref[member, pl.ds(base, 1), :] - first
     target = idx_ref[member, pl.ds(base + 1, 1), :]
     relation = idx_ref[member, pl.ds(base + 2, 1), :]
     negative = idx_ref[member, pl.ds(base + 3, 1), :]
-    edges = dot(one_hot(target, rows), one_hot(relation * rows + source, pairs), (1, 1))
+    pair = jnp.where((source >= 0) & (source < half), relation * half + source, -1)
+    edges = dot(one_hot(target, rows), one_hot(pair, NREL * half), (1, 1))
     counts = dot(one_hot(negative, rows), jnp.ones((negative.shape[1], 128), BF), (1, 0))
     return edges, counts
 
 
 def each_live_batch(idx_ref, bucket, nbatch, step):
-    def member_step(member, slot):
-        live = jnp.max(idx_ref[member, pl.ds(8 * nbatch + bucket, 1), :])
-
-        def batch_step(batch, slot):
-            step(member, (bucket * nbatch + batch) * 4, slot)
-            return slot + 1
-
-        return lax.fori_loop(0, live, batch_step, slot)
-
-    return lax.fori_loop(0, idx_ref.shape[0], member_step, 0)
+    members = idx_ref.shape[0]
+    row = 8 * nbatch + bucket
+    ends = [jnp.max(idx_ref[member, row : row + 1, :]) for member in range(members)]
+    for member in range(1, members):
+        ends[member] = ends[member] + ends[member - 1]
+
+    def slot_step(slot, _):
+        member, begin = jnp.int32(0), jnp.int32(0)
+        for end in ends[:-1]:
+            member = member + jnp.where(slot >= end, 1, 0)
+            begin = jnp.where(slot >= end, end, begin)
+        step(member, (bucket * nbatch + slot - begin) * 4, slot)
+        return 0
+
+    lax.fori_loop(0, ends[-1], slot_step, 0)
+    return ends[-1]
 
 
 def score_grad(scores_t, edges_of, counts, total):
@@ -82,12 +90,28 @@
 
 
 def queries_and_scores(left_bf, right_bf, op_ref, query_t, scores_t):
-    rows = left_bf.shape[0]
-    for r in range(op_ref.shape[0]):
-        cols = slice(r * rows, (r + 1) * rows)
-        query = dot(op_ref[r].astype(BF), left_bf, (1, 1)).astype(BF)
-        query_t[:, cols] = query
-        scores_t[:, cols] = dot(right_bf, query, (1, 0))
+    half = left_bf.shape[0]
+    for r in range(NREL):
+        cols = slice(r * half, (r + 1) * half)
+        query_t[:, cols] = dot(op_ref[r].astype(BF), left_bf, (1, 1)).astype(BF)
+    scores_t[...] = dot(right_bf, query_t[...], (1, 0))
+
+
+def table_products(table_t, op_ref):
+    half = table_t.shape[1] // NREL
+    return sum(dot(table_t[:, r * half : (r + 1) * half], op_ref[r].astype(BF), (0, 0)) for r in range(NREL))
+
+
+def operator_products(table_t, left_bf, r):
+    half = left_bf.shape[0]
+    return dot(table_t[:, r * half : (r + 1) * half], left_bf, (1, 0))
+
+
+def pack_rows(out_ref, embedding, accum):
+    half, width = embedding.shape
+    out_ref[0:half, :] = embedding
+    row = jnp.concatenate([to_row(accum)] * (width // half), axis=1)
+    out_ref[half : half + 8, :] = jnp.broadcast_to(row, (8, width))
 
 
 def gather_kernel(nbatch, *refs):
@@ -109,17 +133,25 @@
                 out_ref[row : row + 1, :] = buffer[0, 0, bucket, batch : batch + 1, :]
 
 
-def first_kernel(nbatch, idx_ref, left_hbm, accum_hbm, right_hbm, op_hbm, left_out, query_t, grad_bf, left_ref, accum_ref, right_ref, op_ref, scores_t, total, edges_ref, counts_ref, sems):
-    pairs = ((op_hbm, op_ref), (left_hbm, left_ref), (right_hbm, right_ref), (accum_hbm, accum_ref))
+def first_kernel(
+    nbatch, idx_ref, left_hbm, accum_hbm, right_hbm, op_hbm, left_out, query_t, grad_bf, table_t,
+    left_ref, accum_ref, right_ref, op_ref, scores_t, total, edges_ref, counts_ref, sems
+):
+    rows, width = right_ref.shape
+    half = left_ref.shape[0]
+    first = pl.multiple_of(lax.axis_index("core") * half, half)
+    pairs = (
+        (op_hbm, op_ref),
+        (left_hbm.at[pl.ds(first, half), :], left_ref),
+        (right_hbm, right_ref),
+        (accum_hbm, accum_ref),
+    )
     copies = [pltpu.make_async_copy(*pair, sems.at[i]) for i, pair in enumerate(pairs)]
     for copy in copies:
         copy.start()
-    nrel = op_ref.shape[0]
-    rows, width = left_ref.shape
-    half = rows // 2
 
     def count(member, base, slot):
-        edges_ref[slot], counts_ref[slot] = count_batch(idx_ref, member, base, rows, nrel * rows)
+        edges_ref[slot], counts_ref[slot] = count_batch(idx_ref, member, base, rows, half, first)
 
     live = each_live_batch(idx_ref, 0, nbatch, count)
     for copy in copies:
@@ -134,49 +166,40 @@
 
     lax.fori_loop(0, live, step, 0)
     grad_bf[...] = total[...].astype(BF)
-    first = lax.axis_index("core") * half
-    left_grad = jnp.zeros((half, width), F32)
-    for r in range(nrel):
-        cols = pl.ds(pl.multiple_of(r * rows + first, half), half)
-        table_t = dot(right_bf, grad_bf[:, cols], (0, 0)).astype(BF)
-        left_grad += dot(table_t, op_ref[r].astype(BF), (0, 0))
-    mine = pl.ds(pl.multiple_of(first, half), half)
-    accum = to_column(accum_ref[:, mine])
-    left_out[0:half, :], accum = row_update(left_ref[mine, :], accum, left_grad)
-    accum = jnp.concatenate([to_row(accum)] * (width // half), axis=1)
-    left_out[half : half + 8, :] = jnp.broadcast_to(accum, (8, width))
-
-
-def between_kernel(
-    nbatch, idx_ref, left_ref, right_ref, accum_ref, query_t, grad_bf, op_ref, right_out, accum_out, grad_out, edges_out, counts_out
+    table_t[...] = dot(right_bf, grad_bf[...], (0, 0)).astype(BF)
+    left_grad = table_products(table_t, op_ref)
+    accum = to_column(accum_ref[:, pl.ds(first, half)])
+    pack_rows(left_out, *row_update(left_ref[...], accum, left_grad))
+
+
+def between_kernel(nbatch, idx_ref, left_ref, query_t, grad_bf, table_t, right_grad_out, grad_out, edges_out, counts_out):
+    rows = query_t.shape[0]
+    half = query_t.shape[1] // NREL
+    first = pl.multiple_of(lax.axis_index("core") * half, half)
+    right_grad_out[...] = dot(grad_bf[...], query_t[...], (1, 1))
+    left_bf = left_ref[pl.ds(first, half), :].astype(BF)
+    for r in range(NREL):
+        grad_out[r] = operator_products(table_t, left_bf, r)
+
+    def count(member, base, slot):
+        edges_out[slot], counts_out[slot] = count_batch(idx_ref, member, base, rows, half, first)
+
+    each_live_batch(idx_ref, 1, nbatch, count)
+
+
+def right_kernel(grads_ref, right_ref, accum_ref, right_out, accum_out):
+    grad = grads_ref[0] + grads_ref[1]
+    right_out[...], accum = row_update(right_ref[...], to_column(accum_ref[...]), grad)
+    accum_out[...] = to_row(accum)
+
+
+def second_kernel(
+    nbatch, idx_ref, edges_ref, counts_ref, left_ref, right_ref, op_ref, grad_ref,
+    grad_out, query_t, grad_bf, table_t, scores_t, total
 ):
-    rows = right_ref.shape[0]
-    pairs = query_t.shape[1]
-
-    def step(member, base, slot):
-        edges_out[slot], counts_out[slot] = count_batch(idx_ref, member, base, rows, pairs)
-
-    each_live_batch(idx_ref, 1, nbatch, step)
-    right = right_ref[...]
-    right_grad = dot(grad_bf[...], query_t[...], (1, 1))
-    cols = pl.ds(pl.multiple_of(lax.axis_index("core") * rows, rows), rows)
-    table_t = dot(right.astype(BF), grad_bf[:, cols], (0, 0)).astype(BF)
-    grad_out[...] = dot(table_t, left_ref[...].astype(BF), (1, 0))
-    right_out[...], accum = row_update(right, to_column(accum_ref[...]), right_grad)
-    accum_out[...] = to_row(accum)
-
-
-def second_kernel(
-    nbatch, idx_ref, edges_ref, counts_ref, left_ref, right_ref, accum_ref, op_ref, grad_ref,
-    left_out, left_accum_out, right_out, right_accum_out, grad_out, query_t, scores_t, total, grad_bf, table_t
-):
-    nrel = op_ref.shape[0]
-    rows, width = right_ref.shape
-    half = rows // 2
-    left = jnp.concatenate([left_ref[0, 0:half, :], left_ref[1, 0:half, :]], axis=0)
-    left_accum = jnp.concatenate([left_ref[0, half : half + 1, 0:half], left_ref[1, half : half + 1, 0:half]], axis=1)
-    right = right_ref[...]
-    left_bf, right_bf = left.astype(BF), right.astype(BF)
+    half = query_t.shape[1] // NREL
+    left_bf = left_ref[0:half, :].astype(BF)
+    right_bf = right_ref[...].astype(BF)
     queries_and_scores(left_bf, right_bf, op_ref, query_t, scores_t)
     total[...] = jnp.zeros_like(total)
     live = 0
@@ -190,17 +213,27 @@
     lax.fori_loop(0, jnp.max(live), step, 0)
     grad_bf[...] = total[...].astype(BF)
     table_t[...] = dot(right_bf, grad_bf[...], (0, 0)).astype(BF)
-    mine = pl.ds(pl.multiple_of(lax.axis_index("core") * rows, rows), rows)
-    grad = dot(table_t[:, mine], left_bf, (1, 0)) + grad_ref[...]
+    for r in range(NREL):
+        grad = operator_products(table_t, left_bf, r) + grad_ref[r]
+        for part in range(2):
+            grad_out[r, part] = grad[:, part * 128 : (part + 1) * 128].reshape(grad_out.shape[2:])
+
+
+def last_rows_kernel(left_ref, op_ref, query_t, grad_bf, table_t, out_ref):
+    half = left_ref.shape[0] - 8
+    accum = to_column(left_ref[half : half + 1, 0:half])
+    pack_rows(out_ref, *row_update(left_ref[0:half, :], accum, table_products(table_t, op_ref)))
+    out_ref[half + 8 :, :] = dot(grad_bf[...], query_t[...], (1, 1))
+
+
+def rows_kernel(parts_ref, right_ref, accum_ref, left_out, left_accum_out, right_out, right_accum_out):
+    half = left_out.shape[0] // 2
     for part in range(2):
-        grad_out[part] = grad[:, part * 128 : (part + 1) * 128].reshape(grad_out.shape[1:])
-    left_grad = jnp.zeros((rows, width), F32)
-    for r in range(nrel):
-        left_grad += dot(table_t[:, r * rows : (r + 1) * rows], op_ref[r].astype(BF), (0, 0))
-    left_out[...], accum = row_update(left, to_column(left_accum), left_grad)
-    left_accum_out[...] = to_row(accum)
-    right_grad = dot(grad_bf[...], query_t[...], (1, 1))
-    right_out[...], accum = row_update(right, to_column(accum_ref[...]), right_grad)
+        mine = slice(part * half, (part + 1) * half)
+        left_out[mine, :] = parts_ref[part, 0:half, :]
+        left_accum_out[:, mine] = parts_ref[part, half : half + 1, 0:half]
+    grad = parts_ref[0, half + 8 :, :] + parts_ref[1, half + 8 :, :]
+    right_out[...], accum = row_update(right_ref[...], to_column(accum_ref[...]), grad)
     right_accum_out[...] = to_row(accum)
 
 
@@ -235,37 +268,57 @@
 
 
 def buckets(index, left, left_accum, right, right_accum, relation, nbatch, move):
-    nrel, width, _ = relation.shape
+    width = relation.shape[-1]
     rows = left.shape[0]
-    pairs = nrel * rows
-    pair_bf = jax.ShapeDtypeStruct((rows, pairs), BF)
-    left_half, query_t, grad_bf = call(
+    half = rows // 2
+    pairs = NREL * half
+    bf16 = lambda *shape: jax.ShapeDtypeStruct(shape, BF)
+    moved, query_t, grad_bf, table_t = call(
         functools.partial(first_kernel, nbatch),
         "bucket0_left",
-        (f32(rows // 2 + 8, width), jax.ShapeDtypeStruct((width, pairs), BF), pair_bf),
+        (f32(half + 8, width), bf16(width, pairs), bf16(rows, pairs), bf16(width, pairs)),
         (index, left, left_accum, right, relation),
-        [((rows, width), F32), ((1, rows), F32), ((rows, width), F32), (relation.shape, F32), ((rows, pairs), F32), ((rows, pairs), F32),
-         ((SLOTS, rows, pairs), F32), ((SLOTS, rows, 128), F32)],
+        [((half, width), F32), ((1, rows), F32), ((rows, width), F32), (relation.shape, F32), ((rows, pairs), F32),
+         ((rows, pairs), F32), ((SLOTS, rows, pairs), F32), ((SLOTS, rows, 128), F32)],
         flops=2 << 30,
         outside=(1, 2, 3, 4),
     )
-    moved = move(left_half)
-    right, right_accum, grad, edges, counts = call(
+    moved = move(moved)
+    right_grad, grad, edges, counts = call(
         functools.partial(between_kernel, nbatch),
-        "bucket0_right",
-        (f32(rows, width), f32(1, rows), f32(width, width), f32(SLOTS, rows, pairs), f32(SLOTS, rows, 128)),
-        (index, left, right, right_accum, query_t, grad_bf, relation),
+        "bucket0_rest",
+        (f32(rows, width), f32(NREL, width, width), f32(SLOTS, rows, pairs), f32(SLOTS, rows, 128)),
+        (index, left, query_t, grad_bf, table_t),
         flops=1 << 30,
     )
-    moved = lax.all_gather(moved, "core", axis=0, tiled=False)
-    return call(
+    right_grad = lax.all_gather(right_grad, "core", axis=0, tiled=False)
+    right, right_accum = call(
+        right_kernel, "bucket0_right", (f32(rows, width), f32(1, rows)), (right_grad, right, right_accum), flops=1 << 28
+    )
+    grad, query_t, grad_bf, table_t = call(
         functools.partial(second_kernel, nbatch),
         "bucket1",
-        (f32(rows, width), f32(1, rows), f32(rows, width), f32(1, rows), f32(2, width // 4, 4, 128)),
-        (index, edges, counts, moved, right, right_accum, relation, grad),
-        [((width, pairs), BF), ((rows, pairs), F32), ((rows, pairs), F32), ((rows, pairs), BF), ((width, pairs), BF)],
+        (f32(NREL, 2, width // 8, 8, 128), bf16(width, pairs), bf16(rows, pairs), bf16(width, pairs)),
+        (index, edges, counts, moved, right, relation, grad),
+        [((rows, pairs), F32), ((rows, pairs), F32)],
         flops=2 << 30,
     )
+    parts = call(
+        last_rows_kernel,
+        "bucket1_rows",
+        (f32(half + 8 + rows, width),),
+        (moved, relation, query_t, grad_bf, table_t),
+        flops=1 << 30,
+    )[0]
+    parts = lax.all_gather(parts, "core", axis=0, tiled=False)
+    updated = call(
+        rows_kernel,
+        "bucket1_right",
+        (f32(rows, width), f32(1, rows), f32(rows, width), f32(1, rows)),
+        (parts, right, right_accum),
+        flops=1 << 28,
+    )
+    return (*updated, grad)
 
 
 def body(
@@ -307,10 +360,10 @@
     )
     grad = grad.reshape(blocks, -1, 128)
     grad = jnp.sum(lax.all_to_all(grad, BLK, 0, 0, tiled=True), axis=0)
+    grad = jnp.sum(lax.all_gather(grad, "core", axis=0, tiled=False), axis=0)
     grad = jnp.broadcast_to(grad[None], (blocks, *grad.shape))
     grad = lax.all_to_all(grad, BLK, 0, 0, tiled=True)
-    grad = lax.all_gather(grad, "core", axis=0, tiled=False)
-    grad = grad.reshape(relation.shape[0], 2, width // 4, 4, 128)
+    grad = grad.reshape(NREL, 2, width // 8, 8, 128)
     relation_new, relation_state_new = call(
         final_kernel, "final_update", (f32(*relation.shape),) * 2, (grad, relation, relation_state)
     )

time: 88.8 us -> 92 us (1.036)
  the two profiles are of different devices: /device:TPU:1 before, /device:TPU:6 now
where the time goes in v4:
time: 92 us; the launch traced here: 91.6 us
  blocking collectives  52.7 us (57%)
  waiting for transfers between devices  19.8 us (22%)
  starting transfers between devices  9.16 us (10%)
  Pallas kernels  8.29 us (9%)
    all_to_all x1, blocking collectives, body(): grad = jnp.sum(lax.all_to_all(grad, BLK, 0, 0, tiled=True), axis=0)  39.1 us
    all_to_all x1, waiting for transfers between devices, body(): grad = lax.all_to_all(grad, BLK, 0, 0, tiled=True)  16.5 us
    pallas_call x8, Pallas kernels, call(): pl.pallas_call(kernel, out_shape=outs, in_specs=[pl.BlockSpec(memory_spac...  8.29 us
    all_gather x1, blocking collectives, body(): index = lax.all_gather(index, REP, axis=0, tiled=False)  7.11 us
    all_to_all x1, starting transfers between devices, body(): grad = lax.all_to_all(grad, BLK, 0, 0, tiled=True)  6.33 us
    ppermute x1, waiting for transfers between devices, body(): lax.ppermute(half, BLK, route)  3.3 us
    ppermute x1, starting transfers between devices, body(): lax.ppermute(half, BLK, route)  2.83 us
    all_gather x1, blocking collectives, buckets(): parts = lax.all_gather(parts, 'core', axis=0, tiled=False)  2.38 us
  transfers between devices with their start and end apart: 2, of which 2 were waited for; matrix products, arithmetic and copies ran while one was open for 0% of the time, Pallas kernels for 2%

profile of v4, /device:TPU:6, one launch (start us, length us, event | category | flops | bytes accessed | tf_op | source)
XLA Modules:
  0.0 91.6 jit_solution(14171999919227580525)
XLA Ops:
  0.6 0.9 gather_index.1
  1.5 7.1 %all-gather = s32[96,512]{1,0:T(8,128)S(1)} all-gather(s32[24,512]{1,0:T(8,128)S(1)} %gather_index.1), channel_id=2, replica_groups=mesh['z'=8,'y'=8,'xl'=2,'xh'=2,'core'=2] {'xh','core'}, dimensions={0}, use_global_device_ids=true | all-gather | bytes 245760 | tf_op jit(solution)/shard_map/all_gather | solution.py:349
  8.6 0.0 copy-start.2
  8.6 3.8 %bucket0_left.1 = (f32[136,256]{1,0:T(8,128)S(1)}, bf16[256,256]{1,0:T(8,128)(2,1)S(1)}, bf16[256,256]{1,0:T(8,128)(2,1)S(1)}, bf16[256,256]{1,0:T(8,128)(2,1)S(1)}) custom-call(s32[4,24,512]{2,1,0:T(8,128)S(1)} %bitcast.15, f32[256,256]{1,0:T(8,128)} %left_ref.1, f32[1,256]{1,0:T(1,128)} %bitcast.19, f32[256,256]{1,0:T(8,128)} %right_ref.1, ...), custom_call_target="tpu_custom_call" | custom-call | flops 2147483648 | bytes 4194304 | tf_op jit(solution)/shard_map/bucket0_left/pallas_call | solution.py:258
  12.4 2.8 %collective-permute-start = (f32[136,256]{1,0:T(8,128)S(1)}, f32[136,256]{1,0:T(8,128)S(1)}, u32[]{:S(2)}, u32[]{:S(2)}) collective-permute-start(f32[136,256]{1,0:T(8,128)S(1)} %get-tuple-element.26), channel_id=1, source_target_pairs={{0,4},{4,8},{8,12},{12,16},{16,20},{20,24},{24,28},{28,32},{32,36}... | collective-permute-start | bytes 417800 | tf_op jit(solution)/shard_map/ppermute | solution.py:359
  15.2 0.0 copy-done.2
  15.2 0.3 bucket0_rest.1
  15.5 0.0 copy-start.3
  15.5 0.0 copy-start.4
  15.5 2.3 %all-gather.1 = f32[512,256]{1,0:T(8,128)S(1)} all-gather(f32[256,256]{1,0:T(8,128)S(1)} %get-tuple-element.32), channel_id=3, replica_groups=mesh['z'=8,'y'=8,'xl'=2,'xh'=2,'core'=2] {'core'}, dimensions={0}, use_global_device_ids=true | all-gather | bytes 786432 | tf_op jit(solution)/shard_map/all_gather | solution.py:294
  17.9 0.0 copy-start
  17.9 0.0 copy-done.3
  17.9 0.0 copy-done.4
  17.9 0.2 bucket0_right.1
  18.0 3.3 %collective-permute-done.left_ref = f32[136,256]{1,0:T(8,128)S(1)} collective-permute-done((f32[136,256]{1,0:T(8,128)S(1)}, f32[136,256]{1,0:T(8,128)S(1)}, u32[]{:S(2)}, u32[]{:S(2)}) %collective-permute-start) | collective-permute-done | bytes 139296 | tf_op jit(solution)/shard_map/ppermute | solution.py:359
  21.3 0.0 copy-done
  21.3 0.8 bucket1.1
  22.2 39.1 %all_to_all.10 = f32[128,8,128]{2,1,0:T(8,128)S(1)} all-to-all(f32[128,8,128]{2,1,0:T(8,128)S(1)} %bitcast.14), channel_id=1, replica_groups=mesh['z'=8,'y'=8,'xl'=2,'xh'=2,'core'=2] {'z','y','xl'}, dimensions={0} | all-to-all | bytes 1048576 | tf_op jit(solution)/shard_map/all_to_all | solution.py:362
  61.2 0.1 reduce_sum.18
  61.4 1.8 %all-gather.3 = f32[16,128]{1,0:T(8,128)S(1)} all-gather(f32[8,128]{1,0:T(8,128)S(1)} %reduce_sum.18), channel_id=5, replica_groups=mesh['z'=8,'y'=8,'xl'=2,'xh'=2,'core'=2] {'core'}, dimensions={0}, use_global_device_ids=true | all-gather | bytes 12288 | tf_op jit(solution)/shard_map/all_gather | solution.py:363
  63.2 0.8 broadcast_in_dim.2
  64.0 6.3 %all-to-all-start.1 = ((f32[128,8,128]{2,1,0:T(8,128)}), f32[128,8,128]{2,1,0:T(8,128)S(1)}, u32[]{:S(2)}, u32[]{:S(2)}) async-start(f32[128,8,128]{2,1,0:T(8,128)} %broadcast_in_dim.2), calls=%async_computation.1 | async-start | bytes 1048576 | tf_op jit(solution)/shard_map/all_to_all | solution.py:365
  70.3 0.3 bucket1_rows.1
  70.7 2.4 %all-gather.2 = f32[784,256]{1,0:T(8,128)S(1)} all-gather(f32[392,256]{1,0:T(8,128)S(1)} %bucket1_rows.1), channel_id=4, replica_groups=mesh['z'=8,'y'=8,'xl'=2,'xh'=2,'core'=2] {'core'}, dimensions={0}, use_global_device_ids=true | all-gather | bytes 1204224 | tf_op jit(solution)/shard_map/all_gather | solution.py:313
  73.1 0.0 copy-start.1
  73.1 0.9 bucket1_right.1
  74.0 16.5 %all-to-all-done.1 = f32[128,8,128]{2,1,0:T(8,128)S(1)} async-done(((f32[128,8,128]{2,1,0:T(8,128)}), f32[128,8,128]{2,1,0:T(8,128)S(1)}, u32[]{:S(2)}, u32[]{:S(2)}) %all-to-all-start.1) | async-done | bytes 524320 | tf_op jit(solution)/shard_map/all_to_all | solution.py:365
  90.4 0.0 copy-done.1
  90.4 1.1 %final_update.1 = (f32[2,256,256]{2,1,0:T(8,128)}, f32[2,256,256]{2,1,0:T(8,128)}) custom-call(f32[2,2,32,8,128]{4,3,2,1,0:T(8,128)S(1)} %bitcast.12, f32[2,256,256]{2,1,0:T(8,128)S(1)} %copy-done, f32[2,256,256]{2,1,0:T(8,128)S(1)} %copy-done.1), custom_call_target="tpu_custom_call" | custom-call | bytes 4194304 | tf_op jit(solution)/shard_map/final_update/pallas_call | solution.py:258
  (1 shorter events, 0.0 us)
Async XLA Ops:
  8.6 6.6 %copy-start.2 = (f32[256,256]{1,0:T(8,128)S(1)}, f32[256,256]{1,0:T(8,128)}, u32[]{:S(2)}) copy-start(f32[256,256]{1,0:T(8,128)} %left_ref.1) | copy-start | bytes 786436
  12.4 9.0 %collective-permute-start = (f32[136,256]{1,0:T(8,128)S(1)}, f32[136,256]{1,0:T(8,128)S(1)}, u32[]{:S(2)}, u32[]{:S(2)}) collective-permute-start(f32[136,256]{1,0:T(8,128)S(1)} %get-tuple-element.26), channel_id=1, source_target_pairs={{0,4},{4,8},{8,12},{12,16},{16,20},{20,24},{24,28},{28,32},{32,36}... | collective-permute-start | bytes 417800 | tf_op jit(solution)/shard_map/ppermute | solution.py:359
  15.5 2.3 %copy-start.3 = (f32[256,256]{1,0:T(8,128)S(1)}, f32[256,256]{1,0:T(8,128)}, u32[]{:S(2)}) copy-start(f32[256,256]{1,0:T(8,128)} %right_ref.1) | copy-start | bytes 786436
  15.5 2.3 %copy-start.4 = (f32[256]{0:T(256)S(1)}, f32[256]{0:T(256)}, u32[]{:S(2)}) copy-start(f32[256]{0:T(256)} %param.14) | copy-start | bytes 3076
  17.9 3.5 %copy-start = (f32[2,256,256]{2,1,0:T(8,128)S(1)}, f32[2,256,256]{2,1,0:T(8,128)}, u32[]{:S(2)}) copy-start(f32[2,256,256]{2,1,0:T(8,128)} %relation_ref.1) | copy-start | bytes 1572868
  64.0 26.4 %all-to-all-start.1 = ((f32[128,8,128]{2,1,0:T(8,128)}), f32[128,8,128]{2,1,0:T(8,128)S(1)}, u32[]{:S(2)}, u32[]{:S(2)}) async-start(f32[128,8,128]{2,1,0:T(8,128)} %broadcast_in_dim.2), calls=%async_computation.1 | async-start | bytes 1048576 | tf_op jit(solution)/shard_map/all_to_all | solution.py:365
  73.1 17.4 %copy-start.1 = (f32[2,256,256]{2,1,0:T(8,128)S(1)}, f32[2,256,256]{2,1,0:T(8,128)}, u32[]{:S(2)}) copy-start(f32[2,256,256]{2,1,0:T(8,128)} %state_ref.1) | copy-start | bytes 1572868

commit v5 on v3

--- a/solution.py
+++ b/solution.py
@@ -12,6 +12,7 @@
 F32 = jnp.float32
 BLK = ("z", "y", "xl")
 REP = ("xh", "core")
+NREL = 2
 SLOTS = 4
 
 
@@ -42,27 +43,30 @@
     return embedding - learn_rate * gradient / jnp.sqrt(accum), accum
 
 
-def count_batch(idx_ref, member, base, rows, pairs):
-    source = idx_ref[member, pl.ds(base, 1), :]
+def count_batch(idx_ref, member, base, rows, first, half):
+    source = idx_ref[member, pl.ds(base, 1), :] - first
     target = idx_ref[member, pl.ds(base + 1, 1), :]
     relation = idx_ref[member, pl.ds(base + 2, 1), :]
     negative = idx_ref[member, pl.ds(base + 3, 1), :]
-    edges = dot(one_hot(target, rows), one_hot(relation * rows + source, pairs), (1, 1))
+    pair = jnp.where((source >= 0) & (source < half), relation * half + source, -1)
+    edges = dot(one_hot(target, rows), one_hot(pair, NREL * half), (1, 1))
     counts = dot(one_hot(negative, rows), jnp.ones((negative.shape[1], 128), BF), (1, 0))
     return edges, counts
 
 
-def each_live_batch(idx_ref, bucket, nbatch, step):
-    def member_step(member, slot):
-        live = jnp.max(idx_ref[member, pl.ds(8 * nbatch + bucket, 1), :])
-
-        def batch_step(batch, slot):
-            step(member, (bucket * nbatch + batch) * 4, slot)
-            return slot + 1
-
-        return lax.fori_loop(0, live, batch_step, slot)
-
-    return lax.fori_loop(0, idx_ref.shape[0], member_step, 0)
+def live_slots(idx_ref, bucket, nbatch):
+    row = 8 * nbatch + bucket
+    ends = [jnp.max(idx_ref[member, row : row + 1, :]) for member in range(idx_ref.shape[0])]
+    for member in range(1, len(ends)):
+        ends[member] = ends[member] + ends[member - 1]
+    slots = []
+    for slot in range(SLOTS):
+        member, begin = jnp.int32(0), jnp.int32(0)
+        for end in ends[:-1]:
+            member = member + jnp.where(slot >= end, 1, 0)
+            begin = jnp.where(slot >= end, end, begin)
+        slots.append((member, (bucket * nbatch + jnp.minimum(slot - begin, nbatch - 1)) * 4))
+    return ends[-1], slots
 
 
 def score_grad(scores_t, edges_of, counts, total):
@@ -82,12 +86,28 @@
 
 
 def queries_and_scores(left_bf, right_bf, op_ref, query_t, scores_t):
-    rows = left_bf.shape[0]
-    for r in range(op_ref.shape[0]):
-        cols = slice(r * rows, (r + 1) * rows)
-        query = dot(op_ref[r].astype(BF), left_bf, (1, 1)).astype(BF)
-        query_t[:, cols] = query
-        scores_t[:, cols] = dot(right_bf, query, (1, 0))
+    half = left_bf.shape[0]
+    for r in range(NREL):
+        cols = slice(r * half, (r + 1) * half)
+        query_t[:, cols] = dot(op_ref[r].astype(BF), left_bf, (1, 1)).astype(BF)
+    scores_t[...] = dot(right_bf, query_t[...], (1, 0))
+
+
+def table_products(table_t, op_ref):
+    half = table_t.shape[1] // NREL
+    return sum(dot(table_t[:, r * half : (r + 1) * half], op_ref[r].astype(BF), (0, 0)) for r in range(NREL))
+
+
+def operator_products(table_t, left_bf, r):
+    half = left_bf.shape[0]
+    return dot(table_t[:, r * half : (r + 1) * half], left_bf, (1, 0))
+
+
+def pack_rows(out_ref, embedding, accum):
+    half, width = embedding.shape
+    out_ref[0:half, :] = embedding
+    row = jnp.concatenate([to_row(accum)] * (width // half), axis=1)
+    out_ref[half : half + 8, :] = jnp.broadcast_to(row, (8, width))
 
 
 def gather_kernel(nbatch, *refs):
@@ -109,61 +129,75 @@
                 out_ref[row : row + 1, :] = buffer[0, 0, bucket, batch : batch + 1, :]
 
 
-def first_kernel(nbatch, idx_ref, left_hbm, accum_hbm, right_hbm, op_hbm, left_out, query_t, grad_bf, left_ref, accum_ref, right_ref, op_ref, scores_t, total, edges_ref, counts_ref, sems):
-    pairs = ((op_hbm, op_ref), (left_hbm, left_ref), (right_hbm, right_ref), (accum_hbm, accum_ref))
+def score_grads(live, scores_t, edges_ref, counts_ref, total):
+    total[...] = jnp.zeros_like(total)
+
+    def step(slot, _):
+        score_grad(scores_t, lambda cols: edges_ref[slot, :, cols], counts_ref[slot], total)
+        return 0
+
+    lax.fori_loop(0, live, step, 0)
+
+
+def first_kernel(
+    nbatch, idx_ref, left_hbm, accum_hbm, right_hbm, op_hbm, left_out, query_t, grad_bf, table_t,
+    left_ref, accum_ref, right_ref, op_ref, scores_t, total, edges_ref, counts_ref, sems
+):
+    rows, width = right_ref.shape
+    half = left_ref.shape[0]
+    first = pl.multiple_of(lax.axis_index("core") * half, half)
+    pairs = (
+        (op_hbm, op_ref),
+        (left_hbm.at[pl.ds(first, half), :], left_ref),
+        (right_hbm, right_ref),
+        (accum_hbm, accum_ref),
+    )
     copies = [pltpu.make_async_copy(*pair, sems.at[i]) for i, pair in enumerate(pairs)]
     for copy in copies:
         copy.start()
-    nrel = op_ref.shape[0]
-    rows, width = left_ref.shape
-    half = rows // 2
-
-    def count(member, base, slot):
-        edges_ref[slot], counts_ref[slot] = count_batch(idx_ref, member, base, rows, nrel * rows)
-
-    live = each_live_batch(idx_ref, 0, nbatch, count)
+    live, slots = live_slots(idx_ref, 0, nbatch)
+    for slot, (member, base) in enumerate(slots):
+        edges_ref[slot], counts_ref[slot] = count_batch(idx_ref, member, base, rows, first, half)
     for copy in copies:
         copy.wait()
     right_bf = right_ref[...].astype(BF)
     queries_and_scores(left_ref[...].astype(BF), right_bf, op_ref, query_t, scores_t)
-    total[...] = jnp.zeros_like(total)
-
-    def step(slot, _):
-        score_grad(scores_t, lambda cols: edges_ref[slot, :, cols], counts_ref[slot], total)
-        return 0
-
-    lax.fori_loop(0, live, step, 0)
+    score_grads(live, scores_t, edges_ref, counts_ref, total)
     grad_bf[...] = total[...].astype(BF)
-    first = lax.axis_index("core") * half
-    left_grad = jnp.zeros((half, width), F32)
-    for r in range(nrel):
-        cols = pl.ds(pl.multiple_of(r * rows + first, half), half)
-        table_t = dot(right_bf, grad_bf[:, cols], (0, 0)).astype(BF)
-        left_grad += dot(table_t, op_ref[r].astype(BF), (0, 0))
-    mine = pl.ds(pl.multiple_of(first, half), half)
-    accum = to_column(accum_ref[:, mine])
-    left_out[0:half, :], accum = row_update(left_ref[mine, :], accum, left_grad)
-    accum = jnp.concatenate([to_row(accum)] * (width // half), axis=1)
-    left_out[half : half + 8, :] = jnp.broadcast_to(accum, (8, width))
+    table_t[...] = dot(right_bf, grad_bf[...], (0, 0)).astype(BF)
+    left_grad = table_products(table_t, op_ref)
+    accum = to_column(accum_ref[:, pl.ds(first, half)])
+    pack_rows(left_out, *row_update(left_ref[...], accum, left_grad))
 
 
 def between_kernel(
-    nbatch, idx_ref, left_ref, right_ref, accum_ref, query_t, grad_bf, op_ref, right_out, accum_out, grad_out, edges_out, counts_out
+    nbatch, idx_ref, left_ref, right_ref, accum_ref, op_ref, query_t, grad_bf, table_t,
+    right_out, accum_out, grad_out, edges_out, counts_out,
+    other_query_t, scores_t, total, edges_ref, counts_ref
 ):
-    rows = right_ref.shape[0]
-    pairs = query_t.shape[1]
-
-    def step(member, base, slot):
-        edges_out[slot], counts_out[slot] = count_batch(idx_ref, member, base, rows, pairs)
-
-    each_live_batch(idx_ref, 1, nbatch, step)
+    rows, width = right_ref.shape
+    half = query_t.shape[1] // NREL
+    core = lax.axis_index("core")
+    mine = pl.multiple_of(core * half, half)
+    other = pl.multiple_of((1 - core) * half, half)
+    live, slots = live_slots(idx_ref, 0, nbatch)
+    for slot, (member, base) in enumerate(slots):
+        edges_ref[slot], counts_ref[slot] = count_batch(idx_ref, member, base, rows, other, half)
     right = right_ref[...]
-    right_grad = dot(grad_bf[...], query_t[...], (1, 1))
-    cols = pl.ds(pl.multiple_of(lax.axis_index("core") * rows, rows), rows)
-    table_t = dot(right.astype(BF), grad_bf[:, cols], (0, 0)).astype(BF)
-    grad_out[...] = dot(table_t, left_ref[...].astype(BF), (1, 0))
+    right_bf = right.astype(BF)
+    left_bf = left_ref[pl.ds(other, half), :].astype(BF)
+    queries_and_scores(left_bf, right_bf, op_ref, other_query_t, scores_t)
+    _, slots = live_slots(idx_ref, 1, nbatch)
+    for slot, (member, base) in enumerate(slots):
+        edges_out[slot], counts_out[slot] = count_batch(idx_ref, member, base, rows, 0, rows)
+    score_grads(live, scores_t, edges_ref, counts_ref, total)
+    right_grad = dot(grad_bf[...], query_t[...], (1, 1)) + dot(total[...].astype(BF), other_query_t[...], (1, 1))
     right_out[...], accum = row_update(right, to_column(accum_ref[...]), right_grad)
     accum_out[...] = to_row(accum)
+    cols = pl.ds(mine, half)
+    other_table_t = dot(right_bf, total[:, cols].astype(BF), (0, 0)).astype(BF)
+    my_left_bf = left_ref[pl.ds(mine, half), :].astype(BF)
+    grad_out[...] = dot(table_t[:, cols], my_left_bf, (1, 0)) + dot(other_table_t, left_bf, (1, 0))
 
 
 def second_kernel(
@@ -178,16 +212,10 @@
     right = right_ref[...]
     left_bf, right_bf = left.astype(BF), right.astype(BF)
     queries_and_scores(left_bf, right_bf, op_ref, query_t, scores_t)
-    total[...] = jnp.zeros_like(total)
     live = 0
     for member in range(idx_ref.shape[0]):
         live += idx_ref[member, 8 * nbatch + 1 : 8 * nbatch + 2, :]
-
-    def step(slot, _):
-        score_grad(scores_t, lambda cols: edges_ref[slot, :, cols], counts_ref[slot], total)
-        return 0
-
-    lax.fori_loop(0, jnp.max(live), step, 0)
+    score_grads(jnp.max(live), scores_t, edges_ref, counts_ref, total)
     grad_bf[...] = total[...].astype(BF)
     table_t[...] = dot(right_bf, grad_bf[...], (0, 0)).astype(BF)
     mine = pl.ds(pl.multiple_of(lax.axis_index("core") * rows, rows), rows)
@@ -238,23 +266,27 @@
     nrel, width, _ = relation.shape
     rows = left.shape[0]
     pairs = nrel * rows
-    pair_bf = jax.ShapeDtypeStruct((rows, pairs), BF)
-    left_half, query_t, grad_bf = call(
+    half = rows // 2
+    mine = NREL * half
+    bf16 = lambda *shape: jax.ShapeDtypeStruct(shape, BF)
+    counts = [((SLOTS, rows, mine), F32), ((SLOTS, rows, 128), F32)]
+    moved, query_t, grad_bf, table_t = call(
         functools.partial(first_kernel, nbatch),
         "bucket0_left",
-        (f32(rows // 2 + 8, width), jax.ShapeDtypeStruct((width, pairs), BF), pair_bf),
+        (f32(half + 8, width), bf16(width, mine), bf16(rows, mine), bf16(width, mine)),
         (index, left, left_accum, right, relation),
-        [((rows, width), F32), ((1, rows), F32), ((rows, width), F32), (relation.shape, F32), ((rows, pairs), F32), ((rows, pairs), F32),
-         ((SLOTS, rows, pairs), F32), ((SLOTS, rows, 128), F32)],
+        [((half, width), F32), ((1, rows), F32), ((rows, width), F32), (relation.shape, F32),
+         ((rows, mine), F32), ((rows, mine), F32), *counts],
         flops=2 << 30,
         outside=(1, 2, 3, 4),
     )
-    moved = move(left_half)
+    moved = move(moved)
     right, right_accum, grad, edges, counts = call(
         functools.partial(between_kernel, nbatch),
         "bucket0_right",
         (f32(rows, width), f32(1, rows), f32(width, width), f32(SLOTS, rows, pairs), f32(SLOTS, rows, 128)),
-        (index, left, right, right_accum, query_t, grad_bf, relation),
+        (index, left, right, right_accum, relation, query_t, grad_bf, table_t),
+        [((width, mine), BF), ((rows, mine), F32), ((rows, mine), F32), *counts],
         flops=1 << 30,
     )
     moved = lax.all_gather(moved, "core", axis=0, tiled=False)

time: 88.8 us -> 86.3 us (0.972)
  Pallas kernels: 14.6 us -> 12.4 us
  blocking collectives: 63 us -> 62 us
    pallas_call x5, Pallas kernels: 14.6 us -> 12.4 us  [call(): pl.pallas_call(kernel, out_shape=outs, in_specs=[pl.BlockSpec(memory_spac...]
    all_to_all x1, blocking collectives: 22.1 us -> 21.2 us  [body(): grad = jnp.sum(lax.all_to_all(grad, BLK, 0, 0, tiled=True), axis=0)]
where the time goes in v5:
time: 86.3 us; the launch traced here: 86 us
  blocking collectives  62 us (72%)
  Pallas kernels  12.4 us (14%)
  waiting for transfers between devices  8.72 us (10%)
  starting transfers between devices  1.92 us (2%)
    all_to_all x1, blocking collectives, body(): grad = jnp.sum(lax.all_to_all(grad, BLK, 0, 0, tiled=True), axis=0)  21.2 us
    all_to_all x1, blocking collectives, body(): grad = lax.all_to_all(grad, BLK, 0, 0, tiled=True)  19.8 us
    all_gather x1, blocking collectives, body(): index = lax.all_gather(index, REP, axis=0, tiled=False)  13.8 us
    pallas_call x5, Pallas kernels, call(): pl.pallas_call(kernel, out_shape=outs, in_specs=[pl.BlockSpec(memory_spac...  12.4 us
    ppermute x1, waiting for transfers between devices, body(): lax.ppermute(half, BLK, route)  8.72 us
    all_gather x1, blocking collectives, body(): grad = lax.all_gather(grad, 'core', axis=0, tiled=False)  4.94 us
    all_gather x1, blocking collectives, buckets(): moved = lax.all_gather(moved, 'core', axis=0, tiled=False)  2.37 us
    ppermute x1, starting transfers between devices, body(): lax.ppermute(half, BLK, route)  1.92 us
  transfers between devices with their start and end apart: 1, of which 1 were waited for; matrix products, arithmetic and copies ran while one was open for 0% of the time, Pallas kernels for 3%

profile of v5, /device:TPU:1, one launch (start us, length us, event | category | flops | bytes accessed | tf_op | source)
XLA Modules:
  0.0 86.0 jit_solution(12520887634150997966)
XLA Ops:
  0.6 0.9 gather_index.1
  1.5 13.8 %all-gather = s32[96,512]{1,0:T(8,128)S(1)} all-gather(s32[24,512]{1,0:T(8,128)S(1)} %gather_index.1), channel_id=2, replica_groups=mesh['z'=8,'y'=8,'xl'=2,'xh'=2,'core'=2] {'xh','core'}, dimensions={0}, use_global_device_ids=true | all-gather | bytes 245760 | tf_op jit(solution)/shard_map/all_gather | solution.py:328
  15.3 0.0 copy-start
  15.3 0.0 copy-start.2
  15.3 0.0 copy-start.3
  15.3 0.0 copy-start.4
  15.3 3.1 %bucket0_left.1 = (f32[136,256]{1,0:T(8,128)S(1)}, bf16[256,256]{1,0:T(8,128)(2,1)S(1)}, bf16[256,256]{1,0:T(8,128)(2,1)S(1)}, bf16[256,256]{1,0:T(8,128)(2,1)S(1)}) custom-call(s32[4,24,512]{2,1,0:T(8,128)S(1)} %bitcast.11, f32[256,256]{1,0:T(8,128)} %left_ref.1, f32[1,256]{1,0:T(1,128)} %bitcast.15, f32[256,256]{1,0:T(8,128)} %right_ref.1, ...), custom_call_target="tpu_custom_call" | custom-call | flops 2147483648 | bytes 4194304 | tf_op jit(solution)/shard_map/bucket0_left/pallas_call | solution.py:253
  18.4 1.9 %collective-permute-start = (f32[136,256]{1,0:T(8,128)S(1)}, f32[136,256]{1,0:T(8,128)S(1)}, u32[]{:S(2)}, u32[]{:S(2)}) collective-permute-start(f32[136,256]{1,0:T(8,128)S(1)} %get-tuple-element.27), channel_id=1, source_target_pairs={{0,4},{4,8},{8,12},{12,16},{16,20},{20,24},{24,28},{28,32},{32,36}... | collective-permute-start | bytes 417800 | tf_op jit(solution)/shard_map/ppermute | solution.py:338
  20.3 0.0 copy-done
  20.3 0.0 copy-done.2
  20.3 0.0 copy-done.3
  20.3 0.0 copy-done.4
  20.4 2.9 %bucket0_right.1 = (f32[256,256]{1,0:T(8,128)S(1)}, f32[1,256]{1,0:T(1,128)S(1)}, f32[256,256]{1,0:T(8,128)S(1)}, f32[4,256,512]{2,1,0:T(8,128)S(1)}, f32[4,256,128]{2,1,0:T(8,128)S(1)}) custom-call(s32[4,24,512]{2,1,0:T(8,128)S(1)} %bitcast.12, f32[256,256]{1,0:T(8,128)S(1)} %copy-done.2, f32[256,256]{1,0:T(8,128)S(1)} %copy-done.3, f32[1,256]{1,0:T(1,128)S(1)} %bitcast.14, ...), custom_call_target="tpu_custom_call" | custom-call | flops 1073741824 | bytes 4194304 | tf_op jit(solution)/shard_map/bucket0_right/pallas_call | solution.py:253
  23.2 8.7 %collective-permute-done = f32[136,256]{1,0:T(8,128)S(1)} collective-permute-done((f32[136,256]{1,0:T(8,128)S(1)}, f32[136,256]{1,0:T(8,128)S(1)}, u32[]{:S(2)}, u32[]{:S(2)}) %collective-permute-start) | collective-permute-done | bytes 139296 | tf_op jit(solution)/shard_map/ppermute | solution.py:338
  31.9 2.4 %all-gather.1 = f32[272,256]{1,0:T(8,128)S(1)} all-gather(f32[136,256]{1,0:T(8,128)S(1)} %collective-permute-done), channel_id=3, replica_groups=mesh['z'=8,'y'=8,'xl'=2,'xh'=2,'core'=2] {'core'}, dimensions={0}, use_global_device_ids=true | all-gather | bytes 417792 | tf_op jit(solution)/shard_map/all_gather | solution.py:292
  34.3 4.4 %bucket1.1 = (f32[256,256]{1,0:T(8,128)}, f32[1,256]{1,0:T(1,128)}, f32[256,256]{1,0:T(8,128)}, f32[1,256]{1,0:T(1,128)}, f32[2,64,4,128]{3,2,1,0:T(4,128)S(1)}) custom-call(s32[4,24,512]{2,1,0:T(8,128)S(1)} %bitcast.13, f32[4,256,512]{2,1,0:T(8,128)S(1)} %get-tuple-element.25.edges_ref, f32[4,256,128]{2,1,0:T(8,128)S(1)} %get-tuple-element.26.counts_ref, ...), custom_call_target="tpu_custom_call" | custom-call | flops 2147483648 | bytes 4194304 | tf_op jit(solution)/shard_map/bucket1/pallas_call | solution.py:253
  38.7 0.0 copy-start.1
  38.7 21.2 %all_to_all.10 = f32[128,4,128]{2,1,0:T(4,128)S(1)} all-to-all(f32[128,4,128]{2,1,0:T(4,128)S(1)} %bitcast.10), channel_id=1, replica_groups=mesh['z'=8,'y'=8,'xl'=2,'xh'=2,'core'=2] {'z','y','xl'}, dimensions={0} | all-to-all | bytes 524288 | tf_op jit(solution)/shard_map/all_to_all | solution.py:341
  59.8 0.1 reduce_sum.9
  60.0 19.8 %all_to_all.11 = f32[128,4,128]{2,1,0:T(4,128)S(1)} all-to-all(f32[128,4,128]{2,1,0:T(4,128)S(1)} %broadcast_in_dim.2), channel_id=1, replica_groups=mesh['z'=8,'y'=8,'xl'=2,'xh'=2,'core'=2] {'z','y','xl'}, dimensions={0} | all-to-all | bytes 524288 | tf_op jit(solution)/shard_map/all_to_all | solution.py:343
  79.8 4.9 %all-gather.2 = f32[256,4,128]{2,1,0:T(4,128)S(1)} all-gather(f32[128,4,128]{2,1,0:T(4,128)S(1)} %all_to_all.11), channel_id=4, replica_groups=mesh['z'=8,'y'=8,'xl'=2,'xh'=2,'core'=2] {'core'}, dimensions={0}, use_global_device_ids=true | all-gather | bytes 786432 | tf_op jit(solution)/shard_map/all_gather | solution.py:344
  84.7 0.0 copy-done.1
  84.7 1.2 %final_update.1 = (f32[2,256,256]{2,1,0:T(8,128)}, f32[2,256,256]{2,1,0:T(8,128)}) custom-call(f32[2,2,64,4,128]{4,3,2,1,0:T(4,128)S(1)} %bitcast.8, f32[2,256,256]{2,1,0:T(8,128)S(1)} %copy-done, f32[2,256,256]{2,1,0:T(8,128)S(1)} %copy-done.1), custom_call_target="tpu_custom_call" | custom-call | bytes 4194304 | tf_op jit(solution)/shard_map/final_update/pallas_call | solution.py:253
  (1 shorter events, 0.0 us)
Async XLA Ops:
  15.3 5.0 %copy-start = (f32[2,256,256]{2,1,0:T(8,128)S(1)}, f32[2,256,256]{2,1,0:T(8,128)}, u32[]{:S(2)}) copy-start(f32[2,256,256]{2,1,0:T(8,128)} %relation_ref.1) | copy-start | bytes 1572868
  15.3 5.0 %copy-start.2 = (f32[256,256]{1,0:T(8,128)S(1)}, f32[256,256]{1,0:T(8,128)}, u32[]{:S(2)}) copy-start(f32[256,256]{1,0:T(8,128)} %left_ref.1) | copy-start | bytes 786436
  15.3 5.0 %copy-start.3 = (f32[256,256]{1,0:T(8,128)S(1)}, f32[256,256]{1,0:T(8,128)}, u32[]{:S(2)}) copy-start(f32[256,256]{1,0:T(8,128)} %right_ref.1) | copy-start | bytes 786436
  15.3 5.0 %copy-start.4 = (f32[256]{0:T(256)S(1)}, f32[256]{0:T(256)}, u32[]{:S(2)}) copy-start(f32[256]{0:T(256)} %param.14) | copy-start | bytes 3076
  18.4 13.6 %collective-permute-start = (f32[136,256]{1,0:T(8,128)S(1)}, f32[136,256]{1,0:T(8,128)S(1)}, u32[]{:S(2)}, u32[]{:S(2)}) collective-permute-start(f32[136,256]{1,0:T(8,128)S(1)} %get-tuple-element.27), channel_id=1, source_target_pairs={{0,4},{4,8},{8,12},{12,16},{16,20},{20,24},{24,28},{28,32},{32,36}... | collective-permute-start | bytes 417800 | tf_op jit(solution)/shard_map/ppermute | solution.py:338
  38.7 46.0 %copy-start.1 = (f32[2,256,256]{2,1,0:T(8,128)S(1)}, f32[2,256,256]{2,1,0:T(8,128)}, u32[]{:S(2)}) copy-start(f32[2,256,256]{2,1,0:T(8,128)} %state_ref.1) | copy-start | bytes 1572868

commit v6 on v5

--- a/solution.py
+++ b/solution.py
@@ -70,17 +70,15 @@
 
 
 def score_grad(scores_t, edges_of, counts, total):
+    absent = jnp.where(counts > 0.0, 0.0, -3.0e38)
     for start in range(0, scores_t.shape[1], 128):
         cols = slice(start, start + 128)
         score = scores_t[:, cols]
-        top = jnp.max(jnp.where(counts > 0.0, score, -3.0e38), axis=0, keepdims=True)
-        above = score - top
-        small = jnp.exp(-jnp.abs(above))
-        weighted = counts * small
+        top = jnp.max(score + absent, axis=0, keepdims=True)
+        above = jnp.exp(jnp.minimum(score - top, 88.0))
+        weighted = counts * above
         neg_total = jnp.sum(weighted, axis=0, keepdims=True)
-        neg_scale = jnp.where(above > 0.0, small, 1.0)
-        pos_exp = jnp.where(above > 0.0, 1.0, small)
-        factor = edges_of(cols) * neg_scale / (pos_exp + neg_total * neg_scale)
+        factor = edges_of(cols) / (above + neg_total)
         factor_sum = jnp.sum(factor, axis=0, keepdims=True)
         total[:, cols] += weighted * factor_sum - neg_total * factor
 

time: 86.3 us -> 85.6 us (level)
  Pallas kernels: 12.4 us -> 11.2 us
    pallas_call x5, Pallas kernels: 12.4 us -> 11.2 us  [call(): pl.pallas_call(kernel, out_shape=outs, in_specs=[pl.BlockSpec(memory_spac...]
where the time goes in v6:
time: 85.6 us; the launch traced here: 85.3 us
  blocking collectives  62.5 us (73%)
  Pallas kernels  11.2 us (13%)
  waiting for transfers between devices  8.87 us (10%)
  starting transfers between devices  1.92 us (2%)
    all_to_all x1, blocking collectives, body(): grad = jnp.sum(lax.all_to_all(grad, BLK, 0, 0, tiled=True), axis=0)  21.6 us
    all_to_all x1, blocking collectives, body(): grad = lax.all_to_all(grad, BLK, 0, 0, tiled=True)  19.8 us
    all_gather x1, blocking collectives, body(): index = lax.all_gather(index, REP, axis=0, tiled=False)  13.8 us
    pallas_call x5, Pallas kernels, call(): pl.pallas_call(kernel, out_shape=outs, in_specs=[pl.BlockSpec(memory_spac...  11.2 us
    ppermute x1, waiting for transfers between devices, body(): lax.ppermute(half, BLK, route)  8.87 us
    all_gather x1, blocking collectives, body(): grad = lax.all_gather(grad, 'core', axis=0, tiled=False)  4.94 us
    all_gather x1, blocking collectives, buckets(): moved = lax.all_gather(moved, 'core', axis=0, tiled=False)  2.37 us
    ppermute x1, starting transfers between devices, body(): lax.ppermute(half, BLK, route)  1.92 us
  transfers between devices with their start and end apart: 1, of which 1 were waited for; matrix products, arithmetic and copies ran while one was open for 0% of the time, Pallas kernels for 3%

profile of v6, /device:TPU:1, one launch (start us, length us, event | category | flops | bytes accessed | tf_op | source)
XLA Modules:
  0.0 85.3 jit_solution(442984450519159048)
XLA Ops:
  0.6 0.9 gather_index.1
  1.5 13.8 %all-gather = s32[96,512]{1,0:T(8,128)S(1)} all-gather(s32[24,512]{1,0:T(8,128)S(1)} %gather_index.1), channel_id=2, replica_groups=mesh['z'=8,'y'=8,'xl'=2,'xh'=2,'core'=2] {'xh','core'}, dimensions={0}, use_global_device_ids=true | all-gather | bytes 245760 | tf_op jit(solution)/shard_map/all_gather | solution.py:326
  15.3 0.0 copy-start
  15.3 0.0 copy-start.2
  15.3 0.0 copy-start.3
  15.3 0.0 copy-start.4
  15.3 3.0 %bucket0_left.1 = (f32[136,256]{1,0:T(8,128)S(1)}, bf16[256,256]{1,0:T(8,128)(2,1)S(1)}, bf16[256,256]{1,0:T(8,128)(2,1)S(1)}, bf16[256,256]{1,0:T(8,128)(2,1)S(1)}) custom-call(s32[4,24,512]{2,1,0:T(8,128)S(1)} %bitcast.11, f32[256,256]{1,0:T(8,128)} %left_ref.1, f32[1,256]{1,0:T(1,128)} %bitcast.15, f32[256,256]{1,0:T(8,128)} %right_ref.1, ...), custom_call_target="tpu_custom_call" | custom-call | flops 2147483648 | bytes 4194304 | tf_op jit(solution)/shard_map/bucket0_left/pallas_call | solution.py:251
  18.3 1.9 %collective-permute-start = (f32[136,256]{1,0:T(8,128)S(1)}, f32[136,256]{1,0:T(8,128)S(1)}, u32[]{:S(2)}, u32[]{:S(2)}) collective-permute-start(f32[136,256]{1,0:T(8,128)S(1)} %get-tuple-element.27), channel_id=1, source_target_pairs={{0,4},{4,8},{8,12},{12,16},{16,20},{20,24},{24,28},{28,32},{32,36}... | collective-permute-start | bytes 417800 | tf_op jit(solution)/shard_map/ppermute | solution.py:336
  20.3 0.0 copy-done
  20.3 0.0 copy-done.2
  20.3 0.0 copy-done.3
  20.3 0.0 copy-done.4
  20.3 2.8 %bucket0_right.1 = (f32[256,256]{1,0:T(8,128)S(1)}, f32[1,256]{1,0:T(1,128)S(1)}, f32[256,256]{1,0:T(8,128)S(1)}, f32[4,256,512]{2,1,0:T(8,128)S(1)}, f32[4,256,128]{2,1,0:T(8,128)S(1)}) custom-call(s32[4,24,512]{2,1,0:T(8,128)S(1)} %bitcast.12, f32[256,256]{1,0:T(8,128)S(1)} %copy-done.2, f32[256,256]{1,0:T(8,128)S(1)} %copy-done.3, f32[1,256]{1,0:T(1,128)S(1)} %bitcast.14, ...), custom_call_target="tpu_custom_call" | custom-call | flops 1073741824 | bytes 4194304 | tf_op jit(solution)/shard_map/bucket0_right/pallas_call | solution.py:251
  23.1 8.9 %collective-permute-done = f32[136,256]{1,0:T(8,128)S(1)} collective-permute-done((f32[136,256]{1,0:T(8,128)S(1)}, f32[136,256]{1,0:T(8,128)S(1)}, u32[]{:S(2)}, u32[]{:S(2)}) %collective-permute-start) | collective-permute-done | bytes 139296 | tf_op jit(solution)/shard_map/ppermute | solution.py:336
  32.0 2.4 %all-gather.1 = f32[272,256]{1,0:T(8,128)S(1)} all-gather(f32[136,256]{1,0:T(8,128)S(1)} %collective-permute-done), channel_id=3, replica_groups=mesh['z'=8,'y'=8,'xl'=2,'xh'=2,'core'=2] {'core'}, dimensions={0}, use_global_device_ids=true | all-gather | bytes 417792 | tf_op jit(solution)/shard_map/all_gather | solution.py:290
  34.3 3.3 %bucket1.1 = (f32[256,256]{1,0:T(8,128)}, f32[1,256]{1,0:T(1,128)}, f32[256,256]{1,0:T(8,128)}, f32[1,256]{1,0:T(1,128)}, f32[2,64,4,128]{3,2,1,0:T(4,128)S(1)}) custom-call(s32[4,24,512]{2,1,0:T(8,128)S(1)} %bitcast.13, f32[4,256,512]{2,1,0:T(8,128)S(1)} %get-tuple-element.25.edges_ref, f32[4,256,128]{2,1,0:T(8,128)S(1)} %get-tuple-element.26.counts_ref, ...), custom_call_target="tpu_custom_call" | custom-call | flops 2147483648 | bytes 4194304 | tf_op jit(solution)/shard_map/bucket1/pallas_call | solution.py:251
  37.6 0.0 copy-start.1
  37.6 21.6 %all_to_all.10 = f32[128,4,128]{2,1,0:T(4,128)S(1)} all-to-all(f32[128,4,128]{2,1,0:T(4,128)S(1)} %bitcast.10), channel_id=1, replica_groups=mesh['z'=8,'y'=8,'xl'=2,'xh'=2,'core'=2] {'z','y','xl'}, dimensions={0} | all-to-all | bytes 524288 | tf_op jit(solution)/shard_map/all_to_all | solution.py:339
  59.2 0.1 reduce_sum.9
  59.4 19.8 %all_to_all.11 = f32[128,4,128]{2,1,0:T(4,128)S(1)} all-to-all(f32[128,4,128]{2,1,0:T(4,128)S(1)} %broadcast_in_dim.2), channel_id=1, replica_groups=mesh['z'=8,'y'=8,'xl'=2,'xh'=2,'core'=2] {'z','y','xl'}, dimensions={0} | all-to-all | bytes 524288 | tf_op jit(solution)/shard_map/all_to_all | solution.py:341
  79.2 4.9 %all-gather.2 = f32[256,4,128]{2,1,0:T(4,128)S(1)} all-gather(f32[128,4,128]{2,1,0:T(4,128)S(1)} %all_to_all.11), channel_id=4, replica_groups=mesh['z'=8,'y'=8,'xl'=2,'xh'=2,'core'=2] {'core'}, dimensions={0}, use_global_device_ids=true | all-gather | bytes 786432 | tf_op jit(solution)/shard_map/all_gather | solution.py:342
  84.1 0.0 copy-done.1
  84.1 1.2 %final_update.1 = (f32[2,256,256]{2,1,0:T(8,128)}, f32[2,256,256]{2,1,0:T(8,128)}) custom-call(f32[2,2,64,4,128]{4,3,2,1,0:T(4,128)S(1)} %bitcast.8, f32[2,256,256]{2,1,0:T(8,128)S(1)} %copy-done, f32[2,256,256]{2,1,0:T(8,128)S(1)} %copy-done.1), custom_call_target="tpu_custom_call" | custom-call | bytes 4194304 | tf_op jit(solution)/shard_map/final_update/pallas_call | solution.py:251
  (1 shorter events, 0.0 us)
Async XLA Ops:
  15.3 4.9 %copy-start = (f32[2,256,256]{2,1,0:T(8,128)S(1)}, f32[2,256,256]{2,1,0:T(8,128)}, u32[]{:S(2)}) copy-start(f32[2,256,256]{2,1,0:T(8,128)} %relation_ref.1) | copy-start | bytes 1572868
  15.3 4.9 %copy-start.2 = (f32[256,256]{1,0:T(8,128)S(1)}, f32[256,256]{1,0:T(8,128)}, u32[]{:S(2)}) copy-start(f32[256,256]{1,0:T(8,128)} %left_ref.1) | copy-start | bytes 786436
  15.3 5.0 %copy-start.3 = (f32[256,256]{1,0:T(8,128)S(1)}, f32[256,256]{1,0:T(8,128)}, u32[]{:S(2)}) copy-start(f32[256,256]{1,0:T(8,128)} %right_ref.1) | copy-start | bytes 786436
  15.3 5.0 %copy-start.4 = (f32[256]{0:T(256)S(1)}, f32[256]{0:T(256)}, u32[]{:S(2)}) copy-start(f32[256]{0:T(256)} %param.14) | copy-start | bytes 3076
  18.3 13.6 %collective-permute-start = (f32[136,256]{1,0:T(8,128)S(1)}, f32[136,256]{1,0:T(8,128)S(1)}, u32[]{:S(2)}, u32[]{:S(2)}) collective-permute-start(f32[136,256]{1,0:T(8,128)S(1)} %get-tuple-element.27), channel_id=1, source_target_pairs={{0,4},{4,8},{8,12},{12,16},{16,20},{20,24},{24,28},{28,32},{32,36}... | collective-permute-start | bytes 417800 | tf_op jit(solution)/shard_map/ppermute | solution.py:336
  37.6 46.5 %copy-start.1 = (f32[2,256,256]{2,1,0:T(8,128)S(1)}, f32[2,256,256]{2,1,0:T(8,128)}, u32[]{:S(2)}) copy-start(f32[2,256,256]{2,1,0:T(8,128)} %state_ref.1) | copy-start | bytes 1572868

commit v7 on v6

--- a/solution.py
+++ b/solution.py
@@ -109,12 +109,14 @@
 
 
 def gather_kernel(nbatch, *refs):
-    sources, out_ref, buffers, sems = refs[:5], refs[5], refs[6:11], refs[11]
-    copies = [pltpu.make_async_copy(a, b, sems.at[i]) for i, (a, b) in enumerate(zip(sources, buffers))]
+    sources, staged, out_ref = refs[:5], refs[5:10], refs[10]
+    held, buffers, sems = refs[11:16], refs[16:21], refs[21]
+    pairs = [*zip(sources, buffers), *zip(staged, held)]
+    copies = [pltpu.make_async_copy(*pair, sems.at[i]) for i, pair in enumerate(pairs)]
     for copy in copies:
         copy.start()
     out_ref[8 * nbatch :, :] = jnp.zeros_like(out_ref[8 * nbatch :, :])
-    for copy in copies:
+    for copy in copies[: len(sources)]:
         copy.wait()
     *buffers, live_ref = buffers
     for bucket in range(2):
@@ -125,6 +127,8 @@
             for i, buffer in enumerate(buffers):
                 row = (bucket * nbatch + batch) * 4 + i
                 out_ref[row : row + 1, :] = buffer[0, 0, bucket, batch : batch + 1, :]
+    for copy in copies[len(sources) :]:
+        copy.wait()
 
 
 def score_grads(live, scores_t, edges_ref, counts_ref, total):
@@ -138,34 +142,24 @@
 
 
 def first_kernel(
-    nbatch, idx_ref, left_hbm, accum_hbm, right_hbm, op_hbm, left_out, query_t, grad_bf, table_t,
-    left_ref, accum_ref, right_ref, op_ref, scores_t, total, edges_ref, counts_ref, sems
+    nbatch, idx_ref, left_all_ref, accum_ref, right_ref, op_ref, left_out, query_t, grad_bf, table_t,
+    scores_t, total, edges_ref, counts_ref
 ):
     rows, width = right_ref.shape
-    half = left_ref.shape[0]
+    half = rows // 2
     first = pl.multiple_of(lax.axis_index("core") * half, half)
-    pairs = (
-        (op_hbm, op_ref),
-        (left_hbm.at[pl.ds(first, half), :], left_ref),
-        (right_hbm, right_ref),
-        (accum_hbm, accum_ref),
-    )
-    copies = [pltpu.make_async_copy(*pair, sems.at[i]) for i, pair in enumerate(pairs)]
-    for copy in copies:
-        copy.start()
+    left = left_all_ref[pl.ds(first, half), :]
     live, slots = live_slots(idx_ref, 0, nbatch)
     for slot, (member, base) in enumerate(slots):
         edges_ref[slot], counts_ref[slot] = count_batch(idx_ref, member, base, rows, first, half)
-    for copy in copies:
-        copy.wait()
     right_bf = right_ref[...].astype(BF)
-    queries_and_scores(left_ref[...].astype(BF), right_bf, op_ref, query_t, scores_t)
+    queries_and_scores(left.astype(BF), right_bf, op_ref, query_t, scores_t)
     score_grads(live, scores_t, edges_ref, counts_ref, total)
     grad_bf[...] = total[...].astype(BF)
     table_t[...] = dot(right_bf, grad_bf[...], (0, 0)).astype(BF)
     left_grad = table_products(table_t, op_ref)
     accum = to_column(accum_ref[:, pl.ds(first, half)])
-    pack_rows(left_out, *row_update(left_ref[...], accum, left_grad))
+    pack_rows(left_out, *row_update(left, accum, left_grad))
 
 
 def between_kernel(
@@ -273,10 +267,8 @@
         "bucket0_left",
         (f32(half + 8, width), bf16(width, mine), bf16(rows, mine), bf16(width, mine)),
         (index, left, left_accum, right, relation),
-        [((half, width), F32), ((1, rows), F32), ((rows, width), F32), (relation.shape, F32),
-         ((rows, mine), F32), ((rows, mine), F32), *counts],
+        [((rows, mine), F32), ((rows, mine), F32), *counts],
         flops=2 << 30,
-        outside=(1, 2, 3, 4),
     )
     moved = move(moved)
     right, right_accum, grad, edges, counts = call(
@@ -315,23 +307,20 @@
     rows, width = left_emb.shape
     blocks = lax.axis_size(BLK)
     index_rows = -(-(8 * nbatch + 2) // 8) * 8
-    index = call(
+    arrays = (left_emb, left_state.reshape(1, rows), right_emb, right_state.reshape(1, rows), relation)
+    index, *arrays = call(
         functools.partial(gather_kernel, nbatch),
         "gather_index",
-        (jax.ShapeDtypeStruct((index_rows, batch), jnp.int32),),
-        (edge_src, edge_dst, edge_rel, negatives, batch_counts),
+        (jax.ShapeDtypeStruct((index_rows, batch), jnp.int32), *(f32(*array.shape) for array in arrays)),
+        (edge_src, edge_dst, edge_rel, negatives, batch_counts, *arrays),
         [(edge_src.shape, jnp.int32)] * 4 + [pltpu.SMEM(batch_counts.shape, jnp.int32)],
-        outside=(0, 1, 2, 3, 4),
-    )[0]
+        outside=tuple(range(10)),
+    )
     index = lax.all_gather(index, REP, axis=0, tiled=False)
     route = [(i, (i + 1) % blocks) for i in range(blocks)]
     left, left_accum, right, right_accum, grad = buckets(
         index,
-        left_emb,
-        left_state.reshape(1, rows),
-        right_emb,
-        right_state.reshape(1, rows),
-        relation,
+        *arrays,
         nbatch,
         lambda half: lax.ppermute(half, BLK, route),
     )
@@ -342,7 +331,7 @@
     grad = lax.all_gather(grad, "core", axis=0, tiled=False)
     grad = grad.reshape(relation.shape[0], 2, width // 4, 4, 128)
     relation_new, relation_state_new = call(
-        final_kernel, "final_update", (f32(*relation.shape),) * 2, (grad, relation, relation_state)
+        final_kernel, "final_update", (f32(*relation.shape),) * 2, (grad, arrays[-1], relation_state)
     )
     return (
         left,

time: 85.6 us -> 85.2 us (level)
  waiting for transfers between devices: 8.87 us -> 7.26 us
    ppermute x1, waiting for transfers between devices: 8.87 us -> 7.26 us  [body(): lax.ppermute(half, BLK, route)]
  transfers between devices with their start and end apart: 1 -> 1, of which waited for: 1 -> 1; matrix products, arithmetic and copies ran while one was open for 0% -> 0% of each run, Pallas kernels for 3% -> 4%
where the time goes in v7:
time: 85.2 us; the launch traced here: 84.9 us
  blocking collectives  62.9 us (74%)
  Pallas kernels  12 us (14%)
  waiting for transfers between devices  7.26 us (9%)
  starting transfers between devices  1.92 us (2%)
    all_to_all x1, blocking collectives, body(): grad = jnp.sum(lax.all_to_all(grad, BLK, 0, 0, tiled=True), axis=0)  22 us
    all_to_all x1, blocking collectives, body(): grad = lax.all_to_all(grad, BLK, 0, 0, tiled=True)  19.7 us
    all_gather x1, blocking collectives, body(): index = lax.all_gather(index, REP, axis=0, tiled=False)  13.8 us
    pallas_call x5, Pallas kernels, call(): pl.pallas_call(kernel, out_shape=outs, in_specs=[pl.BlockSpec(memory_spac...  12 us
    ppermute x1, waiting for transfers between devices, body(): lax.ppermute(half, BLK, route)  7.26 us
    all_gather x1, blocking collectives, body(): grad = lax.all_gather(grad, 'core', axis=0, tiled=False)  4.94 us
    all_gather x1, blocking collectives, buckets(): moved = lax.all_gather(moved, 'core', axis=0, tiled=False)  2.37 us
    ppermute x1, starting transfers between devices, body(): lax.ppermute(half, BLK, route)  1.92 us
  transfers between devices with their start and end apart: 1, of which 1 were waited for; matrix products, arithmetic and copies ran while one was open for 0% of the time, Pallas kernels for 4%

profile of v7, /device:TPU:1, one launch (start us, length us, event | category | flops | bytes accessed | tf_op | source)
XLA Modules:
  0.0 84.9 jit_solution(9327182405345897256)
XLA Ops:
  0.6 1.4 %gather_index.1 = (s32[24,512]{1,0:T(8,128)S(1)}, f32[256,256]{1,0:T(8,128)S(1)}, f32[1,256]{1,0:T(1,128)S(1)}, f32[256,256]{1,0:T(8,128)S(1)}, f32[1,256]{1,0:T(1,128)S(1)}, /*index=5*/f32[2,256,256]{2,1,0:T(8,128)S(1)}) custom-call(s32[1,1,2,2,512]{4,3,2,1,0:T(2,128)} %refs_0_.1, s32[1,1,2,2,512]{4,3,2,1,0:T(2,128)} %refs_1_.1, ...), custom_call_target="tpu_custom_call" | custom-call | bytes 4194304 | tf_op jit(solution)/shard_map/gather_index/pallas_call | solution.py:245
  2.0 13.8 %all-gather = s32[96,512]{1,0:T(8,128)S(1)} all-gather(s32[24,512]{1,0:T(8,128)S(1)} %get-tuple-element.28), channel_id=2, replica_groups=mesh['z'=8,'y'=8,'xl'=2,'xh'=2,'core'=2] {'xh','core'}, dimensions={0}, use_global_device_ids=true | all-gather | bytes 245760 | tf_op jit(solution)/shard_map/all_gather | solution.py:319
  15.9 2.7 %bucket0_left.1 = (f32[136,256]{1,0:T(8,128)S(1)}, bf16[256,256]{1,0:T(8,128)(2,1)S(1)}, bf16[256,256]{1,0:T(8,128)(2,1)S(1)}, bf16[256,256]{1,0:T(8,128)(2,1)S(1)}) custom-call(s32[4,24,512]{2,1,0:T(8,128)S(1)} %bitcast.11, f32[256,256]{1,0:T(8,128)S(1)} %get-tuple-element.29.left_all_ref.left_ref, f32[1,256]{1,0:T(1,128)S(1)} %get-tuple-element.33.accum_ref, ...), custom_call_target="tpu_custom_call" | custom-call | flops 2147483648 | bytes 4194304 | tf_op jit(solution)/shard_map/bucket0_left/pallas_call | solution.py:245
  18.5 1.9 %collective-permute-start = (f32[136,256]{1,0:T(8,128)S(1)}, f32[136,256]{1,0:T(8,128)S(1)}, u32[]{:S(2)}, u32[]{:S(2)}) collective-permute-start(f32[136,256]{1,0:T(8,128)S(1)} %get-tuple-element.39), channel_id=1, source_target_pairs={{0,4},{4,8},{8,12},{12,16},{16,20},{20,24},{24,28},{28,32},{32,36}... | collective-permute-start | bytes 417800 | tf_op jit(solution)/shard_map/ppermute | solution.py:325
  20.4 3.4 %bucket0_right.1 = (f32[256,256]{1,0:T(8,128)S(1)}, f32[1,256]{1,0:T(1,128)S(1)}, f32[256,256]{1,0:T(8,128)S(1)}, f32[4,256,512]{2,1,0:T(8,128)S(1)}, f32[4,256,128]{2,1,0:T(8,128)S(1)}) custom-call(s32[4,24,512]{2,1,0:T(8,128)S(1)} %bitcast.12, f32[256,256]{1,0:T(8,128)S(1)} %get-tuple-element.29.left_all_ref.left_ref, ...), custom_call_target="tpu_custom_call" | custom-call | flops 1073741824 | bytes 4194304 | tf_op jit(solution)/shard_map/bucket0_right/pallas_call | solution.py:245
  23.9 7.3 %collective-permute-done = f32[136,256]{1,0:T(8,128)S(1)} collective-permute-done((f32[136,256]{1,0:T(8,128)S(1)}, f32[136,256]{1,0:T(8,128)S(1)}, u32[]{:S(2)}, u32[]{:S(2)}) %collective-permute-start) | collective-permute-done | bytes 139296 | tf_op jit(solution)/shard_map/ppermute | solution.py:325
  31.1 2.4 %all-gather.1 = f32[272,256]{1,0:T(8,128)S(1)} all-gather(f32[136,256]{1,0:T(8,128)S(1)} %collective-permute-done), channel_id=3, replica_groups=mesh['z'=8,'y'=8,'xl'=2,'xh'=2,'core'=2] {'core'}, dimensions={0}, use_global_device_ids=true | all-gather | bytes 417792 | tf_op jit(solution)/shard_map/all_gather | solution.py:282
  33.5 3.3 %bucket1.1 = (f32[256,256]{1,0:T(8,128)}, f32[1,256]{1,0:T(1,128)}, f32[256,256]{1,0:T(8,128)}, f32[1,256]{1,0:T(1,128)}, f32[2,64,4,128]{3,2,1,0:T(4,128)S(1)}) custom-call(s32[4,24,512]{2,1,0:T(8,128)S(1)} %bitcast.13, f32[4,256,512]{2,1,0:T(8,128)S(1)} %get-tuple-element.37.edges_ref, f32[4,256,128]{2,1,0:T(8,128)S(1)} %get-tuple-element.38.counts_ref, ...), custom_call_target="tpu_custom_call" | custom-call | flops 2147483648 | bytes 4194304 | tf_op jit(solution)/shard_map/bucket1/pallas_call | solution.py:245
  36.8 0.0 copy-start
  36.8 22.0 %all_to_all.10 = f32[128,4,128]{2,1,0:T(4,128)S(1)} all-to-all(f32[128,4,128]{2,1,0:T(4,128)S(1)} %bitcast.10), channel_id=1, replica_groups=mesh['z'=8,'y'=8,'xl'=2,'xh'=2,'core'=2] {'z','y','xl'}, dimensions={0} | all-to-all | bytes 524288 | tf_op jit(solution)/shard_map/all_to_all | solution.py:328
  58.8 0.1 reduce_sum.9
  59.0 19.7 %all_to_all.11 = f32[128,4,128]{2,1,0:T(4,128)S(1)} all-to-all(f32[128,4,128]{2,1,0:T(4,128)S(1)} %broadcast_in_dim.2), channel_id=1, replica_groups=mesh['z'=8,'y'=8,'xl'=2,'xh'=2,'core'=2] {'z','y','xl'}, dimensions={0} | all-to-all | bytes 524288 | tf_op jit(solution)/shard_map/all_to_all | solution.py:330
  78.7 4.9 %all-gather.2 = f32[256,4,128]{2,1,0:T(4,128)S(1)} all-gather(f32[128,4,128]{2,1,0:T(4,128)S(1)} %all_to_all.11), channel_id=4, replica_groups=mesh['z'=8,'y'=8,'xl'=2,'xh'=2,'core'=2] {'core'}, dimensions={0}, use_global_device_ids=true | all-gather | bytes 786432 | tf_op jit(solution)/shard_map/all_gather | solution.py:331
  83.7 0.0 copy-done
  83.7 1.2 %final_update.1 = (f32[2,256,256]{2,1,0:T(8,128)}, f32[2,256,256]{2,1,0:T(8,128)}) custom-call(f32[2,2,64,4,128]{4,3,2,1,0:T(4,128)S(1)} %bitcast.8, f32[2,256,256]{2,1,0:T(8,128)S(1)} %get-tuple-element.32.op_ref.relation_ref, f32[2,256,256]{2,1,0:T(8,128)S(1)} %copy-done), custom_call_target="tpu_custom_call" | custom-call | bytes 4194304 | tf_op jit(solution)/shard_map/final_update/pallas_call | solution.py:245
  (1 shorter events, 0.0 us)
Async XLA Ops:
  18.5 12.6 %collective-permute-start = (f32[136,256]{1,0:T(8,128)S(1)}, f32[136,256]{1,0:T(8,128)S(1)}, u32[]{:S(2)}, u32[]{:S(2)}) collective-permute-start(f32[136,256]{1,0:T(8,128)S(1)} %get-tuple-element.39), channel_id=1, source_target_pairs={{0,4},{4,8},{8,12},{12,16},{16,20},{20,24},{24,28},{28,32},{32,36}... | collective-permute-start | bytes 417800 | tf_op jit(solution)/shard_map/ppermute | solution.py:325
  36.8 46.9 %copy-start = (f32[2,256,256]{2,1,0:T(8,128)S(1)}, f32[2,256,256]{2,1,0:T(8,128)}, u32[]{:S(2)}) copy-start(f32[2,256,256]{2,1,0:T(8,128)} %state_ref.1) | copy-start | bytes 1572868

commit v8 on v7

--- a/solution.py
+++ b/solution.py
@@ -13,6 +13,7 @@
 BLK = ("z", "y", "xl")
 REP = ("xh", "core")
 NREL = 2
+LANES = 128
 SLOTS = 4
 
 
@@ -43,15 +44,15 @@
     return embedding - learn_rate * gradient / jnp.sqrt(accum), accum
 
 
-def count_batch(idx_ref, member, base, rows, first, half):
+def count_batch(idx_ref, live, member, base, rows, first, half):
     source = idx_ref[member, pl.ds(base, 1), :] - first
     target = idx_ref[member, pl.ds(base + 1, 1), :]
     relation = idx_ref[member, pl.ds(base + 2, 1), :]
     negative = idx_ref[member, pl.ds(base + 3, 1), :]
-    pair = jnp.where((source >= 0) & (source < half), relation * half + source, -1)
+    pair = jnp.where((source >= 0) & (source < half) & live, relation * half + source, -1)
     edges = dot(one_hot(target, rows), one_hot(pair, NREL * half), (1, 1))
-    counts = dot(one_hot(negative, rows), jnp.ones((negative.shape[1], 128), BF), (1, 0))
-    return edges, counts
+    counts = dot(one_hot(negative, rows), jnp.ones((negative.shape[1], LANES), BF), (1, 0))
+    return edges, jnp.stack([counts, jnp.where(counts > 0.0, 0.0, -3.0e38)])
 
 
 def live_slots(idx_ref, bucket, nbatch):
@@ -65,22 +66,25 @@
         for end in ends[:-1]:
             member = member + jnp.where(slot >= end, 1, 0)
             begin = jnp.where(slot >= end, end, begin)
-        slots.append((member, (bucket * nbatch + jnp.minimum(slot - begin, nbatch - 1)) * 4))
-    return ends[-1], slots
-
-
-def score_grad(scores_t, edges_of, counts, total):
-    absent = jnp.where(counts > 0.0, 0.0, -3.0e38)
-    for start in range(0, scores_t.shape[1], 128):
-        cols = slice(start, start + 128)
+        slots.append((slot < ends[-1], member, (bucket * nbatch + jnp.minimum(slot - begin, nbatch - 1)) * 4))
+    return slots
+
+
+def score_grads(scores_t, edges_ref, counts_ref, grad_bf):
+    for start in range(0, scores_t.shape[1], LANES):
+        cols = slice(start, start + LANES)
         score = scores_t[:, cols]
-        top = jnp.max(score + absent, axis=0, keepdims=True)
-        above = jnp.exp(jnp.minimum(score - top, 88.0))
-        weighted = counts * above
-        neg_total = jnp.sum(weighted, axis=0, keepdims=True)
-        factor = edges_of(cols) / (above + neg_total)
-        factor_sum = jnp.sum(factor, axis=0, keepdims=True)
-        total[:, cols] += weighted * factor_sum - neg_total * factor
+        total = 0.0
+        for slot in range(SLOTS):
+            counts = counts_ref[slot, 0]
+            top = jnp.max(score + counts_ref[slot, 1], axis=0, keepdims=True)
+            above = jnp.exp(jnp.minimum(score - top, 88.0))
+            weighted = counts * above
+            neg_total = jnp.sum(weighted, axis=0, keepdims=True)
+            factor = edges_ref[slot, :, cols] / (above + neg_total)
+            factor_sum = jnp.sum(factor, axis=0, keepdims=True)
+            total += weighted * factor_sum - neg_total * factor
+        grad_bf[:, cols] = total.astype(BF)
 
 
 def queries_and_scores(left_bf, right_bf, op_ref, query_t, scores_t):
@@ -131,31 +135,20 @@
         copy.wait()
 
 
-def score_grads(live, scores_t, edges_ref, counts_ref, total):
-    total[...] = jnp.zeros_like(total)
-
-    def step(slot, _):
-        score_grad(scores_t, lambda cols: edges_ref[slot, :, cols], counts_ref[slot], total)
-        return 0
-
-    lax.fori_loop(0, live, step, 0)
-
-
 def first_kernel(
     nbatch, idx_ref, left_all_ref, accum_ref, right_ref, op_ref, left_out, query_t, grad_bf, table_t,
-    scores_t, total, edges_ref, counts_ref
+    scores_t, edges_ref, counts_ref
 ):
     rows, width = right_ref.shape
     half = rows // 2
     first = pl.multiple_of(lax.axis_index("core") * half, half)
     left = left_all_ref[pl.ds(first, half), :]
-    live, slots = live_slots(idx_ref, 0, nbatch)
-    for slot, (member, base) in enumerate(slots):
-        edges_ref[slot], counts_ref[slot] = count_batch(idx_ref, member, base, rows, first, half)
+    slots = live_slots(idx_ref, 0, nbatch)
+    for slot, batch in enumerate(slots):
+        edges_ref[slot], counts_ref[slot] = count_batch(idx_ref, *batch, rows, first, half)
     right_bf = right_ref[...].astype(BF)
     queries_and_scores(left.astype(BF), right_bf, op_ref, query_t, scores_t)
-    score_grads(live, scores_t, edges_ref, counts_ref, total)
-    grad_bf[...] = total[...].astype(BF)
+    score_grads(scores_t, edges_ref, counts_ref, grad_bf)
     table_t[...] = dot(right_bf, grad_bf[...], (0, 0)).astype(BF)
     left_grad = table_products(table_t, op_ref)
     accum = to_column(accum_ref[:, pl.ds(first, half)])
@@ -165,36 +158,36 @@
 def between_kernel(
     nbatch, idx_ref, left_ref, right_ref, accum_ref, op_ref, query_t, grad_bf, table_t,
     right_out, accum_out, grad_out, edges_out, counts_out,
-    other_query_t, scores_t, total, edges_ref, counts_ref
+    other_query_t, scores_t, other_grad_bf, edges_ref, counts_ref
 ):
     rows, width = right_ref.shape
     half = query_t.shape[1] // NREL
     core = lax.axis_index("core")
     mine = pl.multiple_of(core * half, half)
     other = pl.multiple_of((1 - core) * half, half)
-    live, slots = live_slots(idx_ref, 0, nbatch)
-    for slot, (member, base) in enumerate(slots):
-        edges_ref[slot], counts_ref[slot] = count_batch(idx_ref, member, base, rows, other, half)
+    slots = live_slots(idx_ref, 0, nbatch)
+    for slot, batch in enumerate(slots):
+        edges_ref[slot], counts_ref[slot] = count_batch(idx_ref, *batch, rows, other, half)
     right = right_ref[...]
     right_bf = right.astype(BF)
     left_bf = left_ref[pl.ds(other, half), :].astype(BF)
     queries_and_scores(left_bf, right_bf, op_ref, other_query_t, scores_t)
-    _, slots = live_slots(idx_ref, 1, nbatch)
-    for slot, (member, base) in enumerate(slots):
-        edges_out[slot], counts_out[slot] = count_batch(idx_ref, member, base, rows, 0, rows)
-    score_grads(live, scores_t, edges_ref, counts_ref, total)
-    right_grad = dot(grad_bf[...], query_t[...], (1, 1)) + dot(total[...].astype(BF), other_query_t[...], (1, 1))
+    slots = live_slots(idx_ref, 1, nbatch)
+    for slot, batch in enumerate(slots):
+        edges_out[slot], counts_out[slot] = count_batch(idx_ref, *batch, rows, 0, rows)
+    score_grads(scores_t, edges_ref, counts_ref, other_grad_bf)
+    right_grad = dot(grad_bf[...], query_t[...], (1, 1)) + dot(other_grad_bf[...], other_query_t[...], (1, 1))
     right_out[...], accum = row_update(right, to_column(accum_ref[...]), right_grad)
     accum_out[...] = to_row(accum)
     cols = pl.ds(mine, half)
-    other_table_t = dot(right_bf, total[:, cols].astype(BF), (0, 0)).astype(BF)
+    other_table_t = dot(right_bf, other_grad_bf[:, cols], (0, 0)).astype(BF)
     my_left_bf = left_ref[pl.ds(mine, half), :].astype(BF)
     grad_out[...] = dot(table_t[:, cols], my_left_bf, (1, 0)) + dot(other_table_t, left_bf, (1, 0))
 
 
 def second_kernel(
-    nbatch, idx_ref, edges_ref, counts_ref, left_ref, right_ref, accum_ref, op_ref, grad_ref,
-    left_out, left_accum_out, right_out, right_accum_out, grad_out, query_t, scores_t, total, grad_bf, table_t
+    edges_ref, counts_ref, left_ref, right_ref, accum_ref, op_ref, grad_ref,
+    left_out, left_accum_out, right_out, right_accum_out, grad_out, query_t, scores_t, grad_bf, table_t
 ):
     nrel = op_ref.shape[0]
     rows, width = right_ref.shape
@@ -204,11 +197,7 @@
     right = right_ref[...]
     left_bf, right_bf = left.astype(BF), right.astype(BF)
     queries_and_scores(left_bf, right_bf, op_ref, query_t, scores_t)
-    live = 0
-    for member in range(idx_ref.shape[0]):
-        live += idx_ref[member, 8 * nbatch + 1 : 8 * nbatch + 2, :]
-    score_grads(jnp.max(live), scores_t, edges_ref, counts_ref, total)
-    grad_bf[...] = total[...].astype(BF)
+    score_grads(scores_t, edges_ref, counts_ref, grad_bf)
     table_t[...] = dot(right_bf, grad_bf[...], (0, 0)).astype(BF)
     mine = pl.ds(pl.multiple_of(lax.axis_index("core") * rows, rows), rows)
     grad = dot(table_t[:, mine], left_bf, (1, 0)) + grad_ref[...]
@@ -261,31 +250,31 @@
     half = rows // 2
     mine = NREL * half
     bf16 = lambda *shape: jax.ShapeDtypeStruct(shape, BF)
-    counts = [((SLOTS, rows, mine), F32), ((SLOTS, rows, 128), F32)]
+    counts = [((SLOTS, rows, mine), F32), ((SLOTS, 2, rows, LANES), F32)]
     moved, query_t, grad_bf, table_t = call(
         functools.partial(first_kernel, nbatch),
         "bucket0_left",
         (f32(half + 8, width), bf16(width, mine), bf16(rows, mine), bf16(width, mine)),
         (index, left, left_accum, right, relation),
-        [((rows, mine), F32), ((rows, mine), F32), *counts],
+        [((rows, mine), F32), *counts],
         flops=2 << 30,
     )
     moved = move(moved)
     right, right_accum, grad, edges, counts = call(
         functools.partial(between_kernel, nbatch),
         "bucket0_right",
-        (f32(rows, width), f32(1, rows), f32(width, width), f32(SLOTS, rows, pairs), f32(SLOTS, rows, 128)),
+        (f32(rows, width), f32(1, rows), f32(width, width), f32(SLOTS, rows, pairs), f32(SLOTS, 2, rows, LANES)),
         (index, left, right, right_accum, relation, query_t, grad_bf, table_t),
-        [((width, mine), BF), ((rows, mine), F32), ((rows, mine), F32), *counts],
+        [((width, mine), BF), ((rows, mine), F32), ((rows, mine), BF), *counts],
         flops=1 << 30,
     )
     moved = lax.all_gather(moved, "core", axis=0, tiled=False)
     return call(
-        functools.partial(second_kernel, nbatch),
+        second_kernel,
         "bucket1",
         (f32(rows, width), f32(1, rows), f32(rows, width), f32(1, rows), f32(2, width // 4, 4, 128)),
-        (index, edges, counts, moved, right, right_accum, relation, grad),
-        [((width, pairs), BF), ((rows, pairs), F32), ((rows, pairs), F32), ((rows, pairs), BF), ((width, pairs), BF)],
+        (edges, counts, moved, right, right_accum, relation, grad),
+        [((width, pairs), BF), ((rows, pairs), F32), ((rows, pairs), BF), ((width, pairs), BF)],
         flops=2 << 30,
     )
 

time: 85.2 us -> 84.8 us (level)
  waiting for transfers between devices: 7.26 us -> 8.37 us
  blocking collectives: 62.9 us -> 62 us
    ppermute x1, waiting for transfers between devices: 7.26 us -> 8.37 us  [body(): lax.ppermute(half, BLK, route)]
  transfers between devices with their start and end apart: 1 -> 1, of which waited for: 1 -> 1; matrix products, arithmetic and copies ran while one was open for 0% -> 0% of each run, Pallas kernels for 4% -> 3%
where the time goes in v8:
time: 84.8 us; the launch traced here: 84.5 us
  blocking collectives  62 us (73%)
  Pallas kernels  11.4 us (13%)
  waiting for transfers between devices  8.37 us (10%)
  starting transfers between devices  1.92 us (2%)
    all_to_all x1, blocking collectives, body(): grad = jnp.sum(lax.all_to_all(grad, BLK, 0, 0, tiled=True), axis=0)  21.2 us
    all_to_all x1, blocking collectives, body(): grad = lax.all_to_all(grad, BLK, 0, 0, tiled=True)  19.8 us
    all_gather x1, blocking collectives, body(): index = lax.all_gather(index, REP, axis=0, tiled=False)  13.8 us
    pallas_call x5, Pallas kernels, call(): pl.pallas_call(kernel, out_shape=outs, in_specs=[pl.BlockSpec(memory_spac...  11.4 us
    ppermute x1, waiting for transfers between devices, body(): lax.ppermute(half, BLK, route)  8.37 us
    all_gather x1, blocking collectives, body(): grad = lax.all_gather(grad, 'core', axis=0, tiled=False)  4.94 us
    all_gather x1, blocking collectives, buckets(): moved = lax.all_gather(moved, 'core', axis=0, tiled=False)  2.28 us
    ppermute x1, starting transfers between devices, body(): lax.ppermute(half, BLK, route)  1.92 us
  transfers between devices with their start and end apart: 1, of which 1 were waited for; matrix products, arithmetic and copies ran while one was open for 0% of the time, Pallas kernels for 3%

profile of v8, /device:TPU:1, one launch (start us, length us, event | category | flops | bytes accessed | tf_op | source)
XLA Modules:
  0.0 84.5 jit_solution(16358652621015728226)
XLA Ops:
  0.6 1.4 %gather_index.1 = (s32[24,512]{1,0:T(8,128)S(1)}, f32[256,256]{1,0:T(8,128)S(1)}, f32[1,256]{1,0:T(1,128)S(1)}, f32[256,256]{1,0:T(8,128)S(1)}, f32[1,256]{1,0:T(1,128)S(1)}, /*index=5*/f32[2,256,256]{2,1,0:T(8,128)S(1)}) custom-call(s32[1,1,2,2,512]{4,3,2,1,0:T(2,128)} %refs_0_.1, s32[1,1,2,2,512]{4,3,2,1,0:T(2,128)} %refs_1_.1, ...), custom_call_target="tpu_custom_call" | custom-call | bytes 4194304 | tf_op jit(solution)/shard_map/gather_index/pallas_call | solution.py:234
  2.0 13.8 %all-gather = s32[96,512]{1,0:T(8,128)S(1)} all-gather(s32[24,512]{1,0:T(8,128)S(1)} %get-tuple-element.28), channel_id=2, replica_groups=mesh['z'=8,'y'=8,'xl'=2,'xh'=2,'core'=2] {'xh','core'}, dimensions={0}, use_global_device_ids=true | all-gather | bytes 245760 | tf_op jit(solution)/shard_map/all_gather | solution.py:308
  15.9 2.5 %bucket0_left.1 = (f32[136,256]{1,0:T(8,128)S(1)}, bf16[256,256]{1,0:T(8,128)(2,1)S(1)}, bf16[256,256]{1,0:T(8,128)(2,1)S(1)}, bf16[256,256]{1,0:T(8,128)(2,1)S(1)}) custom-call(s32[4,24,512]{2,1,0:T(8,128)S(1)} %bitcast.11, f32[256,256]{1,0:T(8,128)S(1)} %get-tuple-element.29.left_all_ref.left_ref, f32[1,256]{1,0:T(1,128)S(1)} %get-tuple-element.33.accum_ref, ...), custom_call_target="tpu_custom_call" | custom-call | flops 2147483648 | bytes 4194304 | tf_op jit(solution)/shard_map/bucket0_left/pallas_call | solution.py:234
  18.4 1.9 %collective-permute-start = (f32[136,256]{1,0:T(8,128)S(1)}, f32[136,256]{1,0:T(8,128)S(1)}, u32[]{:S(2)}, u32[]{:S(2)}) collective-permute-start(f32[136,256]{1,0:T(8,128)S(1)} %get-tuple-element.39), channel_id=1, source_target_pairs={{0,4},{4,8},{8,12},{12,16},{16,20},{20,24},{24,28},{28,32},{32,36}... | collective-permute-start | bytes 417800 | tf_op jit(solution)/shard_map/ppermute | solution.py:314
  20.3 2.8 %bucket0_right.1 = (f32[256,256]{1,0:T(8,128)S(1)}, f32[1,256]{1,0:T(1,128)S(1)}, f32[256,256]{1,0:T(8,128)S(1)}, f32[4,256,512]{2,1,0:T(8,128)S(1)}, f32[4,2,256,128]{3,2,1,0:T(8,128)S(1)}) custom-call(s32[4,24,512]{2,1,0:T(8,128)S(1)} %bitcast.12, f32[256,256]{1,0:T(8,128)S(1)} %get-tuple-element.29.left_all_ref.left_ref, ...), custom_call_target="tpu_custom_call" | custom-call | flops 1073741824 | bytes 4194304 | tf_op jit(solution)/shard_map/bucket0_right/pallas_call | solution.py:234
  23.1 8.4 %collective-permute-done = f32[136,256]{1,0:T(8,128)S(1)} collective-permute-done((f32[136,256]{1,0:T(8,128)S(1)}, f32[136,256]{1,0:T(8,128)S(1)}, u32[]{:S(2)}, u32[]{:S(2)}) %collective-permute-start) | collective-permute-done | bytes 139296 | tf_op jit(solution)/shard_map/ppermute | solution.py:314
  31.4 2.3 %all-gather.1 = f32[272,256]{1,0:T(8,128)S(1)} all-gather(f32[136,256]{1,0:T(8,128)S(1)} %collective-permute-done), channel_id=3, replica_groups=mesh['z'=8,'y'=8,'xl'=2,'xh'=2,'core'=2] {'core'}, dimensions={0}, use_global_device_ids=true | all-gather | bytes 417792 | tf_op jit(solution)/shard_map/all_gather | solution.py:271
  33.7 3.4 %bucket1.1 = (f32[256,256]{1,0:T(8,128)}, f32[1,256]{1,0:T(1,128)}, f32[256,256]{1,0:T(8,128)}, f32[1,256]{1,0:T(1,128)}, f32[2,64,4,128]{3,2,1,0:T(4,128)S(1)}) custom-call(f32[4,256,512]{2,1,0:T(8,128)S(1)} %get-tuple-element.37.edges_ref, f32[4,2,256,128]{3,2,1,0:T(8,128)S(1)} %get-tuple-element.38.counts_ref, f32[2,136,256]{2,1,0:T(8,128)S(1)} %bitcast.9, ...), custom_call_target="tpu_custom_call" | custom-call | flops 2147483648 | bytes 4194304 | tf_op jit(solution)/shard_map/bucket1/pallas_call | solution.py:234
  37.2 0.0 copy-start
  37.2 21.2 %all_to_all.10 = f32[128,4,128]{2,1,0:T(4,128)S(1)} all-to-all(f32[128,4,128]{2,1,0:T(4,128)S(1)} %bitcast.10), channel_id=1, replica_groups=mesh['z'=8,'y'=8,'xl'=2,'xh'=2,'core'=2] {'z','y','xl'}, dimensions={0} | all-to-all | bytes 524288 | tf_op jit(solution)/shard_map/all_to_all | solution.py:317
  58.3 0.1 reduce_sum.9
  58.5 19.8 %all_to_all.11 = f32[128,4,128]{2,1,0:T(4,128)S(1)} all-to-all(f32[128,4,128]{2,1,0:T(4,128)S(1)} %broadcast_in_dim.2), channel_id=1, replica_groups=mesh['z'=8,'y'=8,'xl'=2,'xh'=2,'core'=2] {'z','y','xl'}, dimensions={0} | all-to-all | bytes 524288 | tf_op jit(solution)/shard_map/all_to_all | solution.py:319
  78.3 4.9 %all-gather.2 = f32[256,4,128]{2,1,0:T(4,128)S(1)} all-gather(f32[128,4,128]{2,1,0:T(4,128)S(1)} %all_to_all.11), channel_id=4, replica_groups=mesh['z'=8,'y'=8,'xl'=2,'xh'=2,'core'=2] {'core'}, dimensions={0}, use_global_device_ids=true | all-gather | bytes 786432 | tf_op jit(solution)/shard_map/all_gather | solution.py:320
  83.2 0.0 copy-done
  83.2 1.2 %final_update.1 = (f32[2,256,256]{2,1,0:T(8,128)}, f32[2,256,256]{2,1,0:T(8,128)}) custom-call(f32[2,2,64,4,128]{4,3,2,1,0:T(4,128)S(1)} %bitcast.8, f32[2,256,256]{2,1,0:T(8,128)S(1)} %get-tuple-element.32.op_ref.relation_ref, f32[2,256,256]{2,1,0:T(8,128)S(1)} %copy-done), custom_call_target="tpu_custom_call" | custom-call | bytes 4194304 | tf_op jit(solution)/shard_map/final_update/pallas_call | solution.py:234
  (1 shorter events, 0.0 us)
Async XLA Ops:
  18.4 13.1 %collective-permute-start = (f32[136,256]{1,0:T(8,128)S(1)}, f32[136,256]{1,0:T(8,128)S(1)}, u32[]{:S(2)}, u32[]{:S(2)}) collective-permute-start(f32[136,256]{1,0:T(8,128)S(1)} %get-tuple-element.39), channel_id=1, source_target_pairs={{0,4},{4,8},{8,12},{12,16},{16,20},{20,24},{24,28},{28,32},{32,36}... | collective-permute-start | bytes 417800 | tf_op jit(solution)/shard_map/ppermute | solution.py:314
  37.2 46.1 %copy-start = (f32[2,256,256]{2,1,0:T(8,128)S(1)}, f32[2,256,256]{2,1,0:T(8,128)}, u32[]{:S(2)}) copy-start(f32[2,256,256]{2,1,0:T(8,128)} %state_ref.1) | copy-start | bytes 1572868

commit v9 on v8

--- a/solution.py
+++ b/solution.py
@@ -213,8 +213,13 @@
     right_accum_out[...] = to_row(accum)
 
 
-def final_kernel(total_ref, relation_ref, state_ref, relation_out, state_out):
+def final_kernel(total_ref, relation_ref, state_ref, *refs):
+    rows_refs, rows_hbm = refs[:4], refs[6:10]
+    relation_hbm, state_hbm, relation_out, state_out, sems = *refs[4:6], *refs[10:13]
     nrel, width, _ = relation_ref.shape
+    copies = [pltpu.make_async_copy(here, there, sems.at[i]) for i, (here, there) in enumerate(zip(rows_refs, rows_hbm))]
+    for copy in copies:
+        copy.start()
     for r in range(nrel):
         for part in range(2):
             cols = slice(part * 128, (part + 1) * 128)
@@ -222,20 +227,26 @@
             state = state_ref[r, :, cols] + grad * grad
             state_out[r, :, cols] = state
             relation_out[r, :, cols] = relation_ref[r, :, cols] - learn_rate * grad / jnp.sqrt(state)
+        for here, there in ((relation_out, relation_hbm), (state_out, state_hbm)):
+            copies.append(pltpu.make_async_copy(here.at[r], there.at[r], sems.at[len(copies)]))
+            copies[-1].start()
+    for copy in copies:
+        copy.wait()
 
 
 def f32(*shape):
     return jax.ShapeDtypeStruct(shape, F32)
 
 
-def call(kernel, name, outs, args, scratch=(), flops=0, outside=()):
+def call(kernel, name, outs, args, scratch=(), flops=0, outside=(), outputs_outside=False):
+    out_space = pltpu.HBM if outputs_outside else pltpu.VMEM
     spaces = [pltpu.HBM if i in outside else pltpu.VMEM for i in range(len(args))]
     sems = [pltpu.SemaphoreType.DMA((len(outside),))] if outside else []
     return pl.pallas_call(
         kernel,
         out_shape=outs,
         in_specs=[pl.BlockSpec(memory_space=space) for space in spaces],
-        out_specs=[pl.BlockSpec(memory_space=pltpu.VMEM)] * len(outs),
+        out_specs=[pl.BlockSpec(memory_space=out_space)] * len(outs),
         scratch_shapes=[pltpu.VMEM(*one) if isinstance(one, tuple) else one for one in scratch] + sems,
         compiler_params=pltpu.CompilerParams(vmem_limit_bytes=30 << 20),
         cost_estimate=pl.CostEstimate(flops=flops, bytes_accessed=4 << 20, transcendentals=0),
@@ -319,8 +330,14 @@
     grad = lax.all_to_all(grad, BLK, 0, 0, tiled=True)
     grad = lax.all_gather(grad, "core", axis=0, tiled=False)
     grad = grad.reshape(relation.shape[0], 2, width // 4, 4, 128)
-    relation_new, relation_state_new = call(
-        final_kernel, "final_update", (f32(*relation.shape),) * 2, (grad, arrays[-1], relation_state)
+    updated = (left, left_accum, right, right_accum)
+    relation_new, relation_state_new, left, left_accum, right, right_accum = call(
+        final_kernel,
+        "final_update",
+        tuple(f32(*array.shape) for array in (relation, relation_state, *updated)),
+        (grad, arrays[-1], relation_state, *updated),
+        [(relation.shape, F32)] * 2 + [pltpu.SemaphoreType.DMA((8,))],
+        outputs_outside=True,
     )
     return (
         left,

time: 84.8 us -> 83.9 us (0.989)
  Pallas kernels: 11.4 us -> 10.5 us
    pallas_call x5, Pallas kernels: 11.4 us -> 10.5 us  [call(): pl.pallas_call(kernel, out_shape=outs, in_specs=[pl.BlockSpec(memory_spac...]
where the time goes in v9:
time: 83.9 us; the launch traced here: 83.6 us
  blocking collectives  62 us (74%)
  Pallas kernels  10.5 us (13%)
  waiting for transfers between devices  8.37 us (10%)
  starting transfers between devices  1.92 us (2%)
    all_to_all x1, blocking collectives, body(): grad = jnp.sum(lax.all_to_all(grad, BLK, 0, 0, tiled=True), axis=0)  21.2 us
    all_to_all x1, blocking collectives, body(): grad = lax.all_to_all(grad, BLK, 0, 0, tiled=True)  19.8 us
    all_gather x1, blocking collectives, body(): index = lax.all_gather(index, REP, axis=0, tiled=False)  13.8 us
    pallas_call x5, Pallas kernels, call(): pl.pallas_call(kernel, out_shape=outs, in_specs=[pl.BlockSpec(memory_spac...  10.5 us
    ppermute x1, waiting for transfers between devices, body(): lax.ppermute(half, BLK, route)  8.37 us
    all_gather x1, blocking collectives, body(): grad = lax.all_gather(grad, 'core', axis=0, tiled=False)  4.93 us
    all_gather x1, blocking collectives, buckets(): moved = lax.all_gather(moved, 'core', axis=0, tiled=False)  2.28 us
    ppermute x1, starting transfers between devices, body(): lax.ppermute(half, BLK, route)  1.92 us
  transfers between devices with their start and end apart: 1, of which 1 were waited for; matrix products, arithmetic and copies ran while one was open for 0% of the time, Pallas kernels for 3%

profile of v9, /device:TPU:1, one launch (start us, length us, event | category | flops | bytes accessed | tf_op | source)
XLA Modules:
  0.0 83.6 jit_solution(8234678322532864025)
XLA Ops:
  0.6 1.4 %gather_index.1 = (s32[24,512]{1,0:T(8,128)S(1)}, f32[256,256]{1,0:T(8,128)S(1)}, f32[1,256]{1,0:T(1,128)S(1)}, f32[256,256]{1,0:T(8,128)S(1)}, f32[1,256]{1,0:T(1,128)S(1)}, /*index=5*/f32[2,256,256]{2,1,0:T(8,128)S(1)}) custom-call(s32[1,1,2,2,512]{4,3,2,1,0:T(2,128)} %refs_0_.1, s32[1,1,2,2,512]{4,3,2,1,0:T(2,128)} %refs_1_.1, ...), custom_call_target="tpu_custom_call" | custom-call | bytes 4194304 | tf_op jit(solution)/shard_map/gather_index/pallas_call | solution.py:245
  2.0 13.8 %all-gather = s32[96,512]{1,0:T(8,128)S(1)} all-gather(s32[24,512]{1,0:T(8,128)S(1)} %get-tuple-element.32), channel_id=2, replica_groups=mesh['z'=8,'y'=8,'xl'=2,'xh'=2,'core'=2] {'xh','core'}, dimensions={0}, use_global_device_ids=true | all-gather | bytes 245760 | tf_op jit(solution)/shard_map/all_gather | solution.py:319
  15.9 2.5 %bucket0_left.1 = (f32[136,256]{1,0:T(8,128)S(1)}, bf16[256,256]{1,0:T(8,128)(2,1)S(1)}, bf16[256,256]{1,0:T(8,128)(2,1)S(1)}, bf16[256,256]{1,0:T(8,128)(2,1)S(1)}) custom-call(s32[4,24,512]{2,1,0:T(8,128)S(1)} %bitcast.11, f32[256,256]{1,0:T(8,128)S(1)} %get-tuple-element.33.left_all_ref.left_ref, f32[1,256]{1,0:T(1,128)S(1)} %get-tuple-element.37.accum_ref, ...), custom_call_target="tpu_custom_call" | custom-call | flops 2147483648 | bytes 4194304 | tf_op jit(solution)/shard_map/bucket0_left/pallas_call | solution.py:245
  18.4 1.9 %collective-permute-start = (f32[136,256]{1,0:T(8,128)S(1)}, f32[136,256]{1,0:T(8,128)S(1)}, u32[]{:S(2)}, u32[]{:S(2)}) collective-permute-start(f32[136,256]{1,0:T(8,128)S(1)} %get-tuple-element.43), channel_id=1, source_target_pairs={{0,4},{4,8},{8,12},{12,16},{16,20},{20,24},{24,28},{28,32},{32,36}... | collective-permute-start | bytes 417800 | tf_op jit(solution)/shard_map/ppermute | solution.py:325
  20.3 2.8 %bucket0_right.1 = (f32[256,256]{1,0:T(8,128)S(1)}, f32[1,256]{1,0:T(1,128)S(1)}, f32[256,256]{1,0:T(8,128)S(1)}, f32[4,256,512]{2,1,0:T(8,128)S(1)}, f32[4,2,256,128]{3,2,1,0:T(8,128)S(1)}) custom-call(s32[4,24,512]{2,1,0:T(8,128)S(1)} %bitcast.12, f32[256,256]{1,0:T(8,128)S(1)} %get-tuple-element.33.left_all_ref.left_ref, ...), custom_call_target="tpu_custom_call" | custom-call | flops 1073741824 | bytes 4194304 | tf_op jit(solution)/shard_map/bucket0_right/pallas_call | solution.py:245
  23.1 8.4 %collective-permute-done = f32[136,256]{1,0:T(8,128)S(1)} collective-permute-done((f32[136,256]{1,0:T(8,128)S(1)}, f32[136,256]{1,0:T(8,128)S(1)}, u32[]{:S(2)}, u32[]{:S(2)}) %collective-permute-start) | collective-permute-done | bytes 139296 | tf_op jit(solution)/shard_map/ppermute | solution.py:325
  31.4 2.3 %all-gather.1 = f32[272,256]{1,0:T(8,128)S(1)} all-gather(f32[136,256]{1,0:T(8,128)S(1)} %collective-permute-done), channel_id=3, replica_groups=mesh['z'=8,'y'=8,'xl'=2,'xh'=2,'core'=2] {'core'}, dimensions={0}, use_global_device_ids=true | all-gather | bytes 417792 | tf_op jit(solution)/shard_map/all_gather | solution.py:282
  33.7 2.6 %bucket1.1 = (f32[256,256]{1,0:T(8,128)S(1)}, f32[1,256]{1,0:T(1,128)S(1)}, f32[256,256]{1,0:T(8,128)S(1)}, f32[1,256]{1,0:T(1,128)S(1)}, f32[2,64,4,128]{3,2,1,0:T(4,128)S(1)}) custom-call(f32[4,256,512]{2,1,0:T(8,128)S(1)} %get-tuple-element.41.edges_ref, f32[4,2,256,128]{3,2,1,0:T(8,128)S(1)} %get-tuple-element.42.counts_ref, f32[2,136,256]{2,1,0:T(8,128)S(1)} %bitcast.9, ...), custom_call_target="tpu_custom_call" | custom-call | flops 2147483648 | bytes 4194304 | tf_op jit(solution)/shard_map/bucket1/pallas_call | solution.py:245
  36.3 0.0 copy-start
  36.3 21.2 %all_to_all.10 = f32[128,4,128]{2,1,0:T(4,128)S(1)} all-to-all(f32[128,4,128]{2,1,0:T(4,128)S(1)} %bitcast.10), channel_id=1, replica_groups=mesh['z'=8,'y'=8,'xl'=2,'xh'=2,'core'=2] {'z','y','xl'}, dimensions={0} | all-to-all | bytes 524288 | tf_op jit(solution)/shard_map/all_to_all | solution.py:328
  57.5 0.1 reduce_sum.9
  57.7 19.8 %all_to_all.11 = f32[128,4,128]{2,1,0:T(4,128)S(1)} all-to-all(f32[128,4,128]{2,1,0:T(4,128)S(1)} %broadcast_in_dim.2), channel_id=1, replica_groups=mesh['z'=8,'y'=8,'xl'=2,'xh'=2,'core'=2] {'z','y','xl'}, dimensions={0} | all-to-all | bytes 524288 | tf_op jit(solution)/shard_map/all_to_all | solution.py:330
  77.4 4.9 %all-gather.2 = f32[256,4,128]{2,1,0:T(4,128)S(1)} all-gather(f32[128,4,128]{2,1,0:T(4,128)S(1)} %all_to_all.11), channel_id=4, replica_groups=mesh['z'=8,'y'=8,'xl'=2,'xh'=2,'core'=2] {'core'}, dimensions={0}, use_global_device_ids=true | all-gather | bytes 786432 | tf_op jit(solution)/shard_map/all_gather | solution.py:331
  82.4 0.0 copy-done
  82.4 1.2 %final_update.1 = (f32[2,256,256]{2,1,0:T(8,128)}, f32[2,256,256]{2,1,0:T(8,128)}, f32[256,256]{1,0:T(8,128)}, f32[1,256]{1,0:T(1,128)}, f32[256,256]{1,0:T(8,128)}, /*index=5*/f32[1,256]{1,0:T(1,128)}) custom-call(f32[2,2,64,4,128]{4,3,2,1,0:T(4,128)S(1)} %bitcast.8, f32[2,256,256]{2,1,0:T(8,128)S(1)} %get-tuple-element.36.op_ref.relation_ref, ...), custom_call_target="tpu_custom_call" | custom-call | bytes 4194304 | tf_op jit(solution)/shard_map/final_update/pallas_call | solution.py:245
  (1 shorter events, 0.0 us)
Async XLA Ops:
  18.4 13.1 %collective-permute-start = (f32[136,256]{1,0:T(8,128)S(1)}, f32[136,256]{1,0:T(8,128)S(1)}, u32[]{:S(2)}, u32[]{:S(2)}) collective-permute-start(f32[136,256]{1,0:T(8,128)S(1)} %get-tuple-element.43), channel_id=1, source_target_pairs={{0,4},{4,8},{8,12},{12,16},{16,20},{20,24},{24,28},{28,32},{32,36}... | collective-permute-start | bytes 417800 | tf_op jit(solution)/shard_map/ppermute | solution.py:325
  36.3 46.1 %copy-start = (f32[2,256,256]{2,1,0:T(8,128)S(1)}, f32[2,256,256]{2,1,0:T(8,128)}, u32[]{:S(2)}) copy-start(f32[2,256,256]{2,1,0:T(8,128)} %state_ref.1) | copy-start | bytes 1572868

commit v10 on v9

--- a/solution.py
+++ b/solution.py
@@ -70,7 +70,7 @@
     return slots
 
 
-def score_grads(scores_t, edges_ref, counts_ref, grad_bf):
+def score_grads(scores_t, edges_ref, counts_ref, grad_bf, rest_bf=None):
     for start in range(0, scores_t.shape[1], LANES):
         cols = slice(start, start + LANES)
         score = scores_t[:, cols]
@@ -84,7 +84,10 @@
             factor = edges_ref[slot, :, cols] / (above + neg_total)
             factor_sum = jnp.sum(factor, axis=0, keepdims=True)
             total += weighted * factor_sum - neg_total * factor
-        grad_bf[:, cols] = total.astype(BF)
+        rounded = total.astype(BF)
+        grad_bf[:, cols] = rounded
+        if rest_bf is not None:
+            rest_bf[:, cols] = (total - rounded.astype(F32)).astype(BF)
 
 
 def queries_and_scores(left_bf, right_bf, op_ref, query_t, scores_t):
@@ -136,7 +139,7 @@
 
 
 def first_kernel(
-    nbatch, idx_ref, left_all_ref, accum_ref, right_ref, op_ref, left_out, query_t, grad_bf, table_t,
+    nbatch, idx_ref, left_all_ref, accum_ref, right_ref, op_ref, left_out, query_t, grad_bf, rest_bf, table_t,
     scores_t, edges_ref, counts_ref
 ):
     rows, width = right_ref.shape
@@ -148,17 +151,18 @@
         edges_ref[slot], counts_ref[slot] = count_batch(idx_ref, *batch, rows, first, half)
     right_bf = right_ref[...].astype(BF)
     queries_and_scores(left.astype(BF), right_bf, op_ref, query_t, scores_t)
-    score_grads(scores_t, edges_ref, counts_ref, grad_bf)
-    table_t[...] = dot(right_bf, grad_bf[...], (0, 0)).astype(BF)
+    score_grads(scores_t, edges_ref, counts_ref, grad_bf, rest_bf)
+    table = dot(right_bf, grad_bf[...], (0, 0)) + dot(right_bf, rest_bf[...], (0, 0))
+    table_t[...] = table.astype(BF)
     left_grad = table_products(table_t, op_ref)
     accum = to_column(accum_ref[:, pl.ds(first, half)])
     pack_rows(left_out, *row_update(left, accum, left_grad))
 
 
 def between_kernel(
-    nbatch, idx_ref, left_ref, right_ref, accum_ref, op_ref, query_t, grad_bf, table_t,
+    nbatch, idx_ref, left_ref, right_ref, accum_ref, op_ref, query_t, grad_bf, rest_bf, table_t,
     right_out, accum_out, grad_out, edges_out, counts_out,
-    other_query_t, scores_t, other_grad_bf, edges_ref, counts_ref
+    other_query_t, scores_t, other_grad_bf, other_rest_bf, edges_ref, counts_ref
 ):
     rows, width = right_ref.shape
     half = query_t.shape[1] // NREL
@@ -175,12 +179,15 @@
     slots = live_slots(idx_ref, 1, nbatch)
     for slot, batch in enumerate(slots):
         edges_out[slot], counts_out[slot] = count_batch(idx_ref, *batch, rows, 0, rows)
-    score_grads(scores_t, edges_ref, counts_ref, other_grad_bf)
-    right_grad = dot(grad_bf[...], query_t[...], (1, 1)) + dot(other_grad_bf[...], other_query_t[...], (1, 1))
+    score_grads(scores_t, edges_ref, counts_ref, other_grad_bf, other_rest_bf)
+    my_grad = dot(grad_bf[...], query_t[...], (1, 1)) + dot(rest_bf[...], query_t[...], (1, 1))
+    other_grad = dot(other_grad_bf[...], other_query_t[...], (1, 1)) + dot(other_rest_bf[...], other_query_t[...], (1, 1))
+    right_grad = my_grad + other_grad
     right_out[...], accum = row_update(right, to_column(accum_ref[...]), right_grad)
     accum_out[...] = to_row(accum)
     cols = pl.ds(mine, half)
-    other_table_t = dot(right_bf, other_grad_bf[:, cols], (0, 0)).astype(BF)
+    other_table = dot(right_bf, other_grad_bf[:, cols], (0, 0)) + dot(right_bf, other_rest_bf[:, cols], (0, 0))
+    other_table_t = other_table.astype(BF)
     my_left_bf = left_ref[pl.ds(mine, half), :].astype(BF)
     grad_out[...] = dot(table_t[:, cols], my_left_bf, (1, 0)) + dot(other_table_t, left_bf, (1, 0))
 
@@ -262,10 +269,10 @@
     mine = NREL * half
     bf16 = lambda *shape: jax.ShapeDtypeStruct(shape, BF)
     counts = [((SLOTS, rows, mine), F32), ((SLOTS, 2, rows, LANES), F32)]
-    moved, query_t, grad_bf, table_t = call(
+    moved, query_t, grad_bf, rest_bf, table_t = call(
         functools.partial(first_kernel, nbatch),
         "bucket0_left",
-        (f32(half + 8, width), bf16(width, mine), bf16(rows, mine), bf16(width, mine)),
+        (f32(half + 8, width), bf16(width, mine), bf16(rows, mine), bf16(rows, mine), bf16(width, mine)),
         (index, left, left_accum, right, relation),
         [((rows, mine), F32), *counts],
         flops=2 << 30,
@@ -275,8 +282,8 @@
         functools.partial(between_kernel, nbatch),
         "bucket0_right",
         (f32(rows, width), f32(1, rows), f32(width, width), f32(SLOTS, rows, pairs), f32(SLOTS, 2, rows, LANES)),
-        (index, left, right, right_accum, relation, query_t, grad_bf, table_t),
-        [((width, mine), BF), ((rows, mine), F32), ((rows, mine), BF), *counts],
+        (index, left, right, right_accum, relation, query_t, grad_bf, rest_bf, table_t),
+        [((width, mine), BF), ((rows, mine), F32), ((rows, mine), BF), ((rows, mine), BF), *counts],
         flops=1 << 30,
     )
     moved = lax.all_gather(moved, "core", axis=0, tiled=False)

time: 83.9 us -> 83.9 us (level)
  no operation moved by 1% of the time
where the time goes in v10:
time: 83.9 us; the launch traced here: 83.6 us
  blocking collectives  62.1 us (74%)
  Pallas kernels  10.6 us (13%)
  waiting for transfers between devices  8.2 us (10%)
  starting transfers between devices  1.92 us (2%)
    all_to_all x1, blocking collectives, body(): grad = jnp.sum(lax.all_to_all(grad, BLK, 0, 0, tiled=True), axis=0)  21.2 us
    all_to_all x1, blocking collectives, body(): grad = lax.all_to_all(grad, BLK, 0, 0, tiled=True)  19.8 us
    all_gather x1, blocking collectives, body(): index = lax.all_gather(index, REP, axis=0, tiled=False)  13.8 us
    pallas_call x5, Pallas kernels, call(): pl.pallas_call(kernel, out_shape=outs, in_specs=[pl.BlockSpec(memory_spac...  10.6 us
    ppermute x1, waiting for transfers between devices, body(): lax.ppermute(half, BLK, route)  8.2 us
    all_gather x1, blocking collectives, body(): grad = lax.all_gather(grad, 'core', axis=0, tiled=False)  4.94 us
    all_gather x1, blocking collectives, buckets(): moved = lax.all_gather(moved, 'core', axis=0, tiled=False)  2.37 us
    ppermute x1, starting transfers between devices, body(): lax.ppermute(half, BLK, route)  1.92 us
  transfers between devices with their start and end apart: 1, of which 1 were waited for; matrix products, arithmetic and copies ran while one was open for 0% of the time, Pallas kernels for 3%

profile of v10, /device:TPU:1, one launch (start us, length us, event | category | flops | bytes accessed | tf_op | source)
XLA Modules:
  0.0 83.6 jit_solution(2405329466373636826)
XLA Ops:
  0.6 1.4 %gather_index.1 = (s32[24,512]{1,0:T(8,128)S(1)}, f32[256,256]{1,0:T(8,128)S(1)}, f32[1,256]{1,0:T(1,128)S(1)}, f32[256,256]{1,0:T(8,128)S(1)}, f32[1,256]{1,0:T(1,128)S(1)}, /*index=5*/f32[2,256,256]{2,1,0:T(8,128)S(1)}) custom-call(s32[1,1,2,2,512]{4,3,2,1,0:T(2,128)} %refs_0_.1, s32[1,1,2,2,512]{4,3,2,1,0:T(2,128)} %refs_1_.1, ...), custom_call_target="tpu_custom_call" | custom-call | bytes 4194304 | tf_op jit(solution)/shard_map/gather_index/pallas_call | solution.py:252
  2.0 13.8 %all-gather = s32[96,512]{1,0:T(8,128)S(1)} all-gather(s32[24,512]{1,0:T(8,128)S(1)} %get-tuple-element.33), channel_id=2, replica_groups=mesh['z'=8,'y'=8,'xl'=2,'xh'=2,'core'=2] {'xh','core'}, dimensions={0}, use_global_device_ids=true | all-gather | bytes 245760 | tf_op jit(solution)/shard_map/all_gather | solution.py:326
  15.9 2.5 %bucket0_left.1 = (f32[136,256]{1,0:T(8,128)S(1)}, bf16[256,256]{1,0:T(8,128)(2,1)S(1)}, bf16[256,256]{1,0:T(8,128)(2,1)S(1)}, bf16[256,256]{1,0:T(8,128)(2,1)S(1)}, bf16[256,256]{1,0:T(8,128)(2,1)S(1)}) custom-call(s32[4,24,512]{2,1,0:T(8,128)S(1)} %bitcast.11, f32[256,256]{1,0:T(8,128)S(1)} %get-tuple-element.34.left_all_ref.left_ref, ...), custom_call_target="tpu_custom_call" | custom-call | flops 2147483648 | bytes 4194304 | tf_op jit(solution)/shard_map/bucket0_left/pallas_call | solution.py:252
  18.4 1.9 %collective-permute-start = (f32[136,256]{1,0:T(8,128)S(1)}, f32[136,256]{1,0:T(8,128)S(1)}, u32[]{:S(2)}, u32[]{:S(2)}) collective-permute-start(f32[136,256]{1,0:T(8,128)S(1)} %get-tuple-element.45), channel_id=1, source_target_pairs={{0,4},{4,8},{8,12},{12,16},{16,20},{20,24},{24,28},{28,32},{32,36}... | collective-permute-start | bytes 417800 | tf_op jit(solution)/shard_map/ppermute | solution.py:332
  20.3 2.9 %bucket0_right.1 = (f32[256,256]{1,0:T(8,128)S(1)}, f32[1,256]{1,0:T(1,128)S(1)}, f32[256,256]{1,0:T(8,128)S(1)}, f32[4,256,512]{2,1,0:T(8,128)S(1)}, f32[4,2,256,128]{3,2,1,0:T(8,128)S(1)}) custom-call(s32[4,24,512]{2,1,0:T(8,128)S(1)} %bitcast.12, f32[256,256]{1,0:T(8,128)S(1)} %get-tuple-element.34.left_all_ref.left_ref, ...), custom_call_target="tpu_custom_call" | custom-call | flops 1073741824 | bytes 4194304 | tf_op jit(solution)/shard_map/bucket0_right/pallas_call | solution.py:252
  23.2 8.2 %collective-permute-done = f32[136,256]{1,0:T(8,128)S(1)} collective-permute-done((f32[136,256]{1,0:T(8,128)S(1)}, f32[136,256]{1,0:T(8,128)S(1)}, u32[]{:S(2)}, u32[]{:S(2)}) %collective-permute-start) | collective-permute-done | bytes 139296 | tf_op jit(solution)/shard_map/ppermute | solution.py:332
  31.4 2.4 %all-gather.1 = f32[272,256]{1,0:T(8,128)S(1)} all-gather(f32[136,256]{1,0:T(8,128)S(1)} %collective-permute-done), channel_id=3, replica_groups=mesh['z'=8,'y'=8,'xl'=2,'xh'=2,'core'=2] {'core'}, dimensions={0}, use_global_device_ids=true | all-gather | bytes 417792 | tf_op jit(solution)/shard_map/all_gather | solution.py:289
  33.8 2.6 %bucket1.1 = (f32[256,256]{1,0:T(8,128)S(1)}, f32[1,256]{1,0:T(1,128)S(1)}, f32[256,256]{1,0:T(8,128)S(1)}, f32[1,256]{1,0:T(1,128)S(1)}, f32[2,64,4,128]{3,2,1,0:T(4,128)S(1)}) custom-call(f32[4,256,512]{2,1,0:T(8,128)S(1)} %get-tuple-element.43.edges_ref, f32[4,2,256,128]{3,2,1,0:T(8,128)S(1)} %get-tuple-element.44.counts_ref, f32[2,136,256]{2,1,0:T(8,128)S(1)} %bitcast.9, ...), custom_call_target="tpu_custom_call" | custom-call | flops 2147483648 | bytes 4194304 | tf_op jit(solution)/shard_map/bucket1/pallas_call | solution.py:252
  36.3 0.0 copy-start
  36.3 21.2 %all_to_all.10 = f32[128,4,128]{2,1,0:T(4,128)S(1)} all-to-all(f32[128,4,128]{2,1,0:T(4,128)S(1)} %bitcast.10), channel_id=1, replica_groups=mesh['z'=8,'y'=8,'xl'=2,'xh'=2,'core'=2] {'z','y','xl'}, dimensions={0} | all-to-all | bytes 524288 | tf_op jit(solution)/shard_map/all_to_all | solution.py:335
  57.5 0.1 reduce_sum.9
  57.7 19.8 %all_to_all.11 = f32[128,4,128]{2,1,0:T(4,128)S(1)} all-to-all(f32[128,4,128]{2,1,0:T(4,128)S(1)} %broadcast_in_dim.2), channel_id=1, replica_groups=mesh['z'=8,'y'=8,'xl'=2,'xh'=2,'core'=2] {'z','y','xl'}, dimensions={0} | all-to-all | bytes 524288 | tf_op jit(solution)/shard_map/all_to_all | solution.py:337
  77.4 4.9 %all-gather.2 = f32[256,4,128]{2,1,0:T(4,128)S(1)} all-gather(f32[128,4,128]{2,1,0:T(4,128)S(1)} %all_to_all.11), channel_id=4, replica_groups=mesh['z'=8,'y'=8,'xl'=2,'xh'=2,'core'=2] {'core'}, dimensions={0}, use_global_device_ids=true | all-gather | bytes 786432 | tf_op jit(solution)/shard_map/all_gather | solution.py:338
  82.4 0.0 copy-done
  82.4 1.2 %final_update.1 = (f32[2,256,256]{2,1,0:T(8,128)}, f32[2,256,256]{2,1,0:T(8,128)}, f32[256,256]{1,0:T(8,128)}, f32[1,256]{1,0:T(1,128)}, f32[256,256]{1,0:T(8,128)}, /*index=5*/f32[1,256]{1,0:T(1,128)}) custom-call(f32[2,2,64,4,128]{4,3,2,1,0:T(4,128)S(1)} %bitcast.8, f32[2,256,256]{2,1,0:T(8,128)S(1)} %get-tuple-element.37.op_ref.relation_ref, ...), custom_call_target="tpu_custom_call" | custom-call | bytes 4194304 | tf_op jit(solution)/shard_map/final_update/pallas_call | solution.py:252
  (1 shorter events, 0.0 us)
Async XLA Ops:
  18.4 13.0 %collective-permute-start = (f32[136,256]{1,0:T(8,128)S(1)}, f32[136,256]{1,0:T(8,128)S(1)}, u32[]{:S(2)}, u32[]{:S(2)}) collective-permute-start(f32[136,256]{1,0:T(8,128)S(1)} %get-tuple-element.45), channel_id=1, source_target_pairs={{0,4},{4,8},{8,12},{12,16},{16,20},{20,24},{24,28},{28,32},{32,36}... | collective-permute-start | bytes 417800 | tf_op jit(solution)/shard_map/ppermute | solution.py:332
  36.3 46.1 %copy-start = (f32[2,256,256]{2,1,0:T(8,128)S(1)}, f32[2,256,256]{2,1,0:T(8,128)}, u32[]{:S(2)}) copy-start(f32[2,256,256]{2,1,0:T(8,128)} %state_ref.1) | copy-start | bytes 1572868

commit v11 on v9

--- a/solution.py
+++ b/solution.py
@@ -13,7 +13,7 @@
 BLK = ("z", "y", "xl")
 REP = ("xh", "core")
 NREL = 2
-LANES = 128
+LANES = 256
 SLOTS = 4
 
 

time: 83.9 us -> 84.2 us (level)
  no operation moved by 1% of the time
where the time goes in v11:
time: 84.2 us; the launch traced here: 83.9 us
  blocking collectives  62.3 us (74%)
  Pallas kernels  10.3 us (12%)
  waiting for transfers between devices  8.44 us (10%)
  starting transfers between devices  1.92 us (2%)
    all_to_all x1, blocking collectives, body(): grad = jnp.sum(lax.all_to_all(grad, BLK, 0, 0, tiled=True), axis=0)  21.2 us
    all_to_all x1, blocking collectives, body(): grad = lax.all_to_all(grad, BLK, 0, 0, tiled=True)  20.3 us
    all_gather x1, blocking collectives, body(): index = lax.all_gather(index, REP, axis=0, tiled=False)  13.8 us
    pallas_call x5, Pallas kernels, call(): pl.pallas_call(kernel, out_shape=outs, in_specs=[pl.BlockSpec(memory_spac...  10.3 us
    ppermute x1, waiting for transfers between devices, body(): lax.ppermute(half, BLK, route)  8.44 us
    all_gather x1, blocking collectives, body(): grad = lax.all_gather(grad, 'core', axis=0, tiled=False)  4.68 us
    all_gather x1, blocking collectives, buckets(): moved = lax.all_gather(moved, 'core', axis=0, tiled=False)  2.37 us
    ppermute x1, starting transfers between devices, body(): lax.ppermute(half, BLK, route)  1.92 us
  transfers between devices with their start and end apart: 1, of which 1 were waited for; matrix products, arithmetic and copies ran while one was open for 0% of the time, Pallas kernels for 3%

profile of v11, /device:TPU:1, one launch (start us, length us, event | category | flops | bytes accessed | tf_op | source)
XLA Modules:
  0.0 83.9 jit_solution(9578397196775020720)
XLA Ops:
  0.6 1.4 %gather_index.1 = (s32[24,512]{1,0:T(8,128)S(1)}, f32[256,256]{1,0:T(8,128)S(1)}, f32[1,256]{1,0:T(1,128)S(1)}, f32[256,256]{1,0:T(8,128)S(1)}, f32[1,256]{1,0:T(1,128)S(1)}, /*index=5*/f32[2,256,256]{2,1,0:T(8,128)S(1)}) custom-call(s32[1,1,2,2,512]{4,3,2,1,0:T(2,128)} %refs_0_.1, s32[1,1,2,2,512]{4,3,2,1,0:T(2,128)} %refs_1_.1, ...), custom_call_target="tpu_custom_call" | custom-call | bytes 4194304 | tf_op jit(solution)/shard_map/gather_index/pallas_call | solution.py:245
  2.0 13.8 %all-gather = s32[96,512]{1,0:T(8,128)S(1)} all-gather(s32[24,512]{1,0:T(8,128)S(1)} %get-tuple-element.32), channel_id=2, replica_groups=mesh['z'=8,'y'=8,'xl'=2,'xh'=2,'core'=2] {'xh','core'}, dimensions={0}, use_global_device_ids=true | all-gather | bytes 245760 | tf_op jit(solution)/shard_map/all_gather | solution.py:319
  15.9 2.5 %bucket0_left.1 = (f32[136,256]{1,0:T(8,128)S(1)}, bf16[256,256]{1,0:T(8,128)(2,1)S(1)}, bf16[256,256]{1,0:T(8,128)(2,1)S(1)}, bf16[256,256]{1,0:T(8,128)(2,1)S(1)}) custom-call(s32[4,24,512]{2,1,0:T(8,128)S(1)} %bitcast.11, f32[256,256]{1,0:T(8,128)S(1)} %get-tuple-element.33.left_all_ref.left_ref, f32[1,256]{1,0:T(1,128)S(1)} %get-tuple-element.37.accum_ref, ...), custom_call_target="tpu_custom_call" | custom-call | flops 2147483648 | bytes 4194304 | tf_op jit(solution)/shard_map/bucket0_left/pallas_call | solution.py:245
  18.4 1.9 %collective-permute-start = (f32[136,256]{1,0:T(8,128)S(1)}, f32[136,256]{1,0:T(8,128)S(1)}, u32[]{:S(2)}, u32[]{:S(2)}) collective-permute-start(f32[136,256]{1,0:T(8,128)S(1)} %get-tuple-element.43), channel_id=1, source_target_pairs={{0,4},{4,8},{8,12},{12,16},{16,20},{20,24},{24,28},{28,32},{32,36}... | collective-permute-start | bytes 417800 | tf_op jit(solution)/shard_map/ppermute | solution.py:325
  20.3 2.6 %bucket0_right.1 = (f32[256,256]{1,0:T(8,128)S(1)}, f32[1,256]{1,0:T(1,128)S(1)}, f32[256,256]{1,0:T(8,128)S(1)}, f32[4,256,512]{2,1,0:T(8,128)S(1)}, f32[4,2,256,256]{3,2,1,0:T(8,128)S(1)}) custom-call(s32[4,24,512]{2,1,0:T(8,128)S(1)} %bitcast.12, f32[256,256]{1,0:T(8,128)S(1)} %get-tuple-element.33.left_all_ref.left_ref, ...), custom_call_target="tpu_custom_call" | custom-call | flops 1073741824 | bytes 4194304 | tf_op jit(solution)/shard_map/bucket0_right/pallas_call | solution.py:245
  23.0 8.4 %collective-permute-done = f32[136,256]{1,0:T(8,128)S(1)} collective-permute-done((f32[136,256]{1,0:T(8,128)S(1)}, f32[136,256]{1,0:T(8,128)S(1)}, u32[]{:S(2)}, u32[]{:S(2)}) %collective-permute-start) | collective-permute-done | bytes 139296 | tf_op jit(solution)/shard_map/ppermute | solution.py:325
  31.4 2.4 %all-gather.1 = f32[272,256]{1,0:T(8,128)S(1)} all-gather(f32[136,256]{1,0:T(8,128)S(1)} %collective-permute-done), channel_id=3, replica_groups=mesh['z'=8,'y'=8,'xl'=2,'xh'=2,'core'=2] {'core'}, dimensions={0}, use_global_device_ids=true | all-gather | bytes 417792 | tf_op jit(solution)/shard_map/all_gather | solution.py:282
  33.8 2.6 %bucket1.1 = (f32[256,256]{1,0:T(8,128)S(1)}, f32[1,256]{1,0:T(1,128)S(1)}, f32[256,256]{1,0:T(8,128)S(1)}, f32[1,256]{1,0:T(1,128)S(1)}, f32[2,64,4,128]{3,2,1,0:T(4,128)S(1)}) custom-call(f32[4,256,512]{2,1,0:T(8,128)S(1)} %get-tuple-element.41.edges_ref, f32[4,2,256,256]{3,2,1,0:T(8,128)S(1)} %get-tuple-element.42.counts_ref, f32[2,136,256]{2,1,0:T(8,128)S(1)} %bitcast.9, ...), custom_call_target="tpu_custom_call" | custom-call | flops 2147483648 | bytes 4194304 | tf_op jit(solution)/shard_map/bucket1/pallas_call | solution.py:245
  36.3 0.0 copy-start
  36.4 21.2 %all_to_all.10 = f32[128,4,128]{2,1,0:T(4,128)S(1)} all-to-all(f32[128,4,128]{2,1,0:T(4,128)S(1)} %bitcast.10), channel_id=1, replica_groups=mesh['z'=8,'y'=8,'xl'=2,'xh'=2,'core'=2] {'z','y','xl'}, dimensions={0} | all-to-all | bytes 524288 | tf_op jit(solution)/shard_map/all_to_all | solution.py:328
  57.5 0.1 reduce_sum.9
  57.7 20.3 %all_to_all.11 = f32[128,4,128]{2,1,0:T(4,128)S(1)} all-to-all(f32[128,4,128]{2,1,0:T(4,128)S(1)} %broadcast_in_dim.2), channel_id=1, replica_groups=mesh['z'=8,'y'=8,'xl'=2,'xh'=2,'core'=2] {'z','y','xl'}, dimensions={0} | all-to-all | bytes 524288 | tf_op jit(solution)/shard_map/all_to_all | solution.py:330
  78.0 4.7 %all-gather.2 = f32[256,4,128]{2,1,0:T(4,128)S(1)} all-gather(f32[128,4,128]{2,1,0:T(4,128)S(1)} %all_to_all.11), channel_id=4, replica_groups=mesh['z'=8,'y'=8,'xl'=2,'xh'=2,'core'=2] {'core'}, dimensions={0}, use_global_device_ids=true | all-gather | bytes 786432 | tf_op jit(solution)/shard_map/all_gather | solution.py:331
  82.7 0.0 copy-done
  82.7 1.2 %final_update.1 = (f32[2,256,256]{2,1,0:T(8,128)}, f32[2,256,256]{2,1,0:T(8,128)}, f32[256,256]{1,0:T(8,128)}, f32[1,256]{1,0:T(1,128)}, f32[256,256]{1,0:T(8,128)}, /*index=5*/f32[1,256]{1,0:T(1,128)}) custom-call(f32[2,2,64,4,128]{4,3,2,1,0:T(4,128)S(1)} %bitcast.8, f32[2,256,256]{2,1,0:T(8,128)S(1)} %get-tuple-element.36.op_ref.relation_ref, ...), custom_call_target="tpu_custom_call" | custom-call | bytes 4194304 | tf_op jit(solution)/shard_map/final_update/pallas_call | solution.py:245
  (1 shorter events, 0.0 us)
Async XLA Ops:
  18.4 13.0 %collective-permute-start = (f32[136,256]{1,0:T(8,128)S(1)}, f32[136,256]{1,0:T(8,128)S(1)}, u32[]{:S(2)}, u32[]{:S(2)}) collective-permute-start(f32[136,256]{1,0:T(8,128)S(1)} %get-tuple-element.43), channel_id=1, source_target_pairs={{0,4},{4,8},{8,12},{12,16},{16,20},{20,24},{24,28},{28,32},{32,36}... | collective-permute-start | bytes 417800 | tf_op jit(solution)/shard_map/ppermute | solution.py:325
  36.3 46.3 %copy-start = (f32[2,256,256]{2,1,0:T(8,128)S(1)}, f32[2,256,256]{2,1,0:T(8,128)}, u32[]{:S(2)}) copy-start(f32[2,256,256]{2,1,0:T(8,128)} %state_ref.1) | copy-start | bytes 1572868
